TPU v7x, 32 devices: a whole 2x2x4 slice. The times are simulated.
32 devices in a mesh: dp: 16 (over z, y, core), mp: 2 (over x).
Axes of the slice: x: 2, y: 2, z: 4, core: 2. Of those that a mesh axis runs over, the one named last changes fastest.
Arguments:
- tokens: bfloat16 [16, 448, 768], P('dp'), may hold values from -6 to 6
- frames: bfloat16 [16, 1500, 768], P('dp'), may hold values from -6 to 6
- lengths: int32 [16], P('dp'), may hold values from 1 to 448, as said below
- out_cot: bfloat16 [16, 448, 768], P('dp'), may hold values from -6 to 6
- self_query_key_value: bfloat16 [768, 3, 768], P(None, None, 'mp'), may hold values from -0.21875 to 0.21875
- self_qv_bias: float32 [2, 768], P(None, 'mp'), may hold values from -1.75 to 1.75
- self_output_weight: bfloat16 [768, 768], P('mp'), may hold values from -0.875 to 0.875
- cross_query_weight: bfloat16 [768, 768], P(None, 'mp'), may hold values from -0.21875 to 0.21875
- cross_kv: bfloat16 [768, 2, 768], P(None, None, 'mp'), may hold values from -0.21875 to 0.21875
- cross_bias: float32 [2, 768], P(None, 'mp'), may hold values from -1.75 to 1.75
- cross_output_weight: bfloat16 [768, 768], P('mp'), may hold values from -1.25 to 1.25
- first_dense_weight: bfloat16 [768, 3072], P(None, 'mp'), may hold values from -0.21875 to 0.21875
- first_dense_bias: float32 [3072], P('mp'), may hold values from -1.75 to 1.75
- second_dense_weight: bfloat16 [3072, 768], P('mp'), may hold values from -0.109375 to 0.109375
- out_biases: float32 [3, 768], replicated, may hold values from -1.75 to 1.75
- norm_gains: float32 [4, 768], replicated, may hold values from 0.25 to 1.75
- norm_biases: float32 [4, 768], replicated, may hold values from -1.75 to 1.75
Outputs:
- out: bfloat16 [16, 448, 768], P('dp')
- tokens_grad: float32 [16, 448, 768], P('dp')
- frames_grad: float32 [16, 1500, 768], P('dp', None, 'mp')
- self_qkv_grad: float32 [768, 3, 768], P('dp', None, 'mp')
- self_qv_bias_grad: float32 [2, 768], P(None, 'mp')
- self_out_grad: float32 [768, 768], P('mp', 'dp')
- cross_q_grad: float32 [768, 768], P('dp', 'mp')
- cross_kv_grad: float32 [768, 2, 768], P('dp', None, 'mp')
- cross_bias_grad: float32 [2, 768], P(None, 'mp')
- cross_out_grad: float32 [768, 768], P('mp', 'dp')
- fc1_grad: float32 [768, 3072], P('dp', 'mp')
- fc1_bias_grad: float32 [3072], P('mp')
- second_dense_gradient: float32 [3072, 768], P('mp', 'dp')
- out_biases_grad: float32 [3, 768], replicated
- norm_gains_grad: float32 [4, 768], replicated
- norm_biases_grad: float32 [4, 768], replicated
Inputs may be any that keep to these rules, and one draw needn't show every extreme that they name: `lengths`: each transcript has at least one token; some transcript fills all 448 slots.
All inputs are finite; a program needn't handle non-finite values.
Results may differ from a plain program's by a relative error of at most 0.024.
Values sent between devices are 32-bit elements; how exact they have to be, the bound alone decides.
No kernel may reach another device: no remote copies, remote signals or barrier semaphores. Data moves between devices by JAX's collectives and lax.ppermute only.
A program may use at most 192 MiB of HBM per device.

v0:
```python
from functools import partial

import jax
import jax.numpy as jnp
from jax import lax
from jax.experimental import pallas as pl
from jax.experimental.pallas import tpu as pltpu
from jax.sharding import PartitionSpec as P

F32 = jnp.float32
BF = jnp.bfloat16
HEAD_DIM = 64
LANES = 128
NEG = -1e30
COST = {"self_start": 2.0, "self_next": 1.3, "turn": 1.0, "frames_start": 3.0, "cross_start": 2.7, "dense_start": 2.4,
        "dense_back": 2.4, "dense_sent": 6.0, "dense_kept": 6.0, "cross_back": 20.0, "self_back": 12.0,
        "cross_sent": 6.0, "cross_kept": 5.0, "self_sent": 5.0, "self_kept": 4.0, "tokens_end": 5.0, "frames_kept": 6.0,
        "small_end": 1.0, "pause": 8.0}
SCALE = 1.5e10
PIECES = 4
BACK_BLOCKS = 2
ROW_BLOCKS = 1
BYTES = 6.4e-3
PINNED = ("h", "t", "r")


def shaped(shape, dtype=F32):
    return jax.ShapeDtypeStruct(tuple(shape), dtype)


def dg(a, b, ca, cb):
    return lax.dot_general(a, b, (((ca,), (cb,)), ((), ())), preferred_element_type=F32)


def nn(a, b):
    return dg(a, b, 1, 0)


def nt(a, b):
    return dg(a, b, 1, 1)


def tn(a, b):
    return dg(a, b, 0, 0)


class Feed:
    def __init__(self, source, target, sem):
        self.copy = pltpu.make_async_copy(source, target, sem)
        self.copy.start()
        self.target = target
        self.pending = True

    def ready(self):
        if self.pending:
            self.copy.wait()
            self.pending = False
        return self.target


class Drain:
    def __init__(self, source, target, sem):
        self.ref = source
        self.copy = pltpu.make_async_copy(source, target, sem)
        self.pending = True

    def flush(self):
        if self.pending:
            self.copy.start()
            self.pending = False


def use(*inputs):
    made = [i.ready() if isinstance(i, Feed) else i for i in inputs]
    return made if len(made) > 1 else made[0]


def flush(*outputs):
    for o in outputs:
        if isinstance(o, Drain):
            o.flush()


def into(*outputs):
    made = [o.ref if isinstance(o, Drain) else o for o in outputs]
    return made if len(made) > 1 else made[0]


class Pending:
    def __init__(self, make):
        self.make, self.value = make, None


class Chain:
    def __init__(self, seed):
        self.link = seed
        self.pending = []

    def pause(self, *after):
        self(lambda ins, outs, scratch: None, [], [], 0, "pause", after=after)

    def later(self, make):
        self.pending.append(Pending(make))
        return self.pending[-1]

    def settle(self):
        for item in reversed(self.pending):
            item.value = item.make()
        self.pending = []

    def swap_mp(self, v):
        return self.later(lambda: swap_mp(v))

    def swap_dp(self, v, bit, dp_size):
        return self.later(lambda: swap_dp(v, bit, dp_size))

    def tie(self, value):
        return lax.optimization_barrier((value, self.link))[0]

    def __call__(self, kernel, outs, args, flops, name, scratch=(), after=()):
        place = {
            "v": pl.BlockSpec(memory_space=pltpu.VMEM),
            "h": pl.BlockSpec(memory_space=pltpu.HBM),
            "s": pl.BlockSpec(memory_space=pltpu.SMEM),
        }
        args = [(self.link, "t")] + [(a, "t") for a in after] + list(args)
        first = 1 + len(after)
        if any(isinstance(a, Pending) and a.value is None for a, _ in args):
            self.settle()
        args = [(a.value if isinstance(a, Pending) else a, k) for a, k in args]
        outs = [(shaped((8, LANES)), "t")] + list(outs)
        held = []
        for item, kind in args[first:] + outs[1:]:
            if kind == "h":
                held.append(pltpu.VMEM(item.shape, item.dtype))
        n_in, n_out = len(args), len(outs)

        def body(*refs):
            ins, results = refs[first:n_in], refs[n_in + 1 : n_in + n_out]
            rest = refs[n_in + n_out :]
            own, bufs, sems = rest[: len(scratch)], list(rest[len(scratch) : -1]), rest[-1]
            at = 0
            feeds, drains = [], []
            for ref, (_, kind) in zip(ins, args[first:]):
                if kind == "h":
                    feeds.append(Feed(ref, bufs[at], sems.at[at]))
                    at += 1
                else:
                    feeds.append(ref)
            for ref, (_, kind) in zip(results, outs[1:]):
                if kind == "h":
                    drains.append(Drain(bufs[at], ref, sems.at[at]))
                    at += 1
                else:
                    drains.append(ref)
            kernel(feeds, drains, own)
            for feed in feeds:
                use(feed)
            flush(*drains)
            for d in drains:
                if isinstance(d, Drain):
                    d.copy.wait()

        moved = 0
        for item, kind in args + outs:
            size = jnp.dtype(item.dtype).itemsize
            for d in item.shape:
                size *= d
            moved += size
        place["t"] = place["r"] = place["h"]
        made = pl.pallas_call(
            body,
            out_shape=tuple(pltpu.HBM(o.shape, o.dtype) if k in PINNED else o for o, k in outs),
            in_specs=[place[k] for _, k in args],
            out_specs=tuple(place[k] for _, k in outs),
            scratch_shapes=list(scratch) + held + [pltpu.SemaphoreType.DMA((max(1, len(held)),))],
            compiler_params=pltpu.CompilerParams(vmem_limit_bytes=28 * 1024 * 1024),
            cost_estimate=pl.CostEstimate(flops=int(COST.get(name, 1.0) * SCALE), transcendentals=0, bytes_accessed=int(COST.get(name, 1.0) * SCALE * BYTES)),
            name=name,
        )(*[pltpu.with_memory_space_constraint(a, pltpu.HBM) if k in PINNED else a for a, k in args])
        self.link = made[0]
        return made[1:]


def standard(stream):
    centred = stream - jnp.mean(stream, axis=1, keepdims=True)
    spread = jnp.mean(centred * centred, axis=1, keepdims=True)
    scale = lax.rsqrt(spread + 1e-05)
    return centred * scale, scale


def norm_back(grad, unit, scale, gain):
    lifted = grad * gain
    mean_plain = jnp.mean(lifted, axis=1, keepdims=True)
    mean_cross = jnp.mean(lifted * unit, axis=1, keepdims=True)
    return scale * (lifted - mean_plain - unit * mean_cross)


def column_sums(values):
    return jnp.sum(values, axis=0, keepdims=True)


def head_lanes(which):
    lane = lax.broadcasted_iota(jnp.int32, (1, LANES), 1)
    return (lane < HEAD_DIM) if which == 0 else (lane >= HEAD_DIM)


def only(mask, values):
    return jnp.where(mask, values, jnp.zeros_like(values))


def pair_slice(pair):
    return pl.ds(pl.multiple_of(pair * LANES, LANES), LANES)


def attend_rows(q_ref, k_ref, v_ref, rows, keys, bias, mixed_ref, out_ref, lse_ref, lse_all, blocks):
    lane = lax.broadcasted_iota(jnp.int32, (1, LANES), 1)
    size = (rows.stop - rows.start) // blocks

    def body(step, carry):
        pair, part = (step, 0) if blocks == 1 else (step // blocks, step % blocks)
        at = pair_slice(pair)
        here = place(part, size) if blocks > 1 else slice(0, size)
        theirs = pl.ds(pl.multiple_of(rows.start + part * size, 16), size) if blocks > 1 else rows
        k_pair, v_pair, q_pair = k_ref[0:keys, at], v_ref[0:keys, at], q_ref[theirs, at]
        result, lse = None, lse_all[here]
        for which in range(2):
            mask = head_lanes(which)
            scores = nt(only(mask, q_pair), k_pair) + bias(part * size, size)
            top = jnp.max(scores, axis=1, keepdims=True)
            raised = jnp.exp(scores - top)
            total = jnp.sum(raised, axis=1, keepdims=True)
            value = nn(raised.astype(BF), v_pair) * (1.0 / total)
            result = value if which == 0 else jnp.where(mask, value, result)
            lse = jnp.where(lane == 2 * pair + which, top + jnp.log(total), lse)
        lse_all[here] = lse
        out_ref[here, at] = result
        mixed_ref[here, at] = result.astype(BF)
        return carry

    lse_all[...] = jnp.zeros_like(lse_all)
    lax.fori_loop(0, q_ref.shape[1] // LANES * blocks, body, 0)
    lse_ref[...] = lse_all[...].T[0 : lse_ref.shape[0]]


def attend_back(q_ref, g_ref, o_ref, lse_ref, k_ref, v_ref, rows, keys, bias, dq_ref, emit, block=None):
    block = keys if block is None else block
    blocks = keys // block

    def body(step, carry):
        pair, part = (step, 0) if blocks == 1 else (step // blocks, step % blocks)
        at = pair_slice(pair)
        here = pl.ds(0, keys) if blocks == 1 else pl.ds(pl.multiple_of(part * block, block), block)
        k_pair, v_pair = k_ref[here, at], v_ref[here, at]
        q_pair, g_pair = q_ref[rows, at], g_ref[:, at]
        product = (g_pair.astype(F32) * o_ref[:, at]).T
        k_turned = k_pair.T
        parts, grad_k, grad_v = [], None, None
        for which in range(2):
            mask = head_lanes(which)
            q_head, g_head = only(mask, q_pair), only(mask, g_pair)
            inner = column_sums(product[which * HEAD_DIM : (which + 1) * HEAD_DIM])
            scores = nt(k_pair, q_head) + bias(part * block)
            probs = jnp.exp(scores - lse_ref[pl.ds(2 * pair + which, 1), :])
            grad_probs = nt(v_pair, g_head)
            grad_scores = (probs * (grad_probs - inner)).astype(BF)
            here_v = nn(probs.astype(BF), g_head)
            here_k = nn(grad_scores, q_head)
            grad_v = here_v if which == 0 else grad_v + here_v
            grad_k = here_k if which == 0 else grad_k + here_k
            parts.append(nn(k_turned[which * HEAD_DIM : (which + 1) * HEAD_DIM], grad_scores))
        emit(pair, part, at, here, grad_k, grad_v)
        grad_q = jnp.concatenate(parts, axis=0).T
        if blocks == 1:
            dq_ref[:, at] = grad_q
        else:
            dq_ref[:, at] += grad_q
        return carry

    if blocks > 1:
        dq_ref[...] = jnp.zeros_like(dq_ref)
    lax.fori_loop(0, q_ref.shape[1] // LANES * blocks, body, 0)


def causal_bias(start, count, keys, length):
    shape = (count, keys)
    query = lax.broadcasted_iota(jnp.int32, shape, 0) + start
    key = lax.broadcasted_iota(jnp.int32, shape, 1)
    return jnp.where((key <= query) & (key < length), 0.0, NEG).astype(F32)


def tail_bias(keys, real, turned, start=0):
    shape = (keys, 1) if turned else (1, keys)
    key = lax.broadcasted_iota(jnp.int32, shape, 0 if turned else 1) + start
    return jnp.where(key < real, 0.0, NEG).astype(F32)


def place(step, size):
    return pl.ds(pl.multiple_of(step * size, size), size)


def by_rows(count, work):
    size = count // 2

    def body(step, carry):
        work(place(step, size))
        return carry

    lax.fori_loop(0, count // size, body, 0)


def ordered(out, order, left):
    size = 2 * LANES

    def body(step, carry):
        out[place(step, size)] = nt(order[place(step, size)], left[...]).astype(BF)
        return carry

    lax.fori_loop(0, order.shape[0] // size, body, 0)


def self_start(cut, ins, outs, scratch):
    tok, gains, shifts, vb, w, length, wo = ins
    x_lo, x_hi, q_o, k_o, v_o = outs[:5]
    rows = slice(cut, tok.target.shape[0])
    low_ref, high_ref, q_ref, k_ref, v_ref = into(*outs[:5])
    tok, gains, shifts, vb, w = use(tok, gains, shifts, vb, w)
    x_all, size = scratch[1], tok.shape[0] // 2

    def work(here):
        unit, _ = standard(tok[here].astype(F32))
        x_all[here] = (unit * gains[0:1] + shifts[0:1]).astype(BF)

    by_rows(tok.shape[0], work)

    def body(step, carry):
        here = place(step, size)
        x = x_all[here]
        q_ref[here] = ((nn(x, w[0]) + vb[0:1]) * 0.125).astype(BF)
        k_ref[here] = nn(x, w[1]).astype(BF)
        v_ref[here] = (nn(x, w[2]) + vb[1:2]).astype(BF)
        return carry

    lax.fori_loop(0, 2, body, 0)
    low_ref[...] = x_all[:cut]
    high_ref[...] = x_all[cut:]
    flush(x_lo, x_hi, q_o, k_o, v_o)
    self_rows(rows, q_ref, k_ref, v_ref, length, wo, outs[5:], scratch)


def self_next(rows, ins, outs, scratch):
    q_ref, k_ref, v_ref, length, wo = ins
    self_rows(rows, *use(q_ref, k_ref, v_ref), length, wo, outs, scratch)


def self_rows(rows, q_ref, k_ref, v_ref, length, wo, outs, scratch):
    def bias(start, size):
        return causal_bias(rows.start + start, size, rows.stop, length[0])

    mixed, out, lse, part = into(*outs)
    attend_rows(q_ref, k_ref, v_ref, rows, rows.stop, bias, mixed, out, lse, scratch[0], 1)
    flush(*outs[:3])
    part[...] = nn(mixed[...], use(wo)[...])


def turn(plan, ins, outs, scratch):
    orders = ins[: 1 + max(which for which, _ in plan)]
    parts = ins[len(orders) :]
    for (which, part), out in zip(plan, outs):
        ordered(into(out), use(orders[which]), use(parts[part]))
        flush(out)


def frames_start(ins, outs, scratch):
    frames, w, vb, sources = ins
    k_o, v_o, t_o, order_o, other_o = outs
    k_ref, v_ref, t_ref, order, other = into(*outs)
    (frames_all,) = scratch
    sources = use(sources)
    column = lax.broadcasted_iota(jnp.int32, order.shape, 1)
    order[...] = jnp.where(column == sources[:, 0:1], 1.0, 0.0).astype(BF)
    other[...] = jnp.where(column == sources[:, 1:2], 1.0, 0.0).astype(BF)
    flush(order_o, other_o)
    real, padded = frames.target.shape[0], k_ref.shape[0]
    if padded > real:
        low = real // 16 * 16
        frames_all[low:padded] = jnp.zeros((padded - low, frames_all.shape[1]), BF)
    frames, w, vb = use(frames, w, vb)
    frames_all[0:real] = frames[...]
    size = padded // 3

    def body(step, carry):
        rows = frames_all[place(step, size)]
        k_ref[place(step, size)] = nn(rows, w[0]).astype(BF)
        v_ref[place(step, size)] = (nn(rows, w[1]) + vb[1:2]).astype(BF)
        t_ref[:, place(step, size)] = nt(order[...], rows).astype(BF)
        return carry

    lax.fori_loop(0, 3, body, 0)


def assemble(out, spot, pieces):
    block = out.shape[0] // len(pieces)
    for j, piece in enumerate(pieces):
        at = pl.multiple_of(((spot[0] & (len(pieces) - 1)) ^ j) * block, 16)
        out[pl.ds(at, block), :] = use(piece)[...].astype(BF)


def cross_start(rows, real, ins, outs, scratch):
    mine, other, tok, ob, gains, shifts, vb, wq, k_in, v_in, wo = ins
    s_o, x_o, q_o, m_o, out_o, lse_o, part = outs
    mixed, out, lse, part = into(m_o, out_o, lse_o, part)
    s_ref, x_ref, q_ref = into(s_o, x_o, q_o)
    mine, other, tok, ob, gains, shifts = use(mine, other, tok, ob, gains, shifts)
    block = tok.at[rows]

    def work(here):
        stream = block[here].astype(F32) + (mine[here] + other[here]) + ob[0:1]
        s_ref[here] = stream
        unit, _ = standard(stream)
        x_ref[here] = (unit * gains[1:2] + shifts[1:2]).astype(BF)

    by_rows(s_ref.shape[0], work)
    flush(s_o)
    vb, wq = use(vb, wq)
    q_ref[...] = ((nn(x_ref[...], wq[...]) + vb[0:1]) * 0.125).astype(BF)
    flush(x_o, q_o)
    k_ref, v_ref = use(k_in, v_in)
    keys = k_ref.shape[0]
    tail = tail_bias(keys, real, False)
    attend_rows(q_ref, k_ref, v_ref, slice(0, x_ref.shape[0]), keys, lambda start, size: tail, mixed, out, lse, scratch[0], ROW_BLOCKS)
    flush(m_o, out_o, lse_o)
    part[...] = nn(mixed[...], use(wo)[...])


def dense_start(ins, outs, scratch):
    mine, other, s_in, ob, gains, shifts, fb, w1, w2 = ins
    s_o, x_o, a_o, d_o, part = outs
    s_ref, x_ref, active, slope, part = into(s_o, x_o, a_o, d_o, part)
    mine, other, s_in, ob, gains, shifts = use(mine, other, s_in, ob, gains, shifts)
    def work(here):
        stream = s_in[here] + (mine[here] + other[here]) + ob[1:2]
        s_ref[here] = stream
        unit, _ = standard(stream)
        x_ref[here] = (unit * gains[2:3] + shifts[2:3]).astype(BF)

    by_rows(s_ref.shape[0], work)
    flush(s_o, x_o)
    fb, w1, w2 = use(fb, w1, w2)
    wide = 3 * LANES

    def body(step, carry):
        at = pl.ds(pl.multiple_of(step * wide, wide), wide)
        hidden = nn(x_ref[...], w1[:, at]) + fb[:, at]
        below = 0.5 + 0.5 * lax.erf(hidden * 0.7071067811865476)
        slope[:, at] = below + hidden * (0.3989422804014327 * jnp.exp(-0.5 * hidden * hidden))
        value = (hidden * below).astype(BF)
        active[:, at] = value
        part[...] += nn(value, w2[at, :])
        return carry

    part[...] = jnp.zeros_like(part)
    lax.fori_loop(0, w1.shape[1] // wide, body, 0)


def dense_back(rows, ins, outs, scratch):
    mine, other, s_in, ob, gains, shifts, cot, length, w2, slope, w1 = ins
    y_o, g_o, low_o, hid_o, part, sums, hid_sums = outs
    out_ref, g_ref, low_ref, hid_ref, part, sums, hid_sums = into(*outs)
    mine, other, s_in, ob, gains, shifts = use(mine, other, s_in, ob, gains, shifts)
    block = use(cot).at[rows]
    sums[0:3] = jnp.zeros((3, sums.shape[1]), F32)

    def work(here):
        stream = s_in[here] + (mine[here] + other[here]) + ob[2:3]
        unit, scale = standard(stream)
        row = lax.broadcasted_iota(jnp.int32, (stream.shape[0], 1), 0) + (rows.start + here.start)
        valid = (row < length[0]).astype(F32)
        out_ref[here] = ((unit * gains[3:4] + shifts[3:4]) * valid).astype(BF)
        incoming = block[here].astype(F32) * valid
        grad = norm_back(incoming, unit, scale, gains[3:4])
        g_ref[here] = grad
        low_ref[here] = grad.astype(BF)
        sums[0:1] += column_sums(incoming * unit)
        sums[1:2] += column_sums(incoming)
        sums[2:3] += column_sums(grad)

    by_rows(g_ref.shape[0], work)
    flush(y_o, g_o, low_o)
    w2, slope, w1 = use(w2, slope, w1)
    wide = 3 * LANES

    def body(step, carry):
        at = pl.ds(pl.multiple_of(step * wide, wide), wide)
        low = (slope[:, at] * nt(low_ref[...], w2[at, :])).astype(BF)
        hid_ref[:, at] = low
        hid_sums[0:1, at] = column_sums(low.astype(F32))
        part[...] += nt(low, w1[:, at])
        return carry

    part[...] = jnp.zeros_like(part)
    lax.fori_loop(0, w1.shape[1] // wide, body, 0)


def back_head(incoming_at, ins, outs, gm, gains, wo, sums, level, more):
    s_in, g_in = ins
    g_o, low_o = outs
    g_ref, low_ref = into(g_o, low_o)
    s_in, g_in, gains = use(s_in, g_in, gains)
    if not more:
        sums[0:3] = jnp.zeros((3, sums.shape[1]), F32)

    def work(here):
        incoming = incoming_at(here)
        unit, scale = standard(s_in[here])
        grad = g_in[here] + norm_back(incoming, unit, scale, gains[level : level + 1])
        g_ref[here] = grad
        low_ref[here] = grad.astype(BF)
        sums[0:1] += column_sums(incoming * unit)
        sums[1:2] += column_sums(incoming)
        sums[2:3] += column_sums(grad)

    by_rows(g_ref.shape[0], work)
    flush(g_o, low_o)
    gm[...] = nt(low_ref[...], use(wo)[...]).astype(BF)


def gather_heads(count, q_all, o_all, lse_all, refs):
    start = 0
    for q_ref, out_in, lse in refs:
        q_ref, out_in, lse = use(q_ref, out_in, lse)
        stop = start + out_in.shape[0]
        if q_all is not None:
            q_all[start:stop] = q_ref[...]
        o_all[start:stop] = out_in[...]
        lse_all[:, start:stop] = lse[...]
        start = stop


def cross_back(cut, real, ins, outs, scratch):
    blocks = (ins[:7], ins[7:14])
    gains, wo, k_in, v_in, which, kv = ins[14:20]
    lq_outs, part, sums, dk_o, dv_o = outs[4:6], outs[6], outs[7], outs[8], outs[9]
    gm, dq, q_all, o_all, lse_all, held, frame_sems = scratch
    part, sums, dk, dv = into(part, sums, dk_o, dv_o)
    start = 0
    for n, (mine, other, s_in, g_in, q_ref, out_in, lse) in enumerate(blocks):
        mine, other = use(mine, other)
        stop = start + mine.shape[0]
        back_head(lambda here, mine=mine, other=other: mine[here] + other[here], (s_in, g_in), outs[2 * n : 2 * n + 2], gm.at[start:stop], gains, wo, sums, 2, n > 0)
        start = stop
    gather_heads(start, q_all, o_all, lse_all, [b[4:7] for b in blocks])
    k_ref, v_ref = use(k_in, v_in)
    keys, width = k_ref.shape
    block = keys // BACK_BLOCKS

    def emit(pair, n, at, here, grad_k, grad_v):
        dk[here, at] = grad_k.astype(BF)
        dv[here, at] = grad_v.astype(BF)

    attend_back(q_all, gm, o_all, lse_all, k_ref, v_ref, slice(0, start), keys,
                lambda first: tail_bias(block, real, True, first), dq, emit, block)
    flush(dk_o, dv_o)
    low_q = (dq[...].astype(BF).astype(F32) * 0.125).astype(BF)
    part[...] = low_q.astype(F32)
    high = start - cut
    for o, rows in ((lq_outs[0], slice(0, high)), (lq_outs[1], slice(high, start))):
        into(o)[...] = low_q[rows]
        flush(o)
    sums[3:4, 0:width] = column_sums(low_q.astype(F32))
    sums[3:4, width : 2 * width] = column_sums(dv[0:real].astype(F32))
    width = held.shape[1]
    frames_terms(held, dk, dv, use(kv), pl.ds(pl.multiple_of((1 - which[0]) * width, width), width))
    start, copies = 0, []
    for n, out in enumerate(outs[10:]):
        copies.append(pltpu.make_async_copy(held.at[start : start + out.shape[0]], out, frame_sems.at[n]))
        copies[n].start()
        start += out.shape[0]
    for copy in copies:
        copy.wait()


def frames_terms(held, lk, lv, w, at):
    size = lk.shape[0] // 3

    def body(step, carry):
        rows = place(step, size)
        held[rows] = nt(lk[rows], w[0, at, :]) + nt(lv[rows], w[1, at, :])
        return carry

    lax.fori_loop(0, 3, body, 0)


def frames_kept(ins, outs, scratch):
    which, lk, lv, w = use(*ins[:4])
    held, final, sem = scratch
    start, width = 0, held.shape[1]
    frames_terms(held, lk, lv, w, pl.ds(pl.multiple_of(which[0] * width, width), width))
    for other in ins[4:]:
        other = use(other)
        rows = slice(start, min(start + other.shape[0], final.shape[0]))
        final[rows] = held[rows] + other[0 : rows.stop - start]
        start = rows.stop
    copy = pltpu.make_async_copy(final, outs[0].at[:, 0, :], sem)
    copy.start()
    copy.wait()


def self_back(cut, ins, outs, scratch):
    spot, mine, other, wq = ins[:4]
    pieces, (gains, wo, q_in, k_in, v_in, w, length) = ins[4:6], ins[6:13]
    blocks = (ins[13:17], ins[17:21])
    l3_outs, part_high, part_low, sums = outs[4:6], outs[6], outs[7], outs[8]
    gm, dq, wq_other, q_all, o_all, lse_all, lows, incoming = scratch
    l3_high, l3_low, part_high, part_low, sums = into(*l3_outs, part_high, part_low, sums)
    assemble(wq_other, spot, pieces)
    mine, other, wq = use(mine, other, wq)
    incoming[...] = nt(mine[...].astype(BF), wq[...]) + nt(other[...].astype(BF), wq_other[...])
    start = 0
    for n, (s_in, g_in, out_in, lse) in enumerate(blocks):
        stop = start + out_in.target.shape[0]
        block = incoming.at[start:stop]
        back_head(lambda here, block=block: block[here], (s_in, g_in), outs[2 * n : 2 * n + 2], gm.at[start:stop], gains, wo, sums, 1, n > 0)
        start = stop
    high = start - cut
    q_ref = use(q_in)
    q_all[0:high] = q_ref[cut:]
    q_all[high:] = q_ref[:cut]
    gather_heads(start, None, o_all, lse_all, [(b[2], b[2], b[3]) for b in blocks])
    k_ref, v_ref, w = use(k_in, v_in, w)
    width = k_ref.shape[1]
    block = start // 2

    def bias(first):
        lane = lax.broadcasted_iota(jnp.int32, (block, start), 1)
        query = jnp.where(lane < high, lane + cut, lane - high)
        key = lax.broadcasted_iota(jnp.int32, (block, start), 0) + first
        return jnp.where((key <= query) & (key < length[0]), 0.0, NEG).astype(F32)

    def emit(pair, n, at, here, grad_k, grad_v):
        lows[0, here, at] = grad_k.astype(BF)
        lows[1, here, at] = grad_v.astype(BF)

    attend_back(q_all, gm, o_all, lse_all, k_ref, v_ref, slice(0, start), start, bias, dq, emit, block)
    low_q = (dq[...].astype(BF).astype(F32) * 0.125).astype(BF)
    l3_high[0], l3_low[0] = low_q[:high], low_q[high:]
    for n in range(2):
        l3_high[1 + n], l3_low[1 + n] = lows[n, cut:], lows[n, :cut]
    flush(*l3_outs)
    for l3, part in ((l3_low, part_low), (l3_high, part_high)):
        part[...] = nt(l3[0], w[0]) + nt(l3[1], w[1]) + nt(l3[2], w[2])
    sums[3:4, 0:width] = column_sums(low_q.astype(F32))
    sums[3:4, width : 2 * width] = column_sums(lows[1].astype(F32))


def tokens_end(rows, ins, outs, scratch):
    tok, gains, g, mine, other = use(*ins[:5])
    block, (both,) = tok.at[rows], scratch
    target = into(outs[0]) if len(ins) == 6 else into(outs[0]).at[rows]
    both[...] = jnp.zeros_like(both)

    def work(here):
        unit, scale = standard(block[here].astype(F32))
        incoming = mine[here] + other[here]
        target[here] = g[here] + norm_back(incoming, unit, scale, gains[0:1])
        both[0:1] += column_sums(incoming * unit)
        both[1:2] += column_sums(incoming)

    by_rows(target.shape[0], work)
    if len(ins) == 6:
        flush(outs[0])
        into(outs[1])[...] = both[...]
        return
    out, total, y = into(*outs)
    gain, shift = both[0:1], both[1:2]
    earlier, first = use(*ins[5:7])
    sums, hid_sums, (y_low, y_high) = use(*ins[7:11]), use(*ins[11:13]), ins[13:15]
    out[rows.stop :] = earlier[...]
    flush(outs[0])
    y_low, y_high = use(y_low, y_high)
    y[0 : rows.stop] = y_low[...]
    y[rows.stop :] = y_high[...]
    flush(outs[2])
    total[0:1] = gain + first[0:1]
    total[4:5] = shift + first[1:2]
    for level, one in enumerate((sums[0][...], sums[1][...], sums[2][...] + sums[3][...])):
        total[1 + level : 2 + level] = one[0:1]
        total[5 + level : 6 + level] = one[1:2]
        total[8 + level : 9 + level] = one[2:3]
        if level < 2:
            total[11 + level : 12 + level] = one[3:4]
    model = total.shape[1]
    for piece in range(hid_sums[0].shape[1] // model):
        at = slice(piece * model, (piece + 1) * model)
        total[13 + piece : 14 + piece] = hid_sums[0][0:1, at] + hid_sums[1][0:1, at]


def small_end(ins, outs, scratch):
    mine, other = use(*ins)
    gain, shift, ob, svb, cvb, fb = into(*outs)
    total = mine[...] + other[...]
    half = svb.shape[1]
    gain[...] = total[0:4]
    shift[...] = total[4:8]
    ob[...] = total[8:11]
    for target, at in ((svb, 11), (cvb, 12)):
        target[0:1] = total[at : at + 1, :half]
        target[1:2] = total[at : at + 1, half:]
    fb[...] = total[13 : 13 + fb.shape[0]]


def blocks_of(rights, blocks, put):
    first = rights[0]
    if len(first.shape) == 3:
        low, wide = blocks[0], first.shape[2]

        def body(step, carry):
            put(step * wide, [r[low + step] for r in rights])
            return carry

        if len(blocks) == 1:
            body(0, 0)
        else:
            lax.fori_loop(0, len(blocks), body, 0)
        return len(blocks) * first.shape[2]
    put(0, [r[...] for r in rights])
    return first.shape[1]


def columns_at(start, width):
    return pl.ds(start if isinstance(start, int) else pl.multiple_of(start, LANES), width)


def grads_sent(plan, ins, outs, scratch):
    orders = ins[: 1 + max(which for which, _ in plan)]
    at, col = len(orders), 0
    out, turned = into(outs[0]), list(outs[1:])
    half = out.shape[0]
    for which, items in plan:
        for parts, done, blocks in items:
            lefts = ins[at : at + parts]
            at += parts
            made = []
            for left in lefts:
                left = use(left)
                if not done:
                    target = turned.pop(0)
                    ordered(into(target), use(orders[which]), left)
                    flush(target)
                    left = into(target)
                made.append(left)
            rights = [use(i) for i in ins[at : at + parts]]
            at += parts

            def put(start, values, col=col, made=made):
                total = None
                for left, value in zip(made, values):
                    term = nn(left[half:], value)
                    total = term if total is None else total + term
                out[:, columns_at(col + start, total.shape[1])] = total

            col += blocks_of(rights, blocks, put)


def grads_kept(plan, ins, outs, scratch):
    other, at, col = use(ins[0]), 1, 0
    half = other.shape[0]
    for n, (which, items) in enumerate(plan):
        sent, kept = into(outs[2 * n], outs[2 * n + 1])
        low, start = kept.shape[0], col
        for parts, done, blocks in items:
            lefts = [use(i) for i in ins[at : at + parts]]
            at += parts
            rights = [use(i) for i in ins[at : at + parts]]
            at += parts

            def put(first, values, col=col, lefts=lefts, sent=sent, kept=kept, start=start):
                total = None
                for left, value in zip(lefts, values):
                    term = nn(left[:half], value)
                    total = term if total is None else total + term
                width = total.shape[1]
                total = total + other[:, columns_at(col + first, width)]
                here = columns_at(col - start + first, width)
                sent[:, here] = total[low:]
                kept[:, here] = total[:low]

            col += blocks_of(rights, blocks, put)
        flush(outs[2 * n], outs[2 * n + 1])


def halve(ins, outs, scratch):
    for n in range(0, len(outs), 2):
        kept, other = use(*ins[n : n + 2])
        sent, out = into(*outs[n : n + 2])
        low = out.shape[0]
        out[...] = kept[0:low] + other[0:low]
        sent[...] = kept[low:] + other[low:]


def steps(chain, items, after=()):
    outs, args = [], []
    for h, n in items:
        half = shaped((h.kept[n].shape[0] // 2, h.columns[n]))
        outs += [(half, "v"), (half, "v")]
        args += [(h.kept[n], "v"), (h.other[n], "v")]
    made = chain(halve, outs, args, 0, "steps", after=after)
    for place, (h, n) in enumerate(items):
        h.kept[n] = made[2 * place + 1]
        h.swap(n, made[2 * place])


def ends(chain, items, shape):
    while items[0][0].bits[items[0][1]]:
        steps(chain, items)
    args = []
    for h, n in items:
        args += [(h.kept[n], "v"), (h.other[n], "v")]
    return chain(plain_end, [(shape, "v") for _ in items], args, 0, "ends")


def plain_end(ins, outs, scratch):
    for n, out in enumerate(outs):
        out[...] = use(ins[2 * n])[...] + use(ins[2 * n + 1])[...]


def cross_end(ins, outs, scratch):
    kept, other = use(*ins)
    own = outs[0].shape[1]
    out_grad, query_grad, key_value_grad = outs
    out_grad[...] = kept[:, :own] + other[:, :own]
    query_grad[...] = kept[:, own : 2 * own] + other[:, own : 2 * own]
    for n in range(2):
        at = slice((2 + n) * own, (3 + n) * own)
        key_value_grad[:, n, :] = kept[:, at] + other[:, at]


def self_end(ins, outs, scratch):
    kept, other = use(*ins)
    own = outs[0].shape[1]
    for n, out in enumerate(outs):
        at = slice(n * own, (n + 1) * own)
        out[...] = kept[:, at] + other[:, at]


def swap_mp(v):
    return lax.ppermute(v, "mp", [(0, 1), (1, 0)])


def swap_dp(v, bit, dp_size):
    return lax.ppermute(v, "dp", [(i, i ^ bit) for i in range(dp_size)])


def relative_source(width, bits):
    shard = width // (1 << len(bits))
    me = lax.axis_index("dp")
    place = jnp.arange(width, dtype=jnp.int32)
    block = place // shard
    owner = jnp.zeros_like(block)
    for step, bit in enumerate(bits):
        owner = owner + ((block >> (len(bits) - 1 - step)) & 1) * bit
    return (owner ^ me) * shard + place % shard


class Halving:
    def __init__(self, chain, orders, groups, dp_size, name):
        self.chain, self.groups, self.dp_size, self.name = chain, groups, dp_size, name
        self.plan = tuple(
            (place, tuple((len(lhs), ordered, blocks) for lhs, ordered, rhs, blocks in items)) for place, bits, items in groups
        )
        self.model = orders[0].shape[0]
        self.columns = [
            sum(rhs[0].shape[-1] * len(blocks) for lhs, ordered, rhs, blocks in items) for place, bits, items in groups
        ]
        orders = orders[: 1 + max(place for place, bits, items in groups)]
        args = [(order, "h") for order in orders]
        outs = [(shaped((self.model // 2, sum(self.columns))), "v")]
        for place, bits, items in groups:
            for lhs, ordered, rhs, blocks in items:
                args += [(p, "h") for p in lhs] + [(p, "h") for p in rhs]
                if not ordered:
                    outs += [(shaped(p.shape[::-1], BF), "h") for p in lhs]
        made = chain(partial(grads_sent, self.plan), outs, args, 0, name + "_sent")
        self.turned = list(made[1:])
        self.first = chain.swap_dp(made[0], groups[0][1][0], dp_size)
        self.bits = [list(bits[1:]) for place, bits, items in groups]
        self.kept, self.other = [None] * len(groups), [None] * len(groups)

    def swap(self, n, sent):
        self.other[n] = self.chain.swap_dp(sent, self.bits[n].pop(0), self.dp_size)

    def keep(self, after=()):
        args, outs = [(self.first, "v")], []
        turned = list(self.turned)
        for columns, (place, bits, items) in zip(self.columns, self.groups):
            for lhs, ordered, rhs, blocks in items:
                for p in lhs:
                    args.append((p if ordered else turned.pop(0), "h"))
                args += [(p, "h") for p in rhs]
            outs += [(shaped((self.model // 4, columns)), "v")] * 2
        made = self.chain(partial(grads_kept, self.plan), outs, args, 0, self.name + "_kept", after=after)
        for n in range(len(self.groups)):
            self.kept[n] = made[2 * n + 1]
            self.swap(n, made[2 * n])

    def step(self, n, after=()):
        half = shaped((self.kept[n].shape[0] // 2, self.columns[n]))
        sent, self.kept[n] = self.chain(
            halve, [(half, "v"), (half, "v")], [(self.kept[n], "v"), (self.other[n], "v")], 0, self.name + str(n) + "_step",
            after=after,
        )
        self.swap(n, sent)

    def end(self, n, finish, outs):
        while self.bits[n]:
            self.step(n)
        return self.chain(
            finish, [(o, "v") for o in outs], [(self.kept[n], "v"), (self.other[n], "v")], 0, self.name + str(n) + "_end"
        )


def on_device(
    dp_size,
    tokens,
    frames,
    lengths,
    out_cot,
    self_query_key_value,
    self_qv_bias,
    self_output_weight,
    cross_query_weight,
    cross_kv,
    cross_bias,
    cross_output_weight,
    first_dense_weight,
    first_dense_bias,
    second_dense_weight,
    out_biases,
    norm_gains,
    norm_biases,
):
    _, slot, model = tokens.shape
    tok, frames, cot = tokens[0], frames[0], out_cot[0]
    real = frames.shape[0]
    padded = -(-real // 256) * 256
    own = self_output_weight.shape[0]
    ff = second_dense_weight.shape[0]
    cut = slot // 2 // 64 * 64
    low_rows, high_rows = slice(0, cut), slice(cut, slot)
    w3 = self_query_key_value.transpose(1, 0, 2)
    w2kv = cross_kv.transpose(1, 0, 2)
    fb = first_dense_bias[None]
    gains, shifts, ob = norm_gains, norm_biases, out_biases
    bits = [1 << i for i in range(dp_size.bit_length() - 1)]
    turned_bits = bits[:1] + bits[2:] + bits[1:2]
    sources = jnp.stack([relative_source(model, bits), relative_source(model, turned_bits)], axis=1)
    chain = Chain(norm_gains)
    spot = (lax.axis_index("dp") & 3).astype(jnp.int32)
    spots = spot.reshape(1)

    def count(rows):
        return rows.stop - rows.start

    def sized(rows, width, dtype=F32):
        return shaped((count(rows), width), dtype)

    def attended(rows):
        return [(sized(rows, own, BF), "h"), (sized(rows, own), "h"), (shaped((8, count(rows))), "h"), (sized(rows, model), "v")]

    def fetched(weight, parts):
        block = weight.shape[0] // parts
        at = (spot & (parts - 1)) * block
        return swap_mp(lax.dynamic_slice_in_dim(weight, at, block, 0).astype(F32))

    made = chain(
        partial(self_start, cut),
        [(sized(low_rows, model, BF), "h"), (sized(high_rows, model, BF), "h")] + [(shaped((slot, own), BF), "h")] * 3
        + attended(high_rows),
        [(tok, "h"), (gains, "h"), (shifts, "h"), (self_qv_bias, "h"), (w3, "h"), (lengths, "s"), (self_output_weight, "h")],
        0,
        "self_start",
        scratch=[pltpu.VMEM((count(high_rows), LANES), F32), pltpu.VMEM((slot, model), BF)],
    )
    x1_l, x1_h, q1, k1, v1, mix1_h, out1_h, lse1_h, part1_h = made
    other1_h = chain.swap_mp(part1_h)
    mix1_l, out1_l, lse1_l, part1_l = chain(
        partial(self_next, low_rows),
        attended(low_rows),
        [(q1, "h"), (k1, "h"), (v1, "h"), (lengths, "s"), (self_output_weight, "h")],
        0,
        "self_next",
        scratch=[pltpu.VMEM((count(low_rows), LANES), F32)],
    )
    other1_l = chain.swap_mp(part1_l)
    k2, v2, turned_frames, order, order_turned = chain(
        frames_start,
        [(shaped((padded, own), BF), "h")] * 2 + [(shaped((model, padded), BF), "h")] + [(shaped((model, model), BF), "h")] * 2,
        [(frames, "h"), (w2kv, "h"), (cross_bias, "h"), (sources, "h")],
        0,
        "frames_start",
        scratch=[pltpu.VMEM((padded, model), BF)],
    )
    orders = (order, order_turned)

    def turned(plan, parts):
        used = orders[: 1 + max(place for place, _ in plan)]
        return chain(
            partial(turn, plan),
            [(shaped((model, parts[part].shape[0]), BF), "h") for _, part in plan],
            [(o, "h") for o in used] + [(p, "h") for p in parts],
            0,
            "turn",
        )


    def cross(rows, mine, other):
        return chain(
            partial(cross_start, rows, real),
            [(sized(rows, model), "h"), (sized(rows, model, BF), "h"), (sized(rows, own, BF), "h")] + attended(rows),
            [(mine, "v"), (other, "v"), (tok, "h"), (ob, "h"), (gains, "h"), (shifts, "h"), (cross_bias, "h"),
             (cross_query_weight, "h"), (k2, "h"), (v2, "h"), (cross_output_weight, "h")],
            0,
            "cross_start",
            scratch=[pltpu.VMEM((count(rows), LANES), F32)],
        )

    s1_h, x2_h, q2_h, mix2_h, out2_h, lse2_h, part2_h = cross(high_rows, part1_h, other1_h)
    other2_h = chain.swap_mp(part2_h)
    s1_l, x2_l, q2_l, mix2_l, out2_l, lse2_l, part2_l = cross(low_rows, part1_l, other1_l)
    other2_l = chain.swap_mp(part2_l)
    x1t_h, x1t_l, x2t_h, x2t_l = turned(((0, 0), (0, 1), (0, 2), (0, 3)), (x1_h, x1_l, x2_h, x2_l))

    def dense(rows, s1, mine, other):
        return chain(
            dense_start,
            [(sized(rows, model), "h"), (sized(rows, model, BF), "h"), (sized(rows, ff, BF), "h"), (sized(rows, ff), "h"),
             (sized(rows, model), "v")],
            [(mine, "v"), (other, "v"), (s1, "h"), (ob, "h"), (gains, "h"), (shifts, "h"), (fb, "h"),
             (first_dense_weight, "h"), (second_dense_weight, "h")],
            0,
            "dense_start",
        )

    s2_h, x3_h, act_h, slope_h, part3_h = dense(high_rows, s1_h, part2_h, other2_h)
    other3_h = chain.swap_mp(part3_h)
    s2_l, x3_l, act_l, slope_l, part3_l = dense(low_rows, s1_l, part2_l, other2_l)
    other3_l = chain.swap_mp(part3_l)
    x3o_h, x3o_l = turned(((1, 0), (1, 1)), (x3_h, x3_l))

    def dense_b(rows, s2, mine, other, slope):
        return chain(
            partial(dense_back, rows),
            [(sized(rows, model, BF), "h"), (sized(rows, model), "h"), (sized(rows, model, BF), "h"),
             (sized(rows, ff, BF), "h"), (sized(rows, model), "v"), (shaped((8, model)), "v"), (shaped((8, ff)), "v")],
            [(mine, "v"), (other, "v"), (s2, "h"), (ob, "h"), (gains, "h"), (shifts, "h"), (cot, "h"), (lengths, "s"),
             (second_dense_weight, "h"), (slope, "h"), (first_dense_weight, "h")],
            6 * count(rows) * model * ff,
            "dense_back",
        )

    y_h, g3_h, low3_h, hid_h, part4_h, sum3_h, hsum_h = dense_b(high_rows, s2_h, part3_h, other3_h, slope_h)
    other4_h = chain.swap_mp(part4_h)
    y_l, g3_l, low3_l, hid_l, part4_l, sum3_l, hsum_l = dense_b(low_rows, s2_l, part3_l, other3_l, slope_l)

    denses = Halving(
        chain,
        orders,
        [
            (0, bits, [((low3_h, low3_l), False, (act_h, act_l), (0,))]),
            (1, turned_bits, [((x3o_h, x3o_l), True, (hid_h, hid_l), (0,))]),
        ],
        dp_size,
        "dense",
    )
    other4_l = chain.swap_mp(chain.tie(part4_l))
    wq_0 = chain.later(lambda tied=chain.tie(cross_query_weight): fetched(tied, 2))
    chain.pause(other4_h)
    denses.keep()
    all_rows = slice(0, slot)

    def block_sizes(dtype, width):
        return [(sized(high_rows, width, dtype), "h"), (sized(low_rows, width, dtype), "h")]

    heads = [pltpu.VMEM((slot, own), BF), pltpu.VMEM((slot, own), F32)]
    joined = [pltpu.VMEM((slot, own), BF), pltpu.VMEM((slot, own), F32), pltpu.VMEM((8, slot), F32)]
    which = lax.axis_index("mp").astype(jnp.int32).reshape(1)
    half_width = model // 2
    cuts = [-(-real * n // (8 * PIECES)) * 8 for n in range(PIECES)] + [-(-real // 8) * 8]
    g2_h, low2_h, g2_l, low2_l, lq2_h, lq2_l, part5, sum2, lk2, lv2, *frames_parts = chain(
        partial(cross_back, cut, real),
        [(sized(high_rows, model), "h"), (sized(high_rows, model, BF), "h"), (sized(low_rows, model), "h"),
         (sized(low_rows, model, BF), "h")] + block_sizes(BF, own)
        + [(shaped((slot, own)), "v"), (shaped((8, model)), "v")] + [(shaped((padded, own), BF), "h")] * 2
        + [(shaped((cuts[n + 1] - cuts[n], half_width)), "r") for n in range(PIECES)],
        [(part4_h, "h"), (other4_h, "h"), (s2_h, "h"), (g3_h, "h"), (q2_h, "h"), (out2_h, "h"), (lse2_h, "h"),
         (part4_l, "h"), (other4_l, "h"), (s2_l, "h"), (g3_l, "h"), (q2_l, "h"), (out2_l, "h"), (lse2_l, "h"),
         (gains, "h"), (cross_output_weight, "h"), (k2, "h"), (v2, "h"), (which, "s"), (w2kv, "h")],
        0,
        "cross_back",
        scratch=heads + joined + [pltpu.VMEM((padded, half_width), F32), pltpu.SemaphoreType.DMA((PIECES,))],
    )
    other5 = chain.swap_mp(part5)
    wq_1 = chain.later(lambda tied=chain.link: swap_dp(lax.optimization_barrier((wq_0.value, tied))[0], 1, dp_size))
    steps(chain, [(denses, 0), (denses, 1)], (wq_0,))
    crosses = Halving(
        chain,
        orders,
        [
            (
                0,
                bits,
                [
                    ((low2_h, low2_l), False, (mix2_h, mix2_l), (0,)),
                    ((x2t_h, x2t_l), True, (lq2_h, lq2_l), (0,)),
                    ((turned_frames,), True, (lk2,), (0,)),
                    ((turned_frames,), True, (lv2,), (0,)),
                ],
            )
        ],
        dp_size,
        "cross",
    )
    frames_other = [chain.swap_mp(chain.tie(frames_parts[0]))]
    chain.pause(other5)
    crosses.keep()
    frames_other.append(chain.swap_mp(chain.tie(frames_parts[1])))
    g1_h, low1_h, g1_l, low1_l, l3_h, l3_l, part6_h, part6_l, sum1 = chain(
        partial(self_back, cut),
        [(sized(high_rows, model), "h"), (sized(high_rows, model, BF), "h"), (sized(low_rows, model), "h"),
         (sized(low_rows, model, BF), "h"), (shaped((3, count(high_rows), own), BF), "h"),
         (shaped((3, count(low_rows), own), BF), "h"), (sized(high_rows, model), "v"), (sized(low_rows, model), "v"),
         (shaped((8, model)), "v")],
        [(spots, "s"), (part5, "h"), (other5, "h"), (cross_query_weight, "h"), (wq_0, "h"), (wq_1, "h"), (gains, "h"),
         (self_output_weight, "h"), (q1, "h"), (k1, "h"), (v1, "h"), (w3, "h"), (lengths, "s"),
         (s1_h, "h"), (g2_h, "h"), (out1_h, "h"), (lse1_h, "h"), (s1_l, "h"), (g2_l, "h"), (out1_l, "h"), (lse1_l, "h")],
        0,
        "self_back",
        scratch=heads + [pltpu.VMEM((model, own), BF)] + joined + [pltpu.VMEM((2, slot, own), BF), pltpu.VMEM((slot, model), F32)],
    )
    other6_h = chain.swap_mp(part6_h)
    steps(chain, [(denses, 0), (denses, 1)], (frames_other[0],))
    selves = Halving(
        chain,
        orders,
        [
            (
                0,
                bits,
                [((low1_h, low1_l), False, (mix1_h, mix1_l), (0,)), ((x1t_h, x1t_l), True, (l3_h, l3_l), (0,))],
            ),
            (0, bits, [((x1t_h, x1t_l), True, (l3_h, l3_l), (1, 2))]),
        ],
        dp_size,
        "self",
    )
    other6_l = chain.swap_mp(chain.tie(part6_l))
    shard = model // dp_size
    crosses.step(0, (frames_other[1],))
    t_high, sum0_h = chain(
        partial(tokens_end, high_rows),
        [(sized(high_rows, model), "h"), (shaped((8, model)), "h")],
        [(tok, "h"), (gains, "h"), (g1_h, "h"), (part6_h, "v"), (other6_h, "v"), (lengths, "s")],
        0,
        "tokens_end",
        scratch=[pltpu.VMEM((8, model), F32)],
    )
    second_turned, first_grad = ends(chain, [(denses, 0), (denses, 1)], shaped((shard, ff)))
    selves.keep()
    tokens_grad, total, y = chain(
        partial(tokens_end, low_rows),
        [(shaped((slot, model)), "h"), (shaped((13 + ff // model, model)), "v"), (shaped((slot, model), BF), "h")],
        [(tok, "h"), (gains, "h"), (g1_l, "h"), (part6_l, "v"), (other6_l, "v"), (t_high, "h"), (sum0_h, "h"),
         (sum1, "h"), (sum2, "h"), (sum3_h, "h"), (sum3_l, "h"), (hsum_h, "h"), (hsum_l, "h"), (y_l, "h"), (y_h, "h")],
        0,
        "tokens_end",
        scratch=[pltpu.VMEM((8, model), F32)],
    )
    small_bits = list(bits)

    def small_step(total, other):
        (total,) = chain(plain_end, [(shaped(total.shape), "v")], [(total, "v"), (other, "v")], 0, "small_step")
        return total, chain.swap_dp(total, small_bits.pop(0), dp_size)

    small_other = chain.swap_dp(total, small_bits.pop(0), dp_size)
    frames_other.append(chain.swap_mp(chain.tie(frames_parts[2])))
    crosses.step(0)
    selves.step(0)
    total, small_other = small_step(total, small_other)
    frames_other.append(chain.swap_mp(chain.tie(frames_parts[3])))
    selves.step(1, (frames_other[2],))
    cross_out_grad, cross_q_grad, cross_kv_grad = crosses.end(
        0, cross_end, [shaped((shard, own)), shaped((shard, own)), shaped((shard, 2, own))]
    )
    selves.step(0)
    total, small_other = small_step(total, small_other)
    selves.step(1)
    while small_bits:
        total, small_other = small_step(total, small_other)
    (frames_grad,) = chain(
        frames_kept, [(shaped((real, 1, half_width)), "r")],
        [(which, "s"), (lk2, "h"), (lv2, "h"), (w2kv, "h")] + [(o, "h") for o in frames_other],
        0, "frames_kept",
        scratch=[pltpu.VMEM((padded, half_width), F32), pltpu.VMEM((real, half_width), F32), pltpu.SemaphoreType.DMA],
    )
    self_out_grad, q_grad = selves.end(0, self_end, [shaped((shard, own))] * 2)
    k_grad, v_grad = selves.end(1, self_end, [shaped((shard, own))] * 2)
    gains_grad, shifts_grad, ob_grad, svb_grad, cvb_grad, fb_grad = chain(
        small_end,
        [(shaped((4, model)), "v"), (shaped((4, model)), "v"), (shaped((3, model)), "v"), (shaped((2, own)), "v"),
         (shaped((2, own)), "v"), (shaped((ff // model, model)), "v")],
        [(total, "v"), (small_other, "v")],
        0,
        "small_end",
    )
    return (
        y[None],
        tokens_grad[None],
        frames_grad.transpose(1, 0, 2),
        jnp.stack([q_grad, k_grad, v_grad], axis=1),
        svb_grad,
        self_out_grad.T,
        cross_q_grad,
        cross_kv_grad,
        cvb_grad,
        cross_out_grad.T,
        first_grad,
        fb_grad.reshape(ff),
        second_turned.T,
        ob_grad,
        gains_grad,
        shifts_grad,
    )


def solution(mesh):
    in_specs = (
        P("dp", None, None),
        P("dp", None, None),
        P("dp"),
        P("dp", None, None),
        P(None, None, "mp"),
        P(None, "mp"),
        P("mp", None),
        P(None, "mp"),
        P(None, None, "mp"),
        P(None, "mp"),
        P("mp", None),
        P(None, "mp"),
        P("mp"),
        P("mp", None),
        P(),
        P(),
        P(),
    )
    out_specs = (
        P("dp", None, None),
        P("dp", None, None),
        P("dp", None, "mp"),
        P("dp", None, "mp"),
        P(None, "mp"),
        P("mp", "dp"),
        P("dp", "mp"),
        P("dp", None, "mp"),
        P(None, "mp"),
        P("mp", "dp"),
        P("dp", "mp"),
        P("mp"),
        P("mp", "dp"),
        P(),
        P(),
        P(),
    )
    return jax.shard_map(
        partial(on_device, mesh.shape["dp"]),
        mesh=mesh,
        in_specs=in_specs,
        out_specs=out_specs,
        check_vma=False,
    )
```

profile of v0, /device:TPU:0, one launch (start us, length us, event | category | flops | bytes accessed | tf_op | source)
XLA Modules:
  0.0 276.3 jit_solution(8527540528085749306)
XLA Ops:
  1.3 7.1 %self_start.1 = (f32[8,128]{1,0:T(8,128)}, bf16[192,768]{1,0:T(8,128)(2,1)}, bf16[256,768]{1,0:T(8,128)(2,1)}, bf16[448,384]{1,0:T(8,128)(2,1)}, bf16[448,384]{1...) custom-call(f32[4,768]{1,0:T(4,128)} %refs_2_.5, ...), custom_call_target="tpu_custom_call" | custom-call | flops 30000001024 | bytes 192000000 | tf_op jit(solution)/shard_map/self_start/pallas_call | solution.py:171
  8.4 3.0 %collective-permute-start = (f32[256,768]{1,0:T(8,128)S(1)}, f32[256,768]{1,0:T(8,128)S(1)}, u32[]{:S(2)}, u32[]{:S(2)}) collective-permute-start(f32[256,768]{1,0:T(8,128)S(1)} %get-tuple-element.215.refs_1_), channel_id=1, source_target_pairs={{0,1},{1,0},{2,3},{3,2},{4,5},{5,4},{6,7},{7,6},{8,9},{9,8},{10,11... | collective-permute-start | bytes 2359304 | tf_op jit(solution)/shard_map/ppermute | solution.py:847
  11.4 4.2 %self_next.1 = (f32[8,128]{1,0:T(8,128)}, bf16[192,384]{1,0:T(8,128)(2,1)}, f32[192,384]{1,0:T(8,128)}, f32[8,192]{1,0:T(8,128)}, f32[192,768]{1,0:T(8,128)S(1)}) custom-call(f32[8,128]{1,0:T(8,128)} %get-tuple-element.209.refs_0_, bf16[448,384]{1,0:T(8,128)(2,1)} %get-tuple-element.210.refs_1_.refs_9_, ...), custom_call_target="tpu_custom_call" | custom-call | flops 19499999232 | bytes 124800000 | tf_op jit(solution)/shard_map/self_next/pallas_call | solution.py:171
  15.7 1.2 copy.37
  16.9 0.9 copy.35.refs_4_
  17.8 8.9 %frames_start.1 = (f32[8,128]{1,0:T(8,128)}, bf16[1536,384]{1,0:T(8,128)(2,1)}, bf16[1536,384]{1,0:T(8,128)(2,1)}, bf16[768,1536]{1,0:T(8,128)(2,1)}, bf16[768,7...) custom-call(f32[8,128]{1,0:T(8,128)} %get-tuple-element.213.refs_0_, bf16[1500,768]{1,0:T(8,128)(2,1)} %bitcast.24, ...), custom_call_target="tpu_custom_call" | custom-call | flops 44999999488 | bytes 288000000 | tf_op jit(solution)/shard_map/frames_start/pallas_call | solution.py:171
  27.4 2.4 collective-permute-done.refs_2_
  29.8 7.6 %cross_start.2 = (f32[8,128]{1,0:T(8,128)}, f32[256,768]{1,0:T(8,128)}, bf16[256,768]{1,0:T(8,128)(2,1)}, bf16[256,384]{1,0:T(8,128)(2,1)}, bf16[256,384]{1,0:T(...) custom-call(f32[8,128]{1,0:T(8,128)} %get-tuple-element.214.refs_0_, ...), custom_call_target="tpu_custom_call" | custom-call | flops 40499998720 | bytes 259200000 | tf_op jit(solution)/shard_map/cross_start/pallas_call | solution.py:171
  37.4 2.1 collective-permute-start.2
  39.5 2.9 %collective-permute-done.1.refs_2_ = f32[192,768]{1,0:T(8,128)S(1)} collective-permute-done((f32[192,768]{1,0:T(8,128)S(1)}, f32[192,768]{1,0:T(8,128)S(1)}, u32[]{:S(2)}, u32[]{:S(2)}) %collective-permute-start.1) | collective-permute-done | bytes 589856 | tf_op jit(solution)/shard_map/ppermute | solution.py:847
  42.4 6.9 %cross_start.3 = (f32[8,128]{1,0:T(8,128)}, f32[192,768]{1,0:T(8,128)}, bf16[192,768]{1,0:T(8,128)(2,1)}, bf16[192,384]{1,0:T(8,128)(2,1)}, bf16[192,384]{1,0:T(...) custom-call(f32[8,128]{1,0:T(8,128)} %get-tuple-element.218.refs_0_, ...), custom_call_target="tpu_custom_call" | custom-call | flops 40499998720 | bytes 259200000 | tf_op jit(solution)/shard_map/cross_start/pallas_call | solution.py:171
  49.3 2.1 collective-permute-start.3
  51.4 5.7 %turn.2 = (f32[8,128]{1,0:T(8,128)}, bf16[768,256]{1,0:T(8,128)(2,1)}, bf16[768,192]{1,0:T(8,128)(2,1)}, bf16[768,256]{1,0:T(8,128)(2,1)}, bf16[768,192]{1,0:T(8,128)(2,1)}) custom-call(f32[8,128]{1,0:T(8,128)} %get-tuple-element.220.refs_0_, bf16[768,768]{1,0:T(8,128)(2,1)} %get-tuple-element.221.refs_1_, bf16[256,768]{1,0:T(8,128)(2,1)} %get-tuple-element.222.refs_2_, ...), custom_call_target="tpu_custom_call" | custom-call | flops 15000000512 | bytes 96000000 | tf_op jit(solution)/shard_map/turn/pallas_call | solution.py:171
  57.1 2.1 collective-permute-done.2.refs_2_
  59.3 7.4 %dense_start.2 = (f32[8,128]{1,0:T(8,128)}, f32[256,768]{1,0:T(8,128)}, bf16[256,768]{1,0:T(8,128)(2,1)}, bf16[256,1536]{1,0:T(8,128)(2,1)}, f32[256,1536]{1,0:T(8,128)}, /*index=5*/f32[256,768]{1,0:T(8,128)S(1)}) custom-call(f32[8,128]{1,0:T(8,128)} %get-tuple-element.226.refs_0_, f32[256,768]{1,0:T(8,128)S(1)} %get-tuple-element.227.refs_1_, ...), custom_call_target="tpu_custom_call" | custom-call | flops 35999997952 | bytes 230400000 | tf_op jit(solution)/shard_map/dense_start/pallas_call | solution.py:171
  66.7 2.1 collective-permute-start.4
  68.8 3.1 %collective-permute-done.3.refs_2_ = f32[192,768]{1,0:T(8,128)S(1)} collective-permute-done((f32[192,768]{1,0:T(8,128)S(1)}, f32[192,768]{1,0:T(8,128)S(1)}, u32[]{:S(2)}, u32[]{:S(2)}) %collective-permute-start.3) | collective-permute-done | bytes 589856 | tf_op jit(solution)/shard_map/ppermute | solution.py:847
  71.9 6.6 %dense_start.3 = (f32[8,128]{1,0:T(8,128)}, f32[192,768]{1,0:T(8,128)}, bf16[192,768]{1,0:T(8,128)(2,1)}, bf16[192,1536]{1,0:T(8,128)(2,1)}, f32[192,1536]{1,0:T(8,128)}, /*index=5*/f32[192,768]{1,0:T(8,128)S(1)}) custom-call(f32[8,128]{1,0:T(8,128)} %get-tuple-element.229.refs_0_, f32[192,768]{1,0:T(8,128)S(1)} %get-tuple-element.230.refs_1_, ...), custom_call_target="tpu_custom_call" | custom-call | flops 35999997952 | bytes 230400000 | tf_op jit(solution)/shard_map/dense_start/pallas_call | solution.py:171
  78.6 2.1 collective-permute-start.5
  80.7 4.3 %turn.3 = (f32[8,128]{1,0:T(8,128)}, bf16[768,256]{1,0:T(8,128)(2,1)}, bf16[768,192]{1,0:T(8,128)(2,1)}) custom-call(f32[8,128]{1,0:T(8,128)} %get-tuple-element.232.refs_0_, bf16[768,768]{1,0:T(8,128)(2,1)} %get-tuple-element.221.refs_1_, bf16[768,768]{1,0:T(8,128)(2,1)} %get-tuple-element.233.refs_2_, bf16[256,768]{1,0:T(8,128)(2,1)} %get-tuple-element.234.refs_3_, ...), custom_call_target="tpu_custom_call" | custom-call | flops 15000000512 | bytes 96000000 | tf_op jit(solution)/shard_map/turn/pallas_call | solution.py:171
  85.0 3.8 %collective-permute-done.4.refs_2_ = f32[256,768]{1,0:T(8,128)S(1)} collective-permute-done((f32[256,768]{1,0:T(8,128)S(1)}, f32[256,768]{1,0:T(8,128)S(1)}, u32[]{:S(2)}, u32[]{:S(2)}) %collective-permute-start.4) | collective-permute-done | bytes 786464 | tf_op jit(solution)/shard_map/ppermute | solution.py:847
  88.8 7.3 %dense_back.2 = (f32[8,128]{1,0:T(8,128)}, bf16[256,768]{1,0:T(8,128)(2,1)}, f32[256,768]{1,0:T(8,128)}, bf16[256,768]{1,0:T(8,128)(2,1)}, bf16[256,1536]{1,0:T(...) custom-call(f32[8,128]{1,0:T(8,128)} %get-tuple-element.236.refs_0_, ...), custom_call_target="tpu_custom_call" | custom-call | flops 35999997952 | bytes 230400000 | tf_op jit(solution)/shard_map/dense_back/pallas_call | solution.py:171
  96.1 2.1 collective-permute-start.6
  98.2 3.2 %collective-permute-done.5.refs_2_ = f32[192,768]{1,0:T(8,128)S(1)} collective-permute-done((f32[192,768]{1,0:T(8,128)S(1)}, f32[192,768]{1,0:T(8,128)S(1)}, u32[]{:S(2)}, u32[]{:S(2)}) %collective-permute-start.5) | collective-permute-done | bytes 589856 | tf_op jit(solution)/shard_map/ppermute | solution.py:847
  101.4 7.7 %dense_back.3 = (f32[8,128]{1,0:T(8,128)}, bf16[192,768]{1,0:T(8,128)(2,1)}, f32[192,768]{1,0:T(8,128)}, bf16[192,768]{1,0:T(8,128)(2,1)}, bf16[192,1536]{1,0:T(...) custom-call(f32[8,128]{1,0:T(8,128)} %get-tuple-element.240.refs_0_, ...), custom_call_target="tpu_custom_call" | custom-call | flops 35999997952 | bytes 230400000 | tf_op jit(solution)/shard_map/dense_back/pallas_call | solution.py:171
  110.4 5.2 %dense_sent.1 = (f32[8,128]{1,0:T(8,128)}, f32[384,3072]{1,0:T(8,128)S(1)}, bf16[768,256]{1,0:T(8,128)(2,1)}, bf16[768,192]{1,0:T(8,128)(2,1)}) custom-call(f32[8,128]{1,0:T(8,128)} %get-tuple-element.244.refs_0_, bf16[768,768]{1,0:T(8,128)(2,1)} %get-tuple-element.221.refs_1_, bf16[768,768]{1,0:T(8,128)(2,1)} %get-tuple-element.233.refs_2_, ...), custom_call_target="tpu_custom_call" | custom-call | flops 89999998976 | bytes 576000000 | tf_op jit(solution)/shard_map/dense_sent/pallas_call | solution.py:171
  115.6 2.1 collective-permute-start.8
  118.6 0.9 copy-done.11
  119.6 3.9 %collective-permute-done.7.refs_1_ = f32[384,3072]{1,0:T(8,128)S(1)} collective-permute-done((f32[384,3072]{1,0:T(8,128)S(1)}, f32[384,3072]{1,0:T(8,128)S(1)}, u32[]{:S(2)}, u32[]{:S(2)}) %collective-permute-start.7) | collective-permute-done | bytes 4718624 | tf_op jit(solution)/shard_map/ppermute | solution.py:851
  123.5 4.2 %dense_kept.1 = (f32[8,128]{1,0:T(8,128)}, f32[192,1536]{1,0:T(8,128)}, f32[192,1536]{1,0:T(8,128)S(1)}, f32[192,1536]{1,0:T(8,128)}, f32[192,1536]{1,0:T(8,128)S(1)}) custom-call(f32[8,128]{1,0:T(8,128)} %pause.2.refs_0_, f32[384,3072]{1,0:T(8,128)S(1)} %collective-permute-done.7.refs_1_, bf16[768,256]{1,0:T(8,128)(2,1)} %get-tuple-element.256.refs_2_, ...), custom_call_target="tpu_custom_call" | custom-call | flops 89999998976 | bytes 576000000 | tf_op jit(solution)/shard_map/dense_kept/pallas_call | solution.py:171
  127.7 2.1 collective-permute-start.10
  129.9 1.6 collective-permute-start.11
  132.2 22.6 %cross_back.1 = (f32[8,128]{1,0:T(8,128)}, f32[256,768]{1,0:T(8,128)}, bf16[256,768]{1,0:T(8,128)(2,1)}, f32[192,768]{1,0:T(8,128)}, bf16[192,768]{1,0:T(8,128)(...) custom-call(f32[8,128]{1,0:T(8,128)} %get-tuple-element.258.refs_0_,, ...), custom_call_target="tpu_custom_call" | custom-call | flops 299999985664 | bytes 1920000000 | tf_op jit(solution)/shard_map/cross_back/pallas_call | solution.py:171
  154.9 2.0 collective-permute-start.12
  156.9 1.0 collective-permute-done.11.refs_5_
  157.9 2.9 %steps.2 = (f32[8,128]{1,0:T(8,128)}, f32[96,1536]{1,0:T(8,128)}, f32[96,1536]{1,0:T(8,128)S(1)}, f32[96,1536]{1,0:T(8,128)}, f32[96,1536]{1,0:T(8,128)S(1)}) custom-call(f32[8,128]{1,0:T(8,128)} %get-tuple-element.269.refs_0_, f32[384,384]{1,0:T(8,128)} %collective-permute-done.9.refs_1_.refs_5_, f32[192,1536]{1,0:T(8,128)S(1)} %get-tuple-element.271.refs_2_, ...), custom_call_target="tpu_custom_call" | custom-call | flops 15000000512 | bytes 96000000 | tf_op jit(solution)/shard_map/steps/pallas_call | solution.py:171
  160.8 5.8 %cross_sent.1 = (f32[8,128]{1,0:T(8,128)}, f32[384,1536]{1,0:T(8,128)S(1)}, bf16[768,256]{1,0:T(8,128)(2,1)}, bf16[768,192]{1,0:T(8,128)(2,1)}) custom-call(f32[8,128]{1,0:T(8,128)} %get-tuple-element.275.refs_0_, bf16[768,768]{1,0:T(8,128)(2,1)} %get-tuple-element.221.refs_1_, bf16[256,768]{1,0:T(8,128)(2,1)} %get-tuple-element.276.refs_2_, ...), custom_call_target="tpu_custom_call" | custom-call | flops 89999998976 | bytes 576000000 | tf_op jit(solution)/shard_map/cross_sent/pallas_call | solution.py:171
  166.7 1.6 collective-permute-start.15
  168.2 1.6 collective-permute-start.16
  169.8 3.5 %collective-permute-done.12.refs_1_.refs_3_ = f32[448,384]{1,0:T(8,128)S(1)} collective-permute-done((f32[448,384]{1,0:T(8,128)S(1)}, f32[448,384]{1,0:T(8,128)S(1)}, u32[]{:S(2)}, u32[]{:S(2)}) %collective-permute-start.12) | collective-permute-done | bytes 688160 | tf_op jit(solution)/shard_map/ppermute | solution.py:847
  173.3 3.0 %collective-permute-start.17 = (f32[96,1536]{1,0:T(8,128)}, f32[96,1536]{1,0:T(8,128)}, u32[]{:S(2)}, u32[]{:S(2)}) collective-permute-start(f32[96,1536]{1,0:T(8,128)} %get-tuple-element.306), channel_id=1, source_target_pairs={{0,16},{2,18},{4,20},{6,22},{8,24},{10,26},{12,28},{14,30},{16,0},... | collective-permute-start | bytes 1769480 | tf_op jit(solution)/shard_map/ppermute | solution.py:851
  176.4 5.6 %cross_kept.1 = (f32[8,128]{1,0:T(8,128)}, f32[192,1536]{1,0:T(8,128)}, f32[192,1536]{1,0:T(8,128)S(1)}) custom-call(f32[8,128]{1,0:T(8,128)} %pause.3.refs_0_, f32[384,1536]{1,0:T(8,128)S(1)} %collective-permute-done.13.refs_1_, bf16[768,256]{1,0:T(8,128)(2,1)} %get-tuple-element.290.refs_2_, bf16[768,192]{1,0:T(8,128)(2,1)} %get-tuple-element.291.refs_3_, ...), custom_call_target="tpu_custom_call" | custom-call | flops 74999996416 | bytes 480000000 | tf_op jit(solution)/shard_map/cross_kept/pallas_call | solution.py:171
  182.0 1.6 collective-permute-start.18
  183.5 1.5 collective-permute-start.19
  185.1 14.5 %self_back.1 = (f32[8,128]{1,0:T(8,128)}, f32[256,768]{1,0:T(8,128)}, bf16[256,768]{1,0:T(8,128)(2,1)}, f32[192,768]{1,0:T(8,128)}, bf16[192,768]{1,0:T(8,128)(2...) custom-call(f32[8,128]{1,0:T(8,128)} %get-tuple-element.292.refs_0_,, ...), custom_call_target="tpu_custom_call" | custom-call | flops 179999997952 | bytes 1152000000 | tf_op jit(solution)/shard_map/self_back/pallas_call | solution.py:171
  200.7 2.1 steps.3
  202.9 0.9 collective-permute-start.21
  204.3 4.7 %self_sent.1 = (f32[8,128]{1,0:T(8,128)}, f32[384,1536]{1,0:T(8,128)S(1)}, bf16[768,256]{1,0:T(8,128)(2,1)}, bf16[768,192]{1,0:T(8,128)(2,1)}) custom-call(f32[8,128]{1,0:T(8,128)} %get-tuple-element.307.refs_0_, bf16[768,768]{1,0:T(8,128)(2,1)} %get-tuple-element.221.refs_1_, bf16[256,768]{1,0:T(8,128)(2,1)} %get-tuple-element.308.refs_2_, ...), custom_call_target="tpu_custom_call" | custom-call | flops 74999996416 | bytes 480000000 | tf_op jit(solution)/shard_map/self_sent/pallas_call | solution.py:171
  209.1 1.7 collective-permute-done.19.refs_3_
  211.3 2.3 cross0_step.2
  213.6 4.6 %collective-permute-done.20.refs_5_ = f32[256,768]{1,0:T(8,128)S(1)} collective-permute-done((f32[256,768]{1,0:T(8,128)S(1)}, f32[256,768]{1,0:T(8,128)S(1)}, u32[]{:S(2)}, u32[]{:S(2)}) %collective-permute-start.20) | collective-permute-done | bytes 786464 | tf_op jit(solution)/shard_map/ppermute | solution.py:847
  218.3 3.0 %tokens_end.2 = (f32[8,128]{1,0:T(8,128)}, f32[256,768]{1,0:T(8,128)}, f32[8,768]{1,0:T(8,128)}) custom-call(f32[8,128]{1,0:T(8,128)} %get-tuple-element.321.refs_0_, bf16[448,768]{1,0:T(8,128)(2,1)} %bitcast.32, f32[4,768]{1,0:T(4,128)} %refs_2_.5, f32[256,768]{1,0:T(8,128)} %get-tuple-element.322.refs_3_, f32[256,768]{1,0:T(8,128)S(1)} %get-tuple-element.323.refs_4_, ...), custom_call_target="tpu_custom_call" | custom-call | flops 74999996416 | bytes 480000000 | tf_op jit(solution)/shard_map/tokens_end/pallas_call | solution.py:171
  221.4 1.9 ends.1
  223.3 3.3 %self_kept.1 = (f32[8,128]{1,0:T(8,128)}, f32[192,768]{1,0:T(8,128)S(1)}, f32[192,768]{1,0:T(8,128)S(1)}, f32[192,768]{1,0:T(8,128)S(1)}, f32[192,768]{1,0:T(8,128)S(1)}) custom-call(f32[8,128]{1,0:T(8,128)} %get-tuple-element.329.refs_0_, f32[384,1536]{1,0:T(8,128)S(1)} %collective-permute-done.23.refs_1_, bf16[768,256]{1,0:T(8,128)(2,1)} %get-tuple-element.331.refs_2_, ...), custom_call_target="tpu_custom_call" | custom-call | flops 60000002048 | bytes 384000000 | tf_op jit(solution)/shard_map/self_kept/pallas_call | solution.py:171
  228.0 5.0 %tokens_end.3 = (f32[8,128]{1,0:T(8,128)}, f32[448,768]{1,0:T(8,128)}, f32[15,768]{1,0:T(8,128)S(1)}, bf16[448,768]{1,0:T(8,128)(2,1)}) custom-call(f32[8,128]{1,0:T(8,128)} %get-tuple-element.333.refs_0_, bf16[448,768]{1,0:T(8,128)(2,1)} %bitcast.33, f32[4,768]{1,0:T(4,128)} %refs_2_.5, f32[192,768]{1,0:T(8,128)} %get-tuple-element.334.refs_3_, ...), custom_call_target="tpu_custom_call" | custom-call | flops 74999996416 | bytes 480000000 | tf_op jit(solution)/shard_map/tokens_end/pallas_call | solution.py:171
  234.5 1.1 cross0_step.3
  235.6 2.7 collective-permute-start.30
  238.3 3.9 %collective-permute-done.26.refs_2_ = f32[192,768]{1,0:T(8,128)S(1)} collective-permute-done((f32[192,768]{1,0:T(8,128)S(1)}, f32[192,768]{1,0:T(8,128)S(1)}, u32[]{:S(2)}, u32[]{:S(2)}) %collective-permute-start.26) | collective-permute-done | bytes 589856 | tf_op jit(solution)/shard_map/ppermute | solution.py:851
  242.7 5.9 %collective-permute-done.28.refs_1_.refs_7_ = f32[376,384]{1,0:T(8,128)S(1)} collective-permute-done((f32[376,384]{1,0:T(8,128)S(1)}, f32[376,384]{1,0:T(8,128)S(1)}, u32[]{:S(2)}, u32[]{:S(2)}) %collective-permute-start.28) | collective-permute-done | bytes 577568 | tf_op jit(solution)/shard_map/ppermute | solution.py:847
  248.6 3.9 %collective-permute-done.29.refs_3_ = f32[192,768]{1,0:T(8,128)S(1)} collective-permute-done((f32[192,768]{1,0:T(8,128)S(1)}, f32[192,768]{1,0:T(8,128)S(1)}, u32[]{:S(2)}, u32[]{:S(2)}) %collective-permute-start.29) | collective-permute-done | bytes 589856 | tf_op jit(solution)/shard_map/ppermute | solution.py:851
  254.9 1.1 collective-permute-done.31.refs_2_
  256.8 7.2 %collective-permute-done.33.refs_2_ = f32[96,768]{1,0:T(8,128)S(1)} collective-permute-done((f32[96,768]{1,0:T(8,128)S(1)}, f32[96,768]{1,0:T(8,128)S(1)}, u32[]{:S(2)}, u32[]{:S(2)}) %collective-permute-start.33) | collective-permute-done | bytes 294944 | tf_op jit(solution)/shard_map/ppermute | solution.py:851
  264.6 2.6 collective-permute-start.38
  268.0 5.6 %frames_kept.1 = (f32[8,128]{1,0:T(8,128)}, f32[1500,1,384]{2,1,0:T(1,128)}) custom-call(f32[8,128]{1,0:T(8,128)} %get-tuple-element.375.refs_0_, s32[1]{0:T(128)} %bitcast.5.refs_19_.refs_1_, bf16[1536,384]{1,0:T(8,128)(2,1)} %get-tuple-element.285.refs_11_.refs_2_, bf16[1536,384]{1,0:T(8,128)(2,1)} %get-tuple-element.286.refs_13_.refs_3_, ...), custom_call_target="tpu_custom_call" | custom-call | flops 89999998976 | bytes 576000000 | tf_op jit(solution)/shard_map/frames_kept/pallas_call | solution.py:171
  (96 shorter events, 16.9 us)
Async XLA Ops:
  8.4 21.4 %collective-permute-start = (f32[256,768]{1,0:T(8,128)S(1)}, f32[256,768]{1,0:T(8,128)S(1)}, u32[]{:S(2)}, u32[]{:S(2)}) collective-permute-start(f32[256,768]{1,0:T(8,128)S(1)} %get-tuple-element.215.refs_1_), channel_id=1, source_target_pairs={{0,1},{1,0},{2,3},{3,2},{4,5},{5,4},{6,7},{7,6},{8,9},{9,8},{10,11... | collective-permute-start | bytes 2359304 | tf_op jit(solution)/shard_map/ppermute | solution.py:847
  11.4 4.3 %copy-start.8 = (bf16[768,2,384]{2,1,0:T(2,128)(2,1)S(1)}, bf16[768,2,384]{2,1,0:T(2,128)(2,1)}, u32[]{:S(2)}) copy-start(bf16[768,2,384]{2,1,0:T(2,128)(2,1)} %param.25) | copy-start | bytes 3538948
  15.6 26.8 %collective-permute-start.1 = (f32[192,768]{1,0:T(8,128)S(1)}, f32[192,768]{1,0:T(8,128)S(1)}, u32[]{:S(2)}, u32[]{:S(2)}) collective-permute-start(f32[192,768]{1,0:T(8,128)S(1)} %get-tuple-element.219.refs_1_), channel_id=1, source_target_pairs={{0,1},{1,0},{2,3},{3,2},{4,5},{5,4},{6,7},{7,6},{8,9},{9,8},{10,11... | collective-permute-start | bytes 1769480 | tf_op jit(solution)/shard_map/ppermute | solution.py:847
  17.8 8.9 %copy-start.10 = (f32[1536]{0:T(1024)S(1)}, f32[1536]{0:T(1024)}, u32[]{:S(2)}) copy-start(f32[1536]{0:T(1024)} %param.29) | copy-start | bytes 18436
  37.4 21.9 %collective-permute-start.2 = (f32[256,768]{1,0:T(8,128)S(1)}, f32[256,768]{1,0:T(8,128)S(1)}, u32[]{:S(2)}, u32[]{:S(2)}) collective-permute-start(f32[256,768]{1,0:T(8,128)S(1)} %get-tuple-element.227.refs_1_), channel_id=1, source_target_pairs={{0,1},{1,0},{2,3},{3,2},{4,5},{5,4},{6,7},{7,6},{8,9},{9,8},{10,11... | collective-permute-start | bytes 2359304 | tf_op jit(solution)/shard_map/ppermute | solution.py:847
  49.3 22.6 %collective-permute-start.3 = (f32[192,768]{1,0:T(8,128)S(1)}, f32[192,768]{1,0:T(8,128)S(1)}, u32[]{:S(2)}, u32[]{:S(2)}) collective-permute-start(f32[192,768]{1,0:T(8,128)S(1)} %get-tuple-element.230.refs_1_), channel_id=1, source_target_pairs={{0,1},{1,0},{2,3},{3,2},{4,5},{5,4},{6,7},{7,6},{8,9},{9,8},{10,11... | collective-permute-start | bytes 1769480 | tf_op jit(solution)/shard_map/ppermute | solution.py:847
  66.7 22.1 %collective-permute-start.4 = (f32[256,768]{1,0:T(8,128)S(1)}, f32[256,768]{1,0:T(8,128)S(1)}, u32[]{:S(2)}, u32[]{:S(2)}) collective-permute-start(f32[256,768]{1,0:T(8,128)S(1)} %get-tuple-element.237.refs_1_), channel_id=1, source_target_pairs={{0,1},{1,0},{2,3},{3,2},{4,5},{5,4},{6,7},{7,6},{8,9},{9,8},{10,11... | collective-permute-start | bytes 2359304 | tf_op jit(solution)/shard_map/ppermute | solution.py:847
  78.6 22.8 %collective-permute-start.5 = (f32[192,768]{1,0:T(8,128)S(1)}, f32[192,768]{1,0:T(8,128)S(1)}, u32[]{:S(2)}, u32[]{:S(2)}) collective-permute-start(f32[192,768]{1,0:T(8,128)S(1)} %get-tuple-element.241.refs_1_), channel_id=1, source_target_pairs={{0,1},{1,0},{2,3},{3,2},{4,5},{5,4},{6,7},{7,6},{8,9},{9,8},{10,11... | collective-permute-start | bytes 1769480 | tf_op jit(solution)/shard_map/ppermute | solution.py:847
  96.0 13.1 %copy-start = (f32[256,768]{1,0:T(8,128)}, f32[256,768]{1,0:T(8,128)S(1)}, u32[]{:S(2)}) copy-start(f32[256,768]{1,0:T(8,128)S(1)} %get-tuple-element.254.refs_1_) | copy-start | bytes 2359300
  96.0 13.1 %copy-start.2 = (f32[8,1536]{1,0:T(8,128)}, f32[8,1536]{1,0:T(8,128)S(1)}, u32[]{:S(2)}) copy-start(f32[8,1536]{1,0:T(8,128)S(1)} %get-tuple-element.343.refs_12_) | copy-start | bytes 147460
  96.0 13.1 %copy-start.4 = (f32[8,768]{1,0:T(8,128)}, f32[8,768]{1,0:T(8,128)S(1)}, u32[]{:S(2)}) copy-start(f32[8,768]{1,0:T(8,128)S(1)} %get-tuple-element.341.refs_10_) | copy-start | bytes 73732
  96.1 22.6 %collective-permute-start.6 = (f32[256,768]{1,0:T(8,128)S(1)}, f32[256,768]{1,0:T(8,128)S(1)}, u32[]{:S(2)}, u32[]{:S(2)}) collective-permute-start(f32[256,768]{1,0:T(8,128)S(1)} %get-tuple-element.254.refs_1_), channel_id=1, source_target_pairs={{0,1},{1,0},{2,3},{3,2},{4,5},{5,4},{6,7},{7,6},{8,9},{9,8},{10,11... | collective-permute-start | bytes 2359304 | tf_op jit(solution)/shard_map/ppermute | solution.py:847
  109.1 0.6 copy-start.3
  109.7 0.6 copy-start.5
  110.4 7.4 %copy-start.9 = (bf16[768,384]{1,0:T(8,128)(2,1)S(1)}, bf16[768,384]{1,0:T(8,128)(2,1)}, u32[]{:S(2)}) copy-start(bf16[768,384]{1,0:T(8,128)(2,1)} %refs_4_.16) | copy-start | bytes 1769476
  115.5 8.0 %collective-permute-start.7 = (f32[384,3072]{1,0:T(8,128)S(1)}, f32[384,3072]{1,0:T(8,128)S(1)}, u32[]{:S(2)}, u32[]{:S(2)}) collective-permute-start(f32[384,3072]{1,0:T(8,128)S(1)} %get-tuple-element.255), channel_id=1, source_target_pairs={{0,2},{2,0},{4,6},{6,4},{8,10},{10,8},{12,14},{14,12},{16,18},{18,... | collective-permute-start | bytes 14155784 | tf_op jit(solution)/shard_map/ppermute | solution.py:851
  115.6 16.6 %collective-permute-start.8 = (f32[192,768]{1,0:T(8,128)}, f32[192,768]{1,0:T(8,128)}, u32[]{:S(2)}, u32[]{:S(2)}) collective-permute-start(f32[192,768]{1,0:T(8,128)} %get-tuple-element.264.refs_8_), channel_id=1, source_target_pairs={{0,1},{1,0},{2,3},{3,2},{4,5},{5,4},{6,7},{7,6},{8,9},{9,8},{10,11... | collective-permute-start | bytes 1769480 | tf_op jit(solution)/shard_map/ppermute | solution.py:847
  118.6 38.3 %collective-permute-start.9 = (f32[384,384]{1,0:T(8,128)}, f32[384,384]{1,0:T(8,128)}, u32[]{:S(2)}, u32[]{:S(2)}) collective-permute-start(f32[384,384]{1,0:T(8,128)} %dynamic-slice_convert_fusion), channel_id=1, source_target_pairs={{0,1},{1,0},{2,3},{3,2},{4,5},{5,4},{6,7},{7,6},{8,9},{9,8},{10,11... | collective-permute-start | bytes 1769480 | tf_op jit(solution)/shard_map/ppermute | solution.py:847
  118.6 0.9 copy-start.11
  127.7 29.2 %collective-permute-start.10 = (f32[192,1536]{1,0:T(8,128)}, f32[192,1536]{1,0:T(8,128)}, u32[]{:S(2)}, u32[]{:S(2)}) collective-permute-start(f32[192,1536]{1,0:T(8,128)} %get-tuple-element.272), channel_id=1, source_target_pairs={{0,4},{2,6},{4,0},{6,2},{8,12},{10,14},{12,8},{14,10},{16,20},{18,... | collective-permute-start | bytes 3538952 | tf_op jit(solution)/shard_map/ppermute | solution.py:851
  129.9 28.0 %collective-permute-start.11 = (f32[192,1536]{1,0:T(8,128)}, f32[192,1536]{1,0:T(8,128)}, u32[]{:S(2)}, u32[]{:S(2)}) collective-permute-start(f32[192,1536]{1,0:T(8,128)} %get-tuple-element.274), channel_id=1, source_target_pairs={{0,8},{2,10},{4,12},{6,14},{8,0},{10,2},{12,4},{14,6},{16,24},{18,... | collective-permute-start | bytes 3538952 | tf_op jit(solution)/shard_map/ppermute | solution.py:851
  154.9 5.9 %copy-start.1 = (f32[448,384]{1,0:T(8,128)}, f32[448,384]{1,0:T(8,128)S(1)}, u32[]{:S(2)}) copy-start(f32[448,384]{1,0:T(8,128)S(1)} %get-tuple-element.288.refs_2_) | copy-start | bytes 2064388
  154.9 5.9 %copy-start.6 = (f32[8,768]{1,0:T(8,128)}, f32[8,768]{1,0:T(8,128)S(1)}, u32[]{:S(2)}) copy-start(f32[8,768]{1,0:T(8,128)S(1)} %get-tuple-element.340.refs_9_) | copy-start | bytes 73732
  154.9 18.4 %collective-permute-start.12 = (f32[448,384]{1,0:T(8,128)S(1)}, f32[448,384]{1,0:T(8,128)S(1)}, u32[]{:S(2)}, u32[]{:S(2)}) collective-permute-start(f32[448,384]{1,0:T(8,128)S(1)} %get-tuple-element.288.refs_2_), channel_id=1, source_target_pairs={{0,1},{1,0},{2,3},{3,2},{4,5},{5,4},{6,7},{7,6},{8,9},{9,8},{10,11... | collective-permute-start | bytes 2064392 | tf_op jit(solution)/shard_map/ppermute | solution.py:847
  156.9 26.6 %collective-permute-start.14 = (f32[384,384]{1,0:T(8,128)}, f32[384,384]{1,0:T(8,128)}, u32[]{:S(2)}, u32[]{:S(2)}) collective-permute-start(f32[384,384]{1,0:T(8,128)} %collective-permute-done.9.refs_1_.refs_5_), channel_id=1, source_target_pairs={{0,2},{2,0},{4,6},{6,4},{8,10},{10,8},{12,14},{14,12},{16,18},{18,... | collective-permute-start | bytes 1769480 | tf_op jit(solution)/shard_map/ppermute | solution.py:851
  166.6 9.8 %collective-permute-start.13 = (f32[384,1536]{1,0:T(8,128)S(1)}, f32[384,1536]{1,0:T(8,128)S(1)}, u32[]{:S(2)}, u32[]{:S(2)}) collective-permute-start(f32[384,1536]{1,0:T(8,128)S(1)} %get-tuple-element.289), channel_id=1, source_target_pairs={{0,2},{2,0},{4,6},{6,4},{8,10},{10,8},{12,14},{14,12},{16,18},{18,... | collective-permute-start | bytes 7077896 | tf_op jit(solution)/shard_map/ppermute | solution.py:851
  166.7 33.5 %collective-permute-start.15 = (f32[376,384]{1,0:T(8,128)}, f32[376,384]{1,0:T(8,128)}, u32[]{:S(2)}, u32[]{:S(2)}) collective-permute-start(f32[376,384]{1,0:T(8,128)} %get-tuple-element.302), channel_id=1, source_target_pairs={{0,1},{1,0},{2,3},{3,2},{4,5},{5,4},{6,7},{7,6},{8,9},{9,8},{10,11... | collective-permute-start | bytes 1732616 | tf_op jit(solution)/shard_map/ppermute | solution.py:847
  168.2 32.5 %collective-permute-start.16 = (f32[96,1536]{1,0:T(8,128)}, f32[96,1536]{1,0:T(8,128)}, u32[]{:S(2)}, u32[]{:S(2)}) collective-permute-start(f32[96,1536]{1,0:T(8,128)} %get-tuple-element.304), channel_id=1, source_target_pairs={{0,8},{2,10},{4,12},{6,14},{8,0},{10,2},{12,4},{14,6},{16,24},{18,... | collective-permute-start | bytes 1769480 | tf_op jit(solution)/shard_map/ppermute | solution.py:851
  173.3 3.0 %copy-start.12 = (f32[448,384]{1,0:T(8,128)}, f32[448,384]{1,0:T(8,128)S(1)}, u32[]{:S(2)}) copy-start(f32[448,384]{1,0:T(8,128)S(1)} %collective-permute-done.12.refs_1_.refs_3_) | copy-start | bytes 2064388
  173.3 27.4 %collective-permute-start.17 = (f32[96,1536]{1,0:T(8,128)}, f32[96,1536]{1,0:T(8,128)}, u32[]{:S(2)}, u32[]{:S(2)}) collective-permute-start(f32[96,1536]{1,0:T(8,128)} %get-tuple-element.306), channel_id=1, source_target_pairs={{0,16},{2,18},{4,20},{6,22},{8,24},{10,26},{12,28},{14,30},{16,0},... | collective-permute-start | bytes 1769480 | tf_op jit(solution)/shard_map/ppermute | solution.py:851
  182.0 27.0 %collective-permute-start.18 = (f32[376,384]{1,0:T(8,128)}, f32[376,384]{1,0:T(8,128)}, u32[]{:S(2)}, u32[]{:S(2)}) collective-permute-start(f32[376,384]{1,0:T(8,128)} %get-tuple-element.318), channel_id=1, source_target_pairs={{0,1},{1,0},{2,3},{3,2},{4,5},{5,4},{6,7},{7,6},{8,9},{9,8},{10,11... | collective-permute-start | bytes 1732616 | tf_op jit(solution)/shard_map/ppermute | solution.py:847
  183.5 27.3 %collective-permute-start.19 = (f32[192,1536]{1,0:T(8,128)}, f32[192,1536]{1,0:T(8,128)}, u32[]{:S(2)}, u32[]{:S(2)}) collective-permute-start(f32[192,1536]{1,0:T(8,128)} %get-tuple-element.320), channel_id=1, source_target_pairs={{0,4},{2,6},{4,0},{6,2},{8,12},{10,14},{12,8},{14,10},{16,20},{18,... | collective-permute-start | bytes 3538952 | tf_op jit(solution)/shard_map/ppermute | solution.py:851
  199.6 0.6 copy-start.7
  200.2 18.0 %collective-permute-start.20 = (f32[256,768]{1,0:T(8,128)S(1)}, f32[256,768]{1,0:T(8,128)S(1)}, u32[]{:S(2)}, u32[]{:S(2)}) collective-permute-start(f32[256,768]{1,0:T(8,128)S(1)} %get-tuple-element.323.refs_4_), channel_id=1, source_target_pairs={{0,1},{1,0},{2,3},{3,2},{4,5},{5,4},{6,7},{7,6},{8,9},{9,8},{10,11... | collective-permute-start | bytes 2359304 | tf_op jit(solution)/shard_map/ppermute | solution.py:847
  202.9 18.5 %collective-permute-start.21 = (f32[48,1536]{1,0:T(8,128)}, f32[48,1536]{1,0:T(8,128)}, u32[]{:S(2)}, u32[]{:S(2)}) collective-permute-start(f32[48,1536]{1,0:T(8,128)} %get-tuple-element.326), channel_id=1, source_target_pairs={{0,16},{2,18},{4,20},{6,22},{8,24},{10,26},{12,28},{14,30},{16,0},... | collective-permute-start | bytes 884744 | tf_op jit(solution)/shard_map/ppermute | solution.py:851
  203.8 17.6 %collective-permute-start.22 = (f32[48,1536]{1,0:T(8,128)}, f32[48,1536]{1,0:T(8,128)}, u32[]{:S(2)}, u32[]{:S(2)}) collective-permute-start(f32[48,1536]{1,0:T(8,128)} %get-tuple-element.328), channel_id=1, source_target_pairs={{0,4},{2,6},{4,0},{6,2},{8,12},{10,14},{12,8},{14,10},{16,20},{18,... | collective-permute-start | bytes 884744 | tf_op jit(solution)/shard_map/ppermute | solution.py:851
  209.0 14.3 %collective-permute-start.23 = (f32[384,1536]{1,0:T(8,128)S(1)}, f32[384,1536]{1,0:T(8,128)S(1)}, u32[]{:S(2)}, u32[]{:S(2)}) collective-permute-start(f32[384,1536]{1,0:T(8,128)S(1)} %get-tuple-element.330), channel_id=1, source_target_pairs={{0,2},{2,0},{4,6},{6,4},{8,10},{10,8},{12,14},{14,12},{16,18},{18,... | collective-permute-start | bytes 7077896 | tf_op jit(solution)/shard_map/ppermute | solution.py:851
  210.8 17.2 %collective-permute-start.24 = (f32[192,768]{1,0:T(8,128)}, f32[192,768]{1,0:T(8,128)}, u32[]{:S(2)}, u32[]{:S(2)}) collective-permute-start(f32[192,768]{1,0:T(8,128)} %get-tuple-element.336.refs_4_), channel_id=1, source_target_pairs={{0,1},{1,0},{2,3},{3,2},{4,5},{5,4},{6,7},{7,6},{8,9},{9,8},{10,11... | collective-permute-start | bytes 1769480 | tf_op jit(solution)/shard_map/ppermute | solution.py:847
  218.2 16.3 %collective-permute-start.25 = (f32[96,1536]{1,0:T(8,128)}, f32[96,1536]{1,0:T(8,128)}, u32[]{:S(2)}, u32[]{:S(2)}) collective-permute-start(f32[96,1536]{1,0:T(8,128)} %get-tuple-element.351), channel_id=1, source_target_pairs={{0,8},{2,10},{4,12},{6,14},{8,0},{10,2},{12,4},{14,6},{16,24},{18,... | collective-permute-start | bytes 1769480 | tf_op jit(solution)/shard_map/ppermute | solution.py:851
  226.5 15.6 %collective-permute-start.26 = (f32[192,768]{1,0:T(8,128)S(1)}, f32[192,768]{1,0:T(8,128)S(1)}, u32[]{:S(2)}, u32[]{:S(2)}) collective-permute-start(f32[192,768]{1,0:T(8,128)S(1)} %get-tuple-element.354), channel_id=1, source_target_pairs={{0,4},{2,6},{4,0},{6,2},{8,12},{10,14},{12,8},{14,10},{16,20},{18,... | collective-permute-start | bytes 1769480 | tf_op jit(solution)/shard_map/ppermute | solution.py:851
  228.0 5.1 %copy-start.14 = (f32[376,384]{1,0:T(8,128)S(1)}, f32[376,384]{1,0:T(8,128)}, u32[]{:S(2)}) copy-start(f32[376,384]{1,0:T(8,128)} %get-tuple-element.359) | copy-start | bytes 1732612
  233.1 9.3 %collective-permute-start.27 = (f32[15,768]{1,0:T(8,128)S(1)}, f32[15,768]{1,0:T(8,128)S(1)}, u32[]{:S(2)}, u32[]{:S(2)}) collective-permute-start(f32[15,768]{1,0:T(8,128)S(1)} %get-tuple-element.356.refs_1_), channel_id=1, source_target_pairs={{0,2},{2,0},{4,6},{6,4},{8,10},{10,8},{12,14},{14,12},{16,18},{18,... | collective-permute-start | bytes 138248 | tf_op jit(solution)/shard_map/ppermute | solution.py:851
  233.2 15.5 %collective-permute-start.28 = (f32[376,384]{1,0:T(8,128)S(1)}, f32[376,384]{1,0:T(8,128)S(1)}, u32[]{:S(2)}, u32[]{:S(2)}) collective-permute-start(f32[376,384]{1,0:T(8,128)S(1)} %copy-done.14), channel_id=1, source_target_pairs={{0,1},{1,0},{2,3},{3,2},{4,5},{5,4},{6,7},{7,6},{8,9},{9,8},{10,11... | collective-permute-start | bytes 1732616 | tf_op jit(solution)/shard_map/ppermute | solution.py:847
  233.8 18.8 %collective-permute-start.29 = (f32[192,768]{1,0:T(8,128)S(1)}, f32[192,768]{1,0:T(8,128)S(1)}, u32[]{:S(2)}, u32[]{:S(2)}) collective-permute-start(f32[192,768]{1,0:T(8,128)S(1)} %get-tuple-element.361), channel_id=1, source_target_pairs={{0,4},{2,6},{4,0},{6,2},{8,12},{10,14},{12,8},{14,10},{16,20},{18,... | collective-permute-start | bytes 1769480 | tf_op jit(solution)/shard_map/ppermute | solution.py:851
  235.6 18.5 %collective-permute-start.30 = (f32[48,1536]{1,0:T(8,128)S(1)}, f32[48,1536]{1,0:T(8,128)S(1)}, u32[]{:S(2)}, u32[]{:S(2)}) collective-permute-start(f32[48,1536]{1,0:T(8,128)S(1)} %get-tuple-element.364), channel_id=1, source_target_pairs={{0,16},{2,18},{4,20},{6,22},{8,24},{10,26},{12,28},{14,30},{16,0},... | collective-permute-start | bytes 884744 | tf_op jit(solution)/shard_map/ppermute | solution.py:851
  242.2 13.7 %collective-permute-start.31 = (f32[96,768]{1,0:T(8,128)S(1)}, f32[96,768]{1,0:T(8,128)S(1)}, u32[]{:S(2)}, u32[]{:S(2)}) collective-permute-start(f32[96,768]{1,0:T(8,128)S(1)} %get-tuple-element.367), channel_id=1, source_target_pairs={{0,8},{2,10},{4,12},{6,14},{8,0},{10,2},{12,4},{14,6},{16,24},{18,... | collective-permute-start | bytes 884744 | tf_op jit(solution)/shard_map/ppermute | solution.py:851
  242.4 13.7 %collective-permute-start.32 = (f32[15,768]{1,0:T(8,128)S(1)}, f32[15,768]{1,0:T(8,128)S(1)}, u32[]{:S(2)}, u32[]{:S(2)}) collective-permute-start(f32[15,768]{1,0:T(8,128)S(1)} %get-tuple-element.369.refs_1_), channel_id=1, source_target_pairs={{0,4},{2,6},{4,0},{6,2},{8,12},{10,14},{12,8},{14,10},{16,20},{18,... | collective-permute-start | bytes 138248 | tf_op jit(solution)/shard_map/ppermute | solution.py:851
  248.6 3.9 %copy-start.15 = (f32[376,384]{1,0:T(8,128)}, f32[376,384]{1,0:T(8,128)S(1)}, u32[]{:S(2)}) copy-start(f32[376,384]{1,0:T(8,128)S(1)} %collective-permute-done.28.refs_1_.refs_7_) | copy-start | bytes 1732612
  252.5 1.1 copy-start.13
  252.6 11.4 %collective-permute-start.33 = (f32[96,768]{1,0:T(8,128)S(1)}, f32[96,768]{1,0:T(8,128)S(1)}, u32[]{:S(2)}, u32[]{:S(2)}) collective-permute-start(f32[96,768]{1,0:T(8,128)S(1)} %get-tuple-element.372), channel_id=1, source_target_pairs={{0,8},{2,10},{4,12},{6,14},{8,0},{10,2},{12,4},{14,6},{16,24},{18,... | collective-permute-start | bytes 884744 | tf_op jit(solution)/shard_map/ppermute | solution.py:851
  253.6 13.6 %collective-permute-start.35 = (f32[376,384]{1,0:T(8,128)S(1)}, f32[376,384]{1,0:T(8,128)S(1)}, u32[]{:S(2)}, u32[]{:S(2)}) collective-permute-start(f32[376,384]{1,0:T(8,128)S(1)} %copy-done.13), channel_id=1, source_target_pairs={{0,1},{1,0},{2,3},{3,2},{4,5},{5,4},{6,7},{7,6},{8,9},{9,8},{10,11... | collective-permute-start | bytes 1732616 | tf_op jit(solution)/shard_map/ppermute | solution.py:847
  256.0 8.5 %collective-permute-start.34 = (f32[15,768]{1,0:T(8,128)S(1)}, f32[15,768]{1,0:T(8,128)S(1)}, u32[]{:S(2)}, u32[]{:S(2)}) collective-permute-start(f32[15,768]{1,0:T(8,128)S(1)} %get-tuple-element.374.refs_1_), channel_id=1, source_target_pairs={{0,8},{2,10},{4,12},{6,14},{8,0},{10,2},{12,4},{14,6},{16,24},{18,... | collective-permute-start | bytes 138248 | tf_op jit(solution)/shard_map/ppermute | solution.py:851
  256.2 17.5 %collective-permute-start.36 = (f32[48,768]{1,0:T(8,128)S(1)}, f32[48,768]{1,0:T(8,128)S(1)}, u32[]{:S(2)}, u32[]{:S(2)}) collective-permute-start(f32[48,768]{1,0:T(8,128)S(1)} %get-tuple-element.381), channel_id=1, source_target_pairs={{0,16},{2,18},{4,20},{6,22},{8,24},{10,26},{12,28},{14,30},{16,0},... | collective-permute-start | bytes 442376 | tf_op jit(solution)/shard_map/ppermute | solution.py:851
  264.1 10.2 %collective-permute-start.37 = (f32[48,768]{1,0:T(8,128)S(1)}, f32[48,768]{1,0:T(8,128)S(1)}, u32[]{:S(2)}, u32[]{:S(2)}) collective-permute-start(f32[48,768]{1,0:T(8,128)S(1)} %get-tuple-element.385), channel_id=1, source_target_pairs={{0,16},{2,18},{4,20},{6,22},{8,24},{10,26},{12,28},{14,30},{16,0},... | collective-permute-start | bytes 442376 | tf_op jit(solution)/shard_map/ppermute | solution.py:851
  264.6 9.8 %collective-permute-start.38 = (f32[15,768]{1,0:T(8,128)S(1)}, f32[15,768]{1,0:T(8,128)S(1)}, u32[]{:S(2)}, u32[]{:S(2)}) collective-permute-start(f32[15,768]{1,0:T(8,128)S(1)} %get-tuple-element.389.refs_1_), channel_id=1, source_target_pairs={{0,16},{2,18},{4,20},{6,22},{8,24},{10,26},{12,28},{14,30},{16,0},... | collective-permute-start | bytes 138248 | tf_op jit(solution)/shard_map/ppermute | solution.py:851
  267.2 0.8 copy-start.16
where the time goes:
time: 277 us; the launch traced here: 276 us
  Pallas kernels  166 us (60%)
  waiting for transfers between devices  56.4 us (20%)
  starting transfers between devices  43.1 us (16%)
  local copies, waits for them, and re-layouts  7.52 us (3%)
    pallas_call x40, Pallas kernels, __call__(): pl.pallas_call(body, out_shape=tuple((pltpu.HBM(o.shape, o.dtype) if k in...  166 us
    ppermute x16, waiting for transfers between devices, swap_mp(): return lax.ppermute(v, 'mp', [(0, 1), (1, 0)])  33.3 us
    ppermute x16, starting transfers between devices, swap_mp(): return lax.ppermute(v, 'mp', [(0, 1), (1, 0)])  23.2 us
    ppermute x23, waiting for transfers between devices, swap_dp(): return lax.ppermute(v, 'dp', [(i, i ^ bit) for i in range(dp_size)])  23.2 us
    ppermute x23, starting transfers between devices, swap_dp(): return lax.ppermute(v, 'dp', [(i, i ^ bit) for i in range(dp_size)])  19.9 us
  transfers between devices with their start and end apart: 39, of which 19 were waited for; matrix products, arithmetic and copies ran while one was open for 1% of the time, Pallas kernels for 57%

commit v1 on v0

--- a/solution.py
+++ b/solution.py
@@ -970,7 +970,7 @@
     def fetched(weight, parts):
         block = weight.shape[0] // parts
         at = (spot & (parts - 1)) * block
-        return swap_mp(lax.dynamic_slice_in_dim(weight, at, block, 0).astype(F32))
+        return lax.dynamic_slice_in_dim(weight, at, block, 0).astype(F32)
 
     made = chain(
         partial(self_start, cut),
@@ -1073,7 +1073,7 @@
         "dense",
     )
     other4_l = chain.swap_mp(chain.tie(part4_l))
-    wq_0 = chain.later(lambda tied=chain.tie(cross_query_weight): fetched(tied, 2))
+    wq_0 = chain.swap_mp(chain.tie(fetched(cross_query_weight, 2)))
     chain.pause(other4_h)
     denses.keep()
     all_rows = slice(0, slot)
@@ -1175,7 +1175,7 @@
         "tokens_end",
         scratch=[pltpu.VMEM((8, model), F32)],
     )
-    small_bits = list(bits)
+    small_bits = bits[:1] + bits[2:] + bits[1:2]
 
     def small_step(total, other):
         (total,) = chain(plain_end, [(shaped(total.shape), "v")], [(total, "v"), (other, "v")], 0, "small_step")

time: 277 us -> 275 us (level)
  waiting for transfers between devices: 56.4 us -> 53.4 us
  transfers between devices with their start and end apart: 39 -> 39, of which waited for: 19 -> 21; matrix products, arithmetic and copies ran while one was open for 1% -> 1% of each run, Pallas kernels for 57% -> 57%
where the time goes in v1:
time: 275 us
  Pallas kernels  166 us (60%)
  waiting for transfers between devices  53.4 us (19%)
  starting transfers between devices  44.7 us (16%)
  local copies, waits for them, and re-layouts  7.53 us (3%)
    pallas_call x40, Pallas kernels, __call__(): pl.pallas_call(body, out_shape=tuple((pltpu.HBM(o.shape, o.dtype) if k in...  166 us
    ppermute x16, waiting for transfers between devices, swap_mp(): return lax.ppermute(v, 'mp', [(0, 1), (1, 0)])  31.2 us
    ppermute x16, starting transfers between devices, swap_mp(): return lax.ppermute(v, 'mp', [(0, 1), (1, 0)])  23.3 us
    ppermute x23, waiting for transfers between devices, swap_dp(): return lax.ppermute(v, 'dp', [(i, i ^ bit) for i in range(dp_size)])  22.2 us
    ppermute x23, starting transfers between devices, swap_dp(): return lax.ppermute(v, 'dp', [(i, i ^ bit) for i in range(dp_size)])  21.5 us
  transfers between devices with their start and end apart: 39, of which 21 were waited for; matrix products, arithmetic and copies ran while one was open for 1% of the time, Pallas kernels for 57%

profile of v1, /device:TPU:0, one launch (start us, length us, event | category | flops | bytes accessed | tf_op | source)
XLA Modules:
  0.0 274.8 jit_solution(6164386631042149302)
XLA Ops:
  1.3 7.1 %self_start.1 = (f32[8,128]{1,0:T(8,128)}, bf16[192,768]{1,0:T(8,128)(2,1)}, bf16[256,768]{1,0:T(8,128)(2,1)}, bf16[448,384]{1,0:T(8,128)(2,1)}, bf16[448,384]{1...) custom-call(f32[4,768]{1,0:T(4,128)} %refs_2_.5, ...), custom_call_target="tpu_custom_call" | custom-call | flops 30000001024 | bytes 192000000 | tf_op jit(solution)/shard_map/self_start/pallas_call | solution.py:171
  8.4 3.0 %collective-permute-start = (f32[256,768]{1,0:T(8,128)S(1)}, f32[256,768]{1,0:T(8,128)S(1)}, u32[]{:S(2)}, u32[]{:S(2)}) collective-permute-start(f32[256,768]{1,0:T(8,128)S(1)} %get-tuple-element.215.refs_1_), channel_id=1, source_target_pairs={{0,1},{1,0},{2,3},{3,2},{4,5},{5,4},{6,7},{7,6},{8,9},{9,8},{10,11... | collective-permute-start | bytes 2359304 | tf_op jit(solution)/shard_map/ppermute | solution.py:847
  11.4 4.2 %self_next.1 = (f32[8,128]{1,0:T(8,128)}, bf16[192,384]{1,0:T(8,128)(2,1)}, f32[192,384]{1,0:T(8,128)}, f32[8,192]{1,0:T(8,128)}, f32[192,768]{1,0:T(8,128)S(1)}) custom-call(f32[8,128]{1,0:T(8,128)} %get-tuple-element.209.refs_0_, bf16[448,384]{1,0:T(8,128)(2,1)} %get-tuple-element.210.refs_1_.refs_9_, ...), custom_call_target="tpu_custom_call" | custom-call | flops 19499999232 | bytes 124800000 | tf_op jit(solution)/shard_map/self_next/pallas_call | solution.py:171
  15.7 1.2 copy.37
  17.8 9.0 %frames_start.1 = (f32[8,128]{1,0:T(8,128)}, bf16[1536,384]{1,0:T(8,128)(2,1)}, bf16[1536,384]{1,0:T(8,128)(2,1)}, bf16[768,1536]{1,0:T(8,128)(2,1)}, bf16[768,7...) custom-call(f32[8,128]{1,0:T(8,128)} %get-tuple-element.213.refs_0_, bf16[1500,768]{1,0:T(8,128)(2,1)} %bitcast.24, ...), custom_call_target="tpu_custom_call" | custom-call | flops 44999999488 | bytes 288000000 | tf_op jit(solution)/shard_map/frames_start/pallas_call | solution.py:171
  28.3 1.5 collective-permute-done.refs_2_
  29.8 7.6 %cross_start.2 = (f32[8,128]{1,0:T(8,128)}, f32[256,768]{1,0:T(8,128)}, bf16[256,768]{1,0:T(8,128)(2,1)}, bf16[256,384]{1,0:T(8,128)(2,1)}, bf16[256,384]{1,0:T(...) custom-call(f32[8,128]{1,0:T(8,128)} %get-tuple-element.214.refs_0_, ...), custom_call_target="tpu_custom_call" | custom-call | flops 40499998720 | bytes 259200000 | tf_op jit(solution)/shard_map/cross_start/pallas_call | solution.py:171
  37.4 2.1 collective-permute-start.2
  39.5 2.9 %collective-permute-done.1.refs_2_ = f32[192,768]{1,0:T(8,128)S(1)} collective-permute-done((f32[192,768]{1,0:T(8,128)S(1)}, f32[192,768]{1,0:T(8,128)S(1)}, u32[]{:S(2)}, u32[]{:S(2)}) %collective-permute-start.1) | collective-permute-done | bytes 589856 | tf_op jit(solution)/shard_map/ppermute | solution.py:847
  42.4 6.9 %cross_start.3 = (f32[8,128]{1,0:T(8,128)}, f32[192,768]{1,0:T(8,128)}, bf16[192,768]{1,0:T(8,128)(2,1)}, bf16[192,384]{1,0:T(8,128)(2,1)}, bf16[192,384]{1,0:T(...) custom-call(f32[8,128]{1,0:T(8,128)} %get-tuple-element.218.refs_0_, ...), custom_call_target="tpu_custom_call" | custom-call | flops 40499998720 | bytes 259200000 | tf_op jit(solution)/shard_map/cross_start/pallas_call | solution.py:171
  49.3 2.1 collective-permute-start.3
  51.4 5.7 %turn.2 = (f32[8,128]{1,0:T(8,128)}, bf16[768,256]{1,0:T(8,128)(2,1)}, bf16[768,192]{1,0:T(8,128)(2,1)}, bf16[768,256]{1,0:T(8,128)(2,1)}, bf16[768,192]{1,0:T(8,128)(2,1)}) custom-call(f32[8,128]{1,0:T(8,128)} %get-tuple-element.220.refs_0_, bf16[768,768]{1,0:T(8,128)(2,1)} %get-tuple-element.221.refs_1_, bf16[256,768]{1,0:T(8,128)(2,1)} %get-tuple-element.222.refs_2_, ...), custom_call_target="tpu_custom_call" | custom-call | flops 15000000512 | bytes 96000000 | tf_op jit(solution)/shard_map/turn/pallas_call | solution.py:171
  57.1 2.1 collective-permute-done.2.refs_2_
  59.3 7.4 %dense_start.2 = (f32[8,128]{1,0:T(8,128)}, f32[256,768]{1,0:T(8,128)}, bf16[256,768]{1,0:T(8,128)(2,1)}, bf16[256,1536]{1,0:T(8,128)(2,1)}, f32[256,1536]{1,0:T(8,128)}, /*index=5*/f32[256,768]{1,0:T(8,128)S(1)}) custom-call(f32[8,128]{1,0:T(8,128)} %get-tuple-element.226.refs_0_, f32[256,768]{1,0:T(8,128)S(1)} %get-tuple-element.227.refs_1_, ...), custom_call_target="tpu_custom_call" | custom-call | flops 35999997952 | bytes 230400000 | tf_op jit(solution)/shard_map/dense_start/pallas_call | solution.py:171
  66.7 2.1 collective-permute-start.4
  68.8 3.1 %collective-permute-done.3.refs_2_ = f32[192,768]{1,0:T(8,128)S(1)} collective-permute-done((f32[192,768]{1,0:T(8,128)S(1)}, f32[192,768]{1,0:T(8,128)S(1)}, u32[]{:S(2)}, u32[]{:S(2)}) %collective-permute-start.3) | collective-permute-done | bytes 589856 | tf_op jit(solution)/shard_map/ppermute | solution.py:847
  71.9 6.6 %dense_start.3 = (f32[8,128]{1,0:T(8,128)}, f32[192,768]{1,0:T(8,128)}, bf16[192,768]{1,0:T(8,128)(2,1)}, bf16[192,1536]{1,0:T(8,128)(2,1)}, f32[192,1536]{1,0:T(8,128)}, /*index=5*/f32[192,768]{1,0:T(8,128)S(1)}) custom-call(f32[8,128]{1,0:T(8,128)} %get-tuple-element.229.refs_0_, f32[192,768]{1,0:T(8,128)S(1)} %get-tuple-element.230.refs_1_, ...), custom_call_target="tpu_custom_call" | custom-call | flops 35999997952 | bytes 230400000 | tf_op jit(solution)/shard_map/dense_start/pallas_call | solution.py:171
  78.5 2.1 collective-permute-start.5
  80.7 4.3 %turn.3 = (f32[8,128]{1,0:T(8,128)}, bf16[768,256]{1,0:T(8,128)(2,1)}, bf16[768,192]{1,0:T(8,128)(2,1)}) custom-call(f32[8,128]{1,0:T(8,128)} %get-tuple-element.232.refs_0_, bf16[768,768]{1,0:T(8,128)(2,1)} %get-tuple-element.221.refs_1_, bf16[768,768]{1,0:T(8,128)(2,1)} %get-tuple-element.233.refs_2_, bf16[256,768]{1,0:T(8,128)(2,1)} %get-tuple-element.234.refs_3_, ...), custom_call_target="tpu_custom_call" | custom-call | flops 15000000512 | bytes 96000000 | tf_op jit(solution)/shard_map/turn/pallas_call | solution.py:171
  85.0 3.8 %collective-permute-done.4.refs_2_ = f32[256,768]{1,0:T(8,128)S(1)} collective-permute-done((f32[256,768]{1,0:T(8,128)S(1)}, f32[256,768]{1,0:T(8,128)S(1)}, u32[]{:S(2)}, u32[]{:S(2)}) %collective-permute-start.4) | collective-permute-done | bytes 786464 | tf_op jit(solution)/shard_map/ppermute | solution.py:847
  88.8 7.3 %dense_back.2 = (f32[8,128]{1,0:T(8,128)}, bf16[256,768]{1,0:T(8,128)(2,1)}, f32[256,768]{1,0:T(8,128)}, bf16[256,768]{1,0:T(8,128)(2,1)}, bf16[256,1536]{1,0:T(...) custom-call(f32[8,128]{1,0:T(8,128)} %get-tuple-element.236.refs_0_, ...), custom_call_target="tpu_custom_call" | custom-call | flops 35999997952 | bytes 230400000 | tf_op jit(solution)/shard_map/dense_back/pallas_call | solution.py:171
  96.1 2.1 collective-permute-start.6
  98.2 3.2 %collective-permute-done.5.refs_2_ = f32[192,768]{1,0:T(8,128)S(1)} collective-permute-done((f32[192,768]{1,0:T(8,128)S(1)}, f32[192,768]{1,0:T(8,128)S(1)}, u32[]{:S(2)}, u32[]{:S(2)}) %collective-permute-start.5) | collective-permute-done | bytes 589856 | tf_op jit(solution)/shard_map/ppermute | solution.py:847
  101.4 7.7 %dense_back.3 = (f32[8,128]{1,0:T(8,128)}, bf16[192,768]{1,0:T(8,128)(2,1)}, f32[192,768]{1,0:T(8,128)}, bf16[192,768]{1,0:T(8,128)(2,1)}, bf16[192,1536]{1,0:T(...) custom-call(f32[8,128]{1,0:T(8,128)} %get-tuple-element.240.refs_0_, ...), custom_call_target="tpu_custom_call" | custom-call | flops 35999997952 | bytes 230400000 | tf_op jit(solution)/shard_map/dense_back/pallas_call | solution.py:171
  110.4 5.1 %dense_sent.1 = (f32[8,128]{1,0:T(8,128)}, f32[384,3072]{1,0:T(8,128)S(1)}, bf16[768,256]{1,0:T(8,128)(2,1)}, bf16[768,192]{1,0:T(8,128)(2,1)}) custom-call(f32[8,128]{1,0:T(8,128)} %get-tuple-element.244.refs_0_, bf16[768,768]{1,0:T(8,128)(2,1)} %get-tuple-element.221.refs_1_, bf16[768,768]{1,0:T(8,128)(2,1)} %get-tuple-element.233.refs_2_, ...), custom_call_target="tpu_custom_call" | custom-call | flops 89999998976 | bytes 576000000 | tf_op jit(solution)/shard_map/dense_sent/pallas_call | solution.py:171
  115.6 2.1 collective-permute-start.8
  118.7 4.7 %collective-permute-done.7.refs_1_ = f32[384,3072]{1,0:T(8,128)S(1)} collective-permute-done((f32[384,3072]{1,0:T(8,128)S(1)}, f32[384,3072]{1,0:T(8,128)S(1)}, u32[]{:S(2)}, u32[]{:S(2)}) %collective-permute-start.7) | collective-permute-done | bytes 4718624 | tf_op jit(solution)/shard_map/ppermute | solution.py:851
  123.5 4.2 %dense_kept.1 = (f32[8,128]{1,0:T(8,128)}, f32[192,1536]{1,0:T(8,128)}, f32[192,1536]{1,0:T(8,128)S(1)}, f32[192,1536]{1,0:T(8,128)}, f32[192,1536]{1,0:T(8,128)S(1)}) custom-call(f32[8,128]{1,0:T(8,128)} %pause.2.refs_0_, f32[384,3072]{1,0:T(8,128)S(1)} %collective-permute-done.7.refs_1_, bf16[768,256]{1,0:T(8,128)(2,1)} %get-tuple-element.256.refs_2_, ...), custom_call_target="tpu_custom_call" | custom-call | flops 89999998976 | bytes 576000000 | tf_op jit(solution)/shard_map/dense_kept/pallas_call | solution.py:171
  127.7 2.1 collective-permute-start.10
  129.8 1.6 collective-permute-start.11
  132.2 22.6 %cross_back.1 = (f32[8,128]{1,0:T(8,128)}, f32[256,768]{1,0:T(8,128)}, bf16[256,768]{1,0:T(8,128)(2,1)}, f32[192,768]{1,0:T(8,128)}, bf16[192,768]{1,0:T(8,128)(...) custom-call(f32[8,128]{1,0:T(8,128)} %get-tuple-element.258.refs_0_,, ...), custom_call_target="tpu_custom_call" | custom-call | flops 299999985664 | bytes 1920000000 | tf_op jit(solution)/shard_map/cross_back/pallas_call | solution.py:171
  154.8 2.0 collective-permute-start.12
  156.9 1.0 collective-permute-done.11.refs_5_
  157.8 2.9 %steps.2 = (f32[8,128]{1,0:T(8,128)}, f32[96,1536]{1,0:T(8,128)}, f32[96,1536]{1,0:T(8,128)S(1)}, f32[96,1536]{1,0:T(8,128)}, f32[96,1536]{1,0:T(8,128)S(1)}) custom-call(f32[8,128]{1,0:T(8,128)} %get-tuple-element.269.refs_0_, f32[384,384]{1,0:T(8,128)} %collective-permute-done.9.refs_1_.refs_5_, f32[192,1536]{1,0:T(8,128)S(1)} %get-tuple-element.271.refs_2_, ...), custom_call_target="tpu_custom_call" | custom-call | flops 15000000512 | bytes 96000000 | tf_op jit(solution)/shard_map/steps/pallas_call | solution.py:171
  160.8 5.8 %cross_sent.1 = (f32[8,128]{1,0:T(8,128)}, f32[384,1536]{1,0:T(8,128)S(1)}, bf16[768,256]{1,0:T(8,128)(2,1)}, bf16[768,192]{1,0:T(8,128)(2,1)}) custom-call(f32[8,128]{1,0:T(8,128)} %get-tuple-element.275.refs_0_, bf16[768,768]{1,0:T(8,128)(2,1)} %get-tuple-element.221.refs_1_, bf16[256,768]{1,0:T(8,128)(2,1)} %get-tuple-element.276.refs_2_, ...), custom_call_target="tpu_custom_call" | custom-call | flops 89999998976 | bytes 576000000 | tf_op jit(solution)/shard_map/cross_sent/pallas_call | solution.py:171
  166.6 1.6 collective-permute-start.15
  168.2 1.6 collective-permute-start.16
  169.7 3.5 %collective-permute-done.12.refs_1_.refs_3_ = f32[448,384]{1,0:T(8,128)S(1)} collective-permute-done((f32[448,384]{1,0:T(8,128)S(1)}, f32[448,384]{1,0:T(8,128)S(1)}, u32[]{:S(2)}, u32[]{:S(2)}) %collective-permute-start.12) | collective-permute-done | bytes 688160 | tf_op jit(solution)/shard_map/ppermute | solution.py:847
  173.3 3.0 %collective-permute-start.17 = (f32[96,1536]{1,0:T(8,128)}, f32[96,1536]{1,0:T(8,128)}, u32[]{:S(2)}, u32[]{:S(2)}) collective-permute-start(f32[96,1536]{1,0:T(8,128)} %get-tuple-element.306), channel_id=1, source_target_pairs={{0,16},{2,18},{4,20},{6,22},{8,24},{10,26},{12,28},{14,30},{16,0},... | collective-permute-start | bytes 1769480 | tf_op jit(solution)/shard_map/ppermute | solution.py:851
  176.3 5.6 %cross_kept.1 = (f32[8,128]{1,0:T(8,128)}, f32[192,1536]{1,0:T(8,128)}, f32[192,1536]{1,0:T(8,128)S(1)}) custom-call(f32[8,128]{1,0:T(8,128)} %pause.3.refs_0_, f32[384,1536]{1,0:T(8,128)S(1)} %collective-permute-done.13.refs_1_, bf16[768,256]{1,0:T(8,128)(2,1)} %get-tuple-element.290.refs_2_, bf16[768,192]{1,0:T(8,128)(2,1)} %get-tuple-element.291.refs_3_, ...), custom_call_target="tpu_custom_call" | custom-call | flops 74999996416 | bytes 480000000 | tf_op jit(solution)/shard_map/cross_kept/pallas_call | solution.py:171
  181.9 1.6 collective-permute-start.18
  183.5 1.5 collective-permute-start.19
  185.0 14.5 %self_back.1 = (f32[8,128]{1,0:T(8,128)}, f32[256,768]{1,0:T(8,128)}, bf16[256,768]{1,0:T(8,128)(2,1)}, f32[192,768]{1,0:T(8,128)}, bf16[192,768]{1,0:T(8,128)(2...) custom-call(f32[8,128]{1,0:T(8,128)} %get-tuple-element.292.refs_0_,, ...), custom_call_target="tpu_custom_call" | custom-call | flops 179999997952 | bytes 1152000000 | tf_op jit(solution)/shard_map/self_back/pallas_call | solution.py:171
  200.7 2.1 steps.3
  204.2 4.7 %self_sent.1 = (f32[8,128]{1,0:T(8,128)}, f32[384,1536]{1,0:T(8,128)S(1)}, bf16[768,256]{1,0:T(8,128)(2,1)}, bf16[768,192]{1,0:T(8,128)(2,1)}) custom-call(f32[8,128]{1,0:T(8,128)} %get-tuple-element.307.refs_0_, bf16[768,768]{1,0:T(8,128)(2,1)} %get-tuple-element.221.refs_1_, bf16[256,768]{1,0:T(8,128)(2,1)} %get-tuple-element.308.refs_2_, ...), custom_call_target="tpu_custom_call" | custom-call | flops 74999996416 | bytes 480000000 | tf_op jit(solution)/shard_map/self_sent/pallas_call | solution.py:171
  209.0 1.7 collective-permute-done.19.refs_3_
  211.3 2.3 cross0_step.2
  213.6 4.5 %collective-permute-done.20.refs_5_ = f32[256,768]{1,0:T(8,128)S(1)} collective-permute-done((f32[256,768]{1,0:T(8,128)S(1)}, f32[256,768]{1,0:T(8,128)S(1)}, u32[]{:S(2)}, u32[]{:S(2)}) %collective-permute-start.20) | collective-permute-done | bytes 786464 | tf_op jit(solution)/shard_map/ppermute | solution.py:847
  218.3 3.0 %tokens_end.2 = (f32[8,128]{1,0:T(8,128)}, f32[256,768]{1,0:T(8,128)}, f32[8,768]{1,0:T(8,128)}) custom-call(f32[8,128]{1,0:T(8,128)} %get-tuple-element.321.refs_0_, bf16[448,768]{1,0:T(8,128)(2,1)} %bitcast.32, f32[4,768]{1,0:T(4,128)} %refs_2_.5, f32[256,768]{1,0:T(8,128)} %get-tuple-element.322.refs_3_, f32[256,768]{1,0:T(8,128)S(1)} %get-tuple-element.323.refs_4_, ...), custom_call_target="tpu_custom_call" | custom-call | flops 74999996416 | bytes 480000000 | tf_op jit(solution)/shard_map/tokens_end/pallas_call | solution.py:171
  221.4 1.9 ends.1
  223.3 3.2 %self_kept.1 = (f32[8,128]{1,0:T(8,128)}, f32[192,768]{1,0:T(8,128)S(1)}, f32[192,768]{1,0:T(8,128)S(1)}, f32[192,768]{1,0:T(8,128)S(1)}, f32[192,768]{1,0:T(8,128)S(1)}) custom-call(f32[8,128]{1,0:T(8,128)} %get-tuple-element.329.refs_0_, f32[384,1536]{1,0:T(8,128)S(1)} %collective-permute-done.23.refs_1_, bf16[768,256]{1,0:T(8,128)(2,1)} %get-tuple-element.331.refs_2_, ...), custom_call_target="tpu_custom_call" | custom-call | flops 60000002048 | bytes 384000000 | tf_op jit(solution)/shard_map/self_kept/pallas_call | solution.py:171
  228.0 5.0 %tokens_end.3 = (f32[8,128]{1,0:T(8,128)}, f32[448,768]{1,0:T(8,128)}, f32[15,768]{1,0:T(8,128)S(1)}, bf16[448,768]{1,0:T(8,128)(2,1)}) custom-call(f32[8,128]{1,0:T(8,128)} %get-tuple-element.333.refs_0_, bf16[448,768]{1,0:T(8,128)(2,1)} %bitcast.33, f32[4,768]{1,0:T(4,128)} %refs_2_.5, f32[192,768]{1,0:T(8,128)} %get-tuple-element.334.refs_3_, ...), custom_call_target="tpu_custom_call" | custom-call | flops 74999996416 | bytes 480000000 | tf_op jit(solution)/shard_map/tokens_end/pallas_call | solution.py:171
  234.4 1.1 cross0_step.3
  235.6 2.7 collective-permute-start.30
  238.2 3.7 %collective-permute-done.26.refs_2_ = f32[192,768]{1,0:T(8,128)S(1)} collective-permute-done((f32[192,768]{1,0:T(8,128)S(1)}, f32[192,768]{1,0:T(8,128)S(1)}, u32[]{:S(2)}, u32[]{:S(2)}) %collective-permute-start.26) | collective-permute-done | bytes 589856 | tf_op jit(solution)/shard_map/ppermute | solution.py:851
  242.1 2.1 collective-permute-start.32
  244.2 4.4 %collective-permute-done.28.refs_1_.refs_7_ = f32[376,384]{1,0:T(8,128)S(1)} collective-permute-done((f32[376,384]{1,0:T(8,128)S(1)}, f32[376,384]{1,0:T(8,128)S(1)}, u32[]{:S(2)}, u32[]{:S(2)}) %collective-permute-start.28) | collective-permute-done | bytes 577568 | tf_op jit(solution)/shard_map/ppermute | solution.py:847
  248.6 3.3 %collective-permute-done.29.refs_3_ = f32[192,768]{1,0:T(8,128)S(1)} collective-permute-done((f32[192,768]{1,0:T(8,128)S(1)}, f32[192,768]{1,0:T(8,128)S(1)}, u32[]{:S(2)}, u32[]{:S(2)}) %collective-permute-start.29) | collective-permute-done | bytes 589856 | tf_op jit(solution)/shard_map/ppermute | solution.py:851
  254.2 1.5 collective-permute-done.31.refs_2_
  255.8 3.0 %collective-permute-done.32.refs_2_ = f32[15,768]{1,0:T(8,128)S(1)} collective-permute-done((f32[15,768]{1,0:T(8,128)S(1)}, f32[15,768]{1,0:T(8,128)S(1)}, u32[]{:S(2)}, u32[]{:S(2)}) %collective-permute-start.32) | collective-permute-done | bytes 46112 | tf_op jit(solution)/shard_map/ppermute | solution.py:851
  258.9 2.9 %collective-permute-start.36 = (f32[48,768]{1,0:T(8,128)S(1)}, f32[48,768]{1,0:T(8,128)S(1)}, u32[]{:S(2)}, u32[]{:S(2)}) collective-permute-start(f32[48,768]{1,0:T(8,128)S(1)} %get-tuple-element.381), channel_id=1, source_target_pairs={{0,16},{2,18},{4,20},{6,22},{8,24},{10,26},{12,28},{14,30},{16,0},... | collective-permute-start | bytes 442376 | tf_op jit(solution)/shard_map/ppermute | solution.py:851
  261.8 1.1 collective-permute-done.33.refs_2_
  263.1 2.1 collective-permute-done.34.refs_2_
  266.5 5.6 %frames_kept.1 = (f32[8,128]{1,0:T(8,128)}, f32[1500,1,384]{2,1,0:T(1,128)}) custom-call(f32[8,128]{1,0:T(8,128)} %get-tuple-element.375.refs_0_, s32[1]{0:T(128)} %bitcast.5.refs_19_.refs_1_, bf16[1536,384]{1,0:T(8,128)(2,1)} %get-tuple-element.285.refs_11_.refs_2_, bf16[1536,384]{1,0:T(8,128)(2,1)} %get-tuple-element.286.refs_13_.refs_3_, ...), custom_call_target="tpu_custom_call" | custom-call | flops 89999998976 | bytes 576000000 | tf_op jit(solution)/shard_map/frames_kept/pallas_call | solution.py:171
  (96 shorter events, 18.8 us)
Async XLA Ops:
  8.4 21.4 %collective-permute-start = (f32[256,768]{1,0:T(8,128)S(1)}, f32[256,768]{1,0:T(8,128)S(1)}, u32[]{:S(2)}, u32[]{:S(2)}) collective-permute-start(f32[256,768]{1,0:T(8,128)S(1)} %get-tuple-element.215.refs_1_), channel_id=1, source_target_pairs={{0,1},{1,0},{2,3},{3,2},{4,5},{5,4},{6,7},{7,6},{8,9},{9,8},{10,11... | collective-permute-start | bytes 2359304 | tf_op jit(solution)/shard_map/ppermute | solution.py:847
  11.4 4.3 %copy-start.8 = (bf16[768,2,384]{2,1,0:T(2,128)(2,1)S(1)}, bf16[768,2,384]{2,1,0:T(2,128)(2,1)}, u32[]{:S(2)}) copy-start(bf16[768,2,384]{2,1,0:T(2,128)(2,1)} %param.25) | copy-start | bytes 3538948
  15.6 26.8 %collective-permute-start.1 = (f32[192,768]{1,0:T(8,128)S(1)}, f32[192,768]{1,0:T(8,128)S(1)}, u32[]{:S(2)}, u32[]{:S(2)}) collective-permute-start(f32[192,768]{1,0:T(8,128)S(1)} %get-tuple-element.219.refs_1_), channel_id=1, source_target_pairs={{0,1},{1,0},{2,3},{3,2},{4,5},{5,4},{6,7},{7,6},{8,9},{9,8},{10,11... | collective-permute-start | bytes 1769480 | tf_op jit(solution)/shard_map/ppermute | solution.py:847
  17.8 9.0 %copy-start.10 = (f32[1536]{0:T(1024)S(1)}, f32[1536]{0:T(1024)}, u32[]{:S(2)}) copy-start(f32[1536]{0:T(1024)} %param.29) | copy-start | bytes 18436
  17.8 9.6 %copy-start.9 = (bf16[768,384]{1,0:T(8,128)(2,1)S(1)}, bf16[768,384]{1,0:T(8,128)(2,1)}, u32[]{:S(2)}) copy-start(bf16[768,384]{1,0:T(8,128)(2,1)} %refs_4_.16) | copy-start | bytes 1769476
  37.4 21.9 %collective-permute-start.2 = (f32[256,768]{1,0:T(8,128)S(1)}, f32[256,768]{1,0:T(8,128)S(1)}, u32[]{:S(2)}, u32[]{:S(2)}) collective-permute-start(f32[256,768]{1,0:T(8,128)S(1)} %get-tuple-element.227.refs_1_), channel_id=1, source_target_pairs={{0,1},{1,0},{2,3},{3,2},{4,5},{5,4},{6,7},{7,6},{8,9},{9,8},{10,11... | collective-permute-start | bytes 2359304 | tf_op jit(solution)/shard_map/ppermute | solution.py:847
  49.3 22.6 %collective-permute-start.3 = (f32[192,768]{1,0:T(8,128)S(1)}, f32[192,768]{1,0:T(8,128)S(1)}, u32[]{:S(2)}, u32[]{:S(2)}) collective-permute-start(f32[192,768]{1,0:T(8,128)S(1)} %get-tuple-element.230.refs_1_), channel_id=1, source_target_pairs={{0,1},{1,0},{2,3},{3,2},{4,5},{5,4},{6,7},{7,6},{8,9},{9,8},{10,11... | collective-permute-start | bytes 1769480 | tf_op jit(solution)/shard_map/ppermute | solution.py:847
  66.7 22.1 %collective-permute-start.4 = (f32[256,768]{1,0:T(8,128)S(1)}, f32[256,768]{1,0:T(8,128)S(1)}, u32[]{:S(2)}, u32[]{:S(2)}) collective-permute-start(f32[256,768]{1,0:T(8,128)S(1)} %get-tuple-element.237.refs_1_), channel_id=1, source_target_pairs={{0,1},{1,0},{2,3},{3,2},{4,5},{5,4},{6,7},{7,6},{8,9},{9,8},{10,11... | collective-permute-start | bytes 2359304 | tf_op jit(solution)/shard_map/ppermute | solution.py:847
  78.5 22.9 %collective-permute-start.5 = (f32[192,768]{1,0:T(8,128)S(1)}, f32[192,768]{1,0:T(8,128)S(1)}, u32[]{:S(2)}, u32[]{:S(2)}) collective-permute-start(f32[192,768]{1,0:T(8,128)S(1)} %get-tuple-element.241.refs_1_), channel_id=1, source_target_pairs={{0,1},{1,0},{2,3},{3,2},{4,5},{5,4},{6,7},{7,6},{8,9},{9,8},{10,11... | collective-permute-start | bytes 1769480 | tf_op jit(solution)/shard_map/ppermute | solution.py:847
  96.0 13.1 %copy-start = (f32[256,768]{1,0:T(8,128)}, f32[256,768]{1,0:T(8,128)S(1)}, u32[]{:S(2)}) copy-start(f32[256,768]{1,0:T(8,128)S(1)} %get-tuple-element.254.refs_1_) | copy-start | bytes 2359300
  96.0 13.1 %copy-start.2 = (f32[8,1536]{1,0:T(8,128)}, f32[8,1536]{1,0:T(8,128)S(1)}, u32[]{:S(2)}) copy-start(f32[8,1536]{1,0:T(8,128)S(1)} %get-tuple-element.343.refs_12_) | copy-start | bytes 147460
  96.0 13.1 %copy-start.4 = (f32[8,768]{1,0:T(8,128)}, f32[8,768]{1,0:T(8,128)S(1)}, u32[]{:S(2)}) copy-start(f32[8,768]{1,0:T(8,128)S(1)} %get-tuple-element.341.refs_10_) | copy-start | bytes 73732
  96.1 21.7 %collective-permute-start.6 = (f32[256,768]{1,0:T(8,128)S(1)}, f32[256,768]{1,0:T(8,128)S(1)}, u32[]{:S(2)}, u32[]{:S(2)}) collective-permute-start(f32[256,768]{1,0:T(8,128)S(1)} %get-tuple-element.254.refs_1_), channel_id=1, source_target_pairs={{0,1},{1,0},{2,3},{3,2},{4,5},{5,4},{6,7},{7,6},{8,9},{9,8},{10,11... | collective-permute-start | bytes 2359304 | tf_op jit(solution)/shard_map/ppermute | solution.py:847
  109.1 0.6 copy-start.3
  109.8 0.6 copy-start.5
  115.5 8.0 %collective-permute-start.7 = (f32[384,3072]{1,0:T(8,128)S(1)}, f32[384,3072]{1,0:T(8,128)S(1)}, u32[]{:S(2)}, u32[]{:S(2)}) collective-permute-start(f32[384,3072]{1,0:T(8,128)S(1)} %get-tuple-element.255), channel_id=1, source_target_pairs={{0,2},{2,0},{4,6},{6,4},{8,10},{10,8},{12,14},{14,12},{16,18},{18,... | collective-permute-start | bytes 14155784 | tf_op jit(solution)/shard_map/ppermute | solution.py:851
  115.6 16.6 %collective-permute-start.8 = (f32[192,768]{1,0:T(8,128)}, f32[192,768]{1,0:T(8,128)}, u32[]{:S(2)}, u32[]{:S(2)}) collective-permute-start(f32[192,768]{1,0:T(8,128)} %get-tuple-element.264.refs_8_), channel_id=1, source_target_pairs={{0,1},{1,0},{2,3},{3,2},{4,5},{5,4},{6,7},{7,6},{8,9},{9,8},{10,11... | collective-permute-start | bytes 1769480 | tf_op jit(solution)/shard_map/ppermute | solution.py:847
  117.7 39.2 %collective-permute-start.9 = (f32[384,384]{1,0:T(8,128)}, f32[384,384]{1,0:T(8,128)}, u32[]{:S(2)}, u32[]{:S(2)}) collective-permute-start(f32[384,384]{1,0:T(8,128)} %dynamic-slice_convert_fusion), channel_id=1, source_target_pairs={{0,1},{1,0},{2,3},{3,2},{4,5},{5,4},{6,7},{7,6},{8,9},{9,8},{10,11... | collective-permute-start | bytes 1769480 | tf_op jit(solution)/shard_map/ppermute | solution.py:847
  117.8 0.9 copy-start.11
  127.7 29.2 %collective-permute-start.10 = (f32[192,1536]{1,0:T(8,128)}, f32[192,1536]{1,0:T(8,128)}, u32[]{:S(2)}, u32[]{:S(2)}) collective-permute-start(f32[192,1536]{1,0:T(8,128)} %get-tuple-element.272), channel_id=1, source_target_pairs={{0,4},{2,6},{4,0},{6,2},{8,12},{10,14},{12,8},{14,10},{16,20},{18,... | collective-permute-start | bytes 3538952 | tf_op jit(solution)/shard_map/ppermute | solution.py:851
  129.8 28.0 %collective-permute-start.11 = (f32[192,1536]{1,0:T(8,128)}, f32[192,1536]{1,0:T(8,128)}, u32[]{:S(2)}, u32[]{:S(2)}) collective-permute-start(f32[192,1536]{1,0:T(8,128)} %get-tuple-element.274), channel_id=1, source_target_pairs={{0,8},{2,10},{4,12},{6,14},{8,0},{10,2},{12,4},{14,6},{16,24},{18,... | collective-permute-start | bytes 3538952 | tf_op jit(solution)/shard_map/ppermute | solution.py:851
  154.8 5.9 %copy-start.1 = (f32[448,384]{1,0:T(8,128)}, f32[448,384]{1,0:T(8,128)S(1)}, u32[]{:S(2)}) copy-start(f32[448,384]{1,0:T(8,128)S(1)} %get-tuple-element.288.refs_2_) | copy-start | bytes 2064388
  154.8 5.9 %copy-start.6 = (f32[8,768]{1,0:T(8,128)}, f32[8,768]{1,0:T(8,128)S(1)}, u32[]{:S(2)}) copy-start(f32[8,768]{1,0:T(8,128)S(1)} %get-tuple-element.340.refs_9_) | copy-start | bytes 73732
  154.8 18.4 %collective-permute-start.12 = (f32[448,384]{1,0:T(8,128)S(1)}, f32[448,384]{1,0:T(8,128)S(1)}, u32[]{:S(2)}, u32[]{:S(2)}) collective-permute-start(f32[448,384]{1,0:T(8,128)S(1)} %get-tuple-element.288.refs_2_), channel_id=1, source_target_pairs={{0,1},{1,0},{2,3},{3,2},{4,5},{5,4},{6,7},{7,6},{8,9},{9,8},{10,11... | collective-permute-start | bytes 2064392 | tf_op jit(solution)/shard_map/ppermute | solution.py:847
  156.8 26.6 %collective-permute-start.14 = (f32[384,384]{1,0:T(8,128)}, f32[384,384]{1,0:T(8,128)}, u32[]{:S(2)}, u32[]{:S(2)}) collective-permute-start(f32[384,384]{1,0:T(8,128)} %collective-permute-done.9.refs_1_.refs_5_), channel_id=1, source_target_pairs={{0,2},{2,0},{4,6},{6,4},{8,10},{10,8},{12,14},{14,12},{16,18},{18,... | collective-permute-start | bytes 1769480 | tf_op jit(solution)/shard_map/ppermute | solution.py:851
  166.5 9.8 %collective-permute-start.13 = (f32[384,1536]{1,0:T(8,128)S(1)}, f32[384,1536]{1,0:T(8,128)S(1)}, u32[]{:S(2)}, u32[]{:S(2)}) collective-permute-start(f32[384,1536]{1,0:T(8,128)S(1)} %get-tuple-element.289), channel_id=1, source_target_pairs={{0,2},{2,0},{4,6},{6,4},{8,10},{10,8},{12,14},{14,12},{16,18},{18,... | collective-permute-start | bytes 7077896 | tf_op jit(solution)/shard_map/ppermute | solution.py:851
  166.6 33.6 %collective-permute-start.15 = (f32[376,384]{1,0:T(8,128)}, f32[376,384]{1,0:T(8,128)}, u32[]{:S(2)}, u32[]{:S(2)}) collective-permute-start(f32[376,384]{1,0:T(8,128)} %get-tuple-element.302), channel_id=1, source_target_pairs={{0,1},{1,0},{2,3},{3,2},{4,5},{5,4},{6,7},{7,6},{8,9},{9,8},{10,11... | collective-permute-start | bytes 1732616 | tf_op jit(solution)/shard_map/ppermute | solution.py:847
  168.2 32.6 %collective-permute-start.16 = (f32[96,1536]{1,0:T(8,128)}, f32[96,1536]{1,0:T(8,128)}, u32[]{:S(2)}, u32[]{:S(2)}) collective-permute-start(f32[96,1536]{1,0:T(8,128)} %get-tuple-element.304), channel_id=1, source_target_pairs={{0,8},{2,10},{4,12},{6,14},{8,0},{10,2},{12,4},{14,6},{16,24},{18,... | collective-permute-start | bytes 1769480 | tf_op jit(solution)/shard_map/ppermute | solution.py:851
  173.3 3.0 %copy-start.12 = (f32[448,384]{1,0:T(8,128)}, f32[448,384]{1,0:T(8,128)S(1)}, u32[]{:S(2)}) copy-start(f32[448,384]{1,0:T(8,128)S(1)} %collective-permute-done.12.refs_1_.refs_3_) | copy-start | bytes 2064388
  173.3 27.5 %collective-permute-start.17 = (f32[96,1536]{1,0:T(8,128)}, f32[96,1536]{1,0:T(8,128)}, u32[]{:S(2)}, u32[]{:S(2)}) collective-permute-start(f32[96,1536]{1,0:T(8,128)} %get-tuple-element.306), channel_id=1, source_target_pairs={{0,16},{2,18},{4,20},{6,22},{8,24},{10,26},{12,28},{14,30},{16,0},... | collective-permute-start | bytes 1769480 | tf_op jit(solution)/shard_map/ppermute | solution.py:851
  181.9 27.0 %collective-permute-start.18 = (f32[376,384]{1,0:T(8,128)}, f32[376,384]{1,0:T(8,128)}, u32[]{:S(2)}, u32[]{:S(2)}) collective-permute-start(f32[376,384]{1,0:T(8,128)} %get-tuple-element.318), channel_id=1, source_target_pairs={{0,1},{1,0},{2,3},{3,2},{4,5},{5,4},{6,7},{7,6},{8,9},{9,8},{10,11... | collective-permute-start | bytes 1732616 | tf_op jit(solution)/shard_map/ppermute | solution.py:847
  183.5 27.3 %collective-permute-start.19 = (f32[192,1536]{1,0:T(8,128)}, f32[192,1536]{1,0:T(8,128)}, u32[]{:S(2)}, u32[]{:S(2)}) collective-permute-start(f32[192,1536]{1,0:T(8,128)} %get-tuple-element.320), channel_id=1, source_target_pairs={{0,4},{2,6},{4,0},{6,2},{8,12},{10,14},{12,8},{14,10},{16,20},{18,... | collective-permute-start | bytes 3538952 | tf_op jit(solution)/shard_map/ppermute | solution.py:851
  199.6 0.6 copy-start.7
  200.2 17.9 %collective-permute-start.20 = (f32[256,768]{1,0:T(8,128)S(1)}, f32[256,768]{1,0:T(8,128)S(1)}, u32[]{:S(2)}, u32[]{:S(2)}) collective-permute-start(f32[256,768]{1,0:T(8,128)S(1)} %get-tuple-element.323.refs_4_), channel_id=1, source_target_pairs={{0,1},{1,0},{2,3},{3,2},{4,5},{5,4},{6,7},{7,6},{8,9},{9,8},{10,11... | collective-permute-start | bytes 2359304 | tf_op jit(solution)/shard_map/ppermute | solution.py:847
  202.8 18.5 %collective-permute-start.21 = (f32[48,1536]{1,0:T(8,128)}, f32[48,1536]{1,0:T(8,128)}, u32[]{:S(2)}, u32[]{:S(2)}) collective-permute-start(f32[48,1536]{1,0:T(8,128)} %get-tuple-element.326), channel_id=1, source_target_pairs={{0,16},{2,18},{4,20},{6,22},{8,24},{10,26},{12,28},{14,30},{16,0},... | collective-permute-start | bytes 884744 | tf_op jit(solution)/shard_map/ppermute | solution.py:851
  203.7 17.6 %collective-permute-start.22 = (f32[48,1536]{1,0:T(8,128)}, f32[48,1536]{1,0:T(8,128)}, u32[]{:S(2)}, u32[]{:S(2)}) collective-permute-start(f32[48,1536]{1,0:T(8,128)} %get-tuple-element.328), channel_id=1, source_target_pairs={{0,4},{2,6},{4,0},{6,2},{8,12},{10,14},{12,8},{14,10},{16,20},{18,... | collective-permute-start | bytes 884744 | tf_op jit(solution)/shard_map/ppermute | solution.py:851
  208.9 14.3 %collective-permute-start.23 = (f32[384,1536]{1,0:T(8,128)S(1)}, f32[384,1536]{1,0:T(8,128)S(1)}, u32[]{:S(2)}, u32[]{:S(2)}) collective-permute-start(f32[384,1536]{1,0:T(8,128)S(1)} %get-tuple-element.330), channel_id=1, source_target_pairs={{0,2},{2,0},{4,6},{6,4},{8,10},{10,8},{12,14},{14,12},{16,18},{18,... | collective-permute-start | bytes 7077896 | tf_op jit(solution)/shard_map/ppermute | solution.py:851
  210.8 17.2 %collective-permute-start.24 = (f32[192,768]{1,0:T(8,128)}, f32[192,768]{1,0:T(8,128)}, u32[]{:S(2)}, u32[]{:S(2)}) collective-permute-start(f32[192,768]{1,0:T(8,128)} %get-tuple-element.336.refs_4_), channel_id=1, source_target_pairs={{0,1},{1,0},{2,3},{3,2},{4,5},{5,4},{6,7},{7,6},{8,9},{9,8},{10,11... | collective-permute-start | bytes 1769480 | tf_op jit(solution)/shard_map/ppermute | solution.py:847
  218.1 16.3 %collective-permute-start.25 = (f32[96,1536]{1,0:T(8,128)}, f32[96,1536]{1,0:T(8,128)}, u32[]{:S(2)}, u32[]{:S(2)}) collective-permute-start(f32[96,1536]{1,0:T(8,128)} %get-tuple-element.351), channel_id=1, source_target_pairs={{0,8},{2,10},{4,12},{6,14},{8,0},{10,2},{12,4},{14,6},{16,24},{18,... | collective-permute-start | bytes 1769480 | tf_op jit(solution)/shard_map/ppermute | solution.py:851
  226.5 15.5 %collective-permute-start.26 = (f32[192,768]{1,0:T(8,128)S(1)}, f32[192,768]{1,0:T(8,128)S(1)}, u32[]{:S(2)}, u32[]{:S(2)}) collective-permute-start(f32[192,768]{1,0:T(8,128)S(1)} %get-tuple-element.354), channel_id=1, source_target_pairs={{0,4},{2,6},{4,0},{6,2},{8,12},{10,14},{12,8},{14,10},{16,20},{18,... | collective-permute-start | bytes 1769480 | tf_op jit(solution)/shard_map/ppermute | solution.py:851
  228.0 5.1 %copy-start.14 = (f32[376,384]{1,0:T(8,128)S(1)}, f32[376,384]{1,0:T(8,128)}, u32[]{:S(2)}) copy-start(f32[376,384]{1,0:T(8,128)} %get-tuple-element.359) | copy-start | bytes 1732612
  233.0 9.1 %collective-permute-start.27 = (f32[15,768]{1,0:T(8,128)S(1)}, f32[15,768]{1,0:T(8,128)S(1)}, u32[]{:S(2)}, u32[]{:S(2)}) collective-permute-start(f32[15,768]{1,0:T(8,128)S(1)} %get-tuple-element.356.refs_1_), channel_id=1, source_target_pairs={{0,2},{2,0},{4,6},{6,4},{8,10},{10,8},{12,14},{14,12},{16,18},{18,... | collective-permute-start | bytes 138248 | tf_op jit(solution)/shard_map/ppermute | solution.py:851
  233.1 15.5 %collective-permute-start.28 = (f32[376,384]{1,0:T(8,128)S(1)}, f32[376,384]{1,0:T(8,128)S(1)}, u32[]{:S(2)}, u32[]{:S(2)}) collective-permute-start(f32[376,384]{1,0:T(8,128)S(1)} %copy-done.14), channel_id=1, source_target_pairs={{0,1},{1,0},{2,3},{3,2},{4,5},{5,4},{6,7},{7,6},{8,9},{9,8},{10,11... | collective-permute-start | bytes 1732616 | tf_op jit(solution)/shard_map/ppermute | solution.py:847
  233.7 18.2 %collective-permute-start.29 = (f32[192,768]{1,0:T(8,128)S(1)}, f32[192,768]{1,0:T(8,128)S(1)}, u32[]{:S(2)}, u32[]{:S(2)}) collective-permute-start(f32[192,768]{1,0:T(8,128)S(1)} %get-tuple-element.361), channel_id=1, source_target_pairs={{0,4},{2,6},{4,0},{6,2},{8,12},{10,14},{12,8},{14,10},{16,20},{18,... | collective-permute-start | bytes 1769480 | tf_op jit(solution)/shard_map/ppermute | solution.py:851
  235.6 17.9 %collective-permute-start.30 = (f32[48,1536]{1,0:T(8,128)S(1)}, f32[48,1536]{1,0:T(8,128)S(1)}, u32[]{:S(2)}, u32[]{:S(2)}) collective-permute-start(f32[48,1536]{1,0:T(8,128)S(1)} %get-tuple-element.364), channel_id=1, source_target_pairs={{0,16},{2,18},{4,20},{6,22},{8,24},{10,26},{12,28},{14,30},{16,0},... | collective-permute-start | bytes 884744 | tf_op jit(solution)/shard_map/ppermute | solution.py:851
  242.0 13.7 %collective-permute-start.31 = (f32[96,768]{1,0:T(8,128)S(1)}, f32[96,768]{1,0:T(8,128)S(1)}, u32[]{:S(2)}, u32[]{:S(2)}) collective-permute-start(f32[96,768]{1,0:T(8,128)S(1)} %get-tuple-element.367), channel_id=1, source_target_pairs={{0,8},{2,10},{4,12},{6,14},{8,0},{10,2},{12,4},{14,6},{16,24},{18,... | collective-permute-start | bytes 884744 | tf_op jit(solution)/shard_map/ppermute | solution.py:851
  242.1 16.7 %collective-permute-start.32 = (f32[15,768]{1,0:T(8,128)S(1)}, f32[15,768]{1,0:T(8,128)S(1)}, u32[]{:S(2)}, u32[]{:S(2)}) collective-permute-start(f32[15,768]{1,0:T(8,128)S(1)} %get-tuple-element.369.refs_1_), channel_id=1, source_target_pairs={{0,8},{2,10},{4,12},{6,14},{8,0},{10,2},{12,4},{14,6},{16,24},{18,... | collective-permute-start | bytes 138248 | tf_op jit(solution)/shard_map/ppermute | solution.py:851
  248.6 3.3 %copy-start.15 = (f32[376,384]{1,0:T(8,128)}, f32[376,384]{1,0:T(8,128)S(1)}, u32[]{:S(2)}) copy-start(f32[376,384]{1,0:T(8,128)S(1)} %collective-permute-done.28.refs_1_.refs_7_) | copy-start | bytes 1732612
  251.9 1.1 copy-start.13
  251.9 10.9 %collective-permute-start.33 = (f32[96,768]{1,0:T(8,128)S(1)}, f32[96,768]{1,0:T(8,128)S(1)}, u32[]{:S(2)}, u32[]{:S(2)}) collective-permute-start(f32[96,768]{1,0:T(8,128)S(1)} %get-tuple-element.372), channel_id=1, source_target_pairs={{0,8},{2,10},{4,12},{6,14},{8,0},{10,2},{12,4},{14,6},{16,24},{18,... | collective-permute-start | bytes 884744 | tf_op jit(solution)/shard_map/ppermute | solution.py:851
  252.9 12.8 %collective-permute-start.35 = (f32[376,384]{1,0:T(8,128)S(1)}, f32[376,384]{1,0:T(8,128)S(1)}, u32[]{:S(2)}, u32[]{:S(2)}) collective-permute-start(f32[376,384]{1,0:T(8,128)S(1)} %copy-done.13), channel_id=1, source_target_pairs={{0,1},{1,0},{2,3},{3,2},{4,5},{5,4},{6,7},{7,6},{8,9},{9,8},{10,11... | collective-permute-start | bytes 1732616 | tf_op jit(solution)/shard_map/ppermute | solution.py:847
  258.8 6.5 %collective-permute-start.34 = (f32[15,768]{1,0:T(8,128)S(1)}, f32[15,768]{1,0:T(8,128)S(1)}, u32[]{:S(2)}, u32[]{:S(2)}) collective-permute-start(f32[15,768]{1,0:T(8,128)S(1)} %get-tuple-element.374.refs_1_), channel_id=1, source_target_pairs={{0,16},{2,18},{4,20},{6,22},{8,24},{10,26},{12,28},{14,30},{16,0},... | collective-permute-start | bytes 138248 | tf_op jit(solution)/shard_map/ppermute | solution.py:851
  258.9 13.3 %collective-permute-start.36 = (f32[48,768]{1,0:T(8,128)S(1)}, f32[48,768]{1,0:T(8,128)S(1)}, u32[]{:S(2)}, u32[]{:S(2)}) collective-permute-start(f32[48,768]{1,0:T(8,128)S(1)} %get-tuple-element.381), channel_id=1, source_target_pairs={{0,16},{2,18},{4,20},{6,22},{8,24},{10,26},{12,28},{14,30},{16,0},... | collective-permute-start | bytes 442376 | tf_op jit(solution)/shard_map/ppermute | solution.py:851
  262.9 9.9 %collective-permute-start.37 = (f32[48,768]{1,0:T(8,128)S(1)}, f32[48,768]{1,0:T(8,128)S(1)}, u32[]{:S(2)}, u32[]{:S(2)}) collective-permute-start(f32[48,768]{1,0:T(8,128)S(1)} %get-tuple-element.385), channel_id=1, source_target_pairs={{0,16},{2,18},{4,20},{6,22},{8,24},{10,26},{12,28},{14,30},{16,0},... | collective-permute-start | bytes 442376 | tf_op jit(solution)/shard_map/ppermute | solution.py:851
  265.3 7.6 %collective-permute-start.38 = (f32[15,768]{1,0:T(8,128)S(1)}, f32[15,768]{1,0:T(8,128)S(1)}, u32[]{:S(2)}, u32[]{:S(2)}) collective-permute-start(f32[15,768]{1,0:T(8,128)S(1)} %get-tuple-element.389.refs_1_), channel_id=1, source_target_pairs={{0,4},{2,6},{4,0},{6,2},{8,12},{10,14},{12,8},{14,10},{16,20},{18,... | collective-permute-start | bytes 138248 | tf_op jit(solution)/shard_map/ppermute | solution.py:851
  265.7 0.8 copy-start.16

commit v2 on v1

--- a/solution.py
+++ b/solution.py
@@ -1175,7 +1175,7 @@
         "tokens_end",
         scratch=[pltpu.VMEM((8, model), F32)],
     )
-    small_bits = bits[:1] + bits[2:] + bits[1:2]
+    small_bits = bits[2:] + bits[:2]
 
     def small_step(total, other):
         (total,) = chain(plain_end, [(shaped(total.shape), "v")], [(total, "v"), (other, "v")], 0, "small_step")

time: 275 us -> 275 us (level)
    ppermute x16, waiting for transfers between devices: 31.2 us -> 34.5 us  [swap_mp(): return lax.ppermute(v, 'mp', [(0, 1), (1, 0)])]
  transfers between devices with their start and end apart: 39 -> 39, of which waited for: 21 -> 19; matrix products, arithmetic and copies ran while one was open for 1% -> 1% of each run, Pallas kernels for 57% -> 57%
where the time goes in v2:
time: 275 us
  Pallas kernels  166 us (60%)
  waiting for transfers between devices  54.2 us (20%)
  starting transfers between devices  44 us (16%)
  local copies, waits for them, and re-layouts  7.53 us (3%)
    pallas_call x40, Pallas kernels, __call__(): pl.pallas_call(body, out_shape=tuple((pltpu.HBM(o.shape, o.dtype) if k in...  166 us
    ppermute x16, waiting for transfers between devices, swap_mp(): return lax.ppermute(v, 'mp', [(0, 1), (1, 0)])  34.5 us
    ppermute x16, starting transfers between devices, swap_mp(): return lax.ppermute(v, 'mp', [(0, 1), (1, 0)])  23.2 us
    ppermute x23, starting transfers between devices, swap_dp(): return lax.ppermute(v, 'dp', [(i, i ^ bit) for i in range(dp_size)])  20.8 us
    ppermute x23, waiting for transfers between devices, swap_dp(): return lax.ppermute(v, 'dp', [(i, i ^ bit) for i in range(dp_size)])  19.7 us
  transfers between devices with their start and end apart: 39, of which 19 were waited for; matrix products, arithmetic and copies ran while one was open for 1% of the time, Pallas kernels for 57%

profile of v2, /device:TPU:0, one launch (start us, length us, event | category | flops | bytes accessed | tf_op | source)
XLA Modules:
  0.0 274.8 jit_solution(7068257763552376258)
XLA Ops:
  1.3 7.1 %self_start.1 = (f32[8,128]{1,0:T(8,128)}, bf16[192,768]{1,0:T(8,128)(2,1)}, bf16[256,768]{1,0:T(8,128)(2,1)}, bf16[448,384]{1,0:T(8,128)(2,1)}, bf16[448,384]{1...) custom-call(f32[4,768]{1,0:T(4,128)} %refs_2_.5, ...), custom_call_target="tpu_custom_call" | custom-call | flops 30000001024 | bytes 192000000 | tf_op jit(solution)/shard_map/self_start/pallas_call | solution.py:171
  8.4 3.0 %collective-permute-start = (f32[256,768]{1,0:T(8,128)S(1)}, f32[256,768]{1,0:T(8,128)S(1)}, u32[]{:S(2)}, u32[]{:S(2)}) collective-permute-start(f32[256,768]{1,0:T(8,128)S(1)} %get-tuple-element.215.refs_1_), channel_id=1, source_target_pairs={{0,1},{1,0},{2,3},{3,2},{4,5},{5,4},{6,7},{7,6},{8,9},{9,8},{10,11... | collective-permute-start | bytes 2359304 | tf_op jit(solution)/shard_map/ppermute | solution.py:847
  11.4 4.2 %self_next.1 = (f32[8,128]{1,0:T(8,128)}, bf16[192,384]{1,0:T(8,128)(2,1)}, f32[192,384]{1,0:T(8,128)}, f32[8,192]{1,0:T(8,128)}, f32[192,768]{1,0:T(8,128)S(1)}) custom-call(f32[8,128]{1,0:T(8,128)} %get-tuple-element.209.refs_0_, bf16[448,384]{1,0:T(8,128)(2,1)} %get-tuple-element.210.refs_1_.refs_9_, ...), custom_call_target="tpu_custom_call" | custom-call | flops 19499999232 | bytes 124800000 | tf_op jit(solution)/shard_map/self_next/pallas_call | solution.py:171
  15.7 1.2 copy.37
  17.8 9.0 %frames_start.1 = (f32[8,128]{1,0:T(8,128)}, bf16[1536,384]{1,0:T(8,128)(2,1)}, bf16[1536,384]{1,0:T(8,128)(2,1)}, bf16[768,1536]{1,0:T(8,128)(2,1)}, bf16[768,7...) custom-call(f32[8,128]{1,0:T(8,128)} %get-tuple-element.213.refs_0_, bf16[1500,768]{1,0:T(8,128)(2,1)} %bitcast.24, ...), custom_call_target="tpu_custom_call" | custom-call | flops 44999999488 | bytes 288000000 | tf_op jit(solution)/shard_map/frames_start/pallas_call | solution.py:171
  28.3 1.5 collective-permute-done.refs_2_
  29.8 7.6 %cross_start.2 = (f32[8,128]{1,0:T(8,128)}, f32[256,768]{1,0:T(8,128)}, bf16[256,768]{1,0:T(8,128)(2,1)}, bf16[256,384]{1,0:T(8,128)(2,1)}, bf16[256,384]{1,0:T(...) custom-call(f32[8,128]{1,0:T(8,128)} %get-tuple-element.214.refs_0_, ...), custom_call_target="tpu_custom_call" | custom-call | flops 40499998720 | bytes 259200000 | tf_op jit(solution)/shard_map/cross_start/pallas_call | solution.py:171
  37.4 2.1 collective-permute-start.2
  39.5 2.9 %collective-permute-done.1.refs_2_ = f32[192,768]{1,0:T(8,128)S(1)} collective-permute-done((f32[192,768]{1,0:T(8,128)S(1)}, f32[192,768]{1,0:T(8,128)S(1)}, u32[]{:S(2)}, u32[]{:S(2)}) %collective-permute-start.1) | collective-permute-done | bytes 589856 | tf_op jit(solution)/shard_map/ppermute | solution.py:847
  42.4 6.9 %cross_start.3 = (f32[8,128]{1,0:T(8,128)}, f32[192,768]{1,0:T(8,128)}, bf16[192,768]{1,0:T(8,128)(2,1)}, bf16[192,384]{1,0:T(8,128)(2,1)}, bf16[192,384]{1,0:T(...) custom-call(f32[8,128]{1,0:T(8,128)} %get-tuple-element.218.refs_0_, ...), custom_call_target="tpu_custom_call" | custom-call | flops 40499998720 | bytes 259200000 | tf_op jit(solution)/shard_map/cross_start/pallas_call | solution.py:171
  49.3 2.1 collective-permute-start.3
  51.4 5.7 %turn.2 = (f32[8,128]{1,0:T(8,128)}, bf16[768,256]{1,0:T(8,128)(2,1)}, bf16[768,192]{1,0:T(8,128)(2,1)}, bf16[768,256]{1,0:T(8,128)(2,1)}, bf16[768,192]{1,0:T(8,128)(2,1)}) custom-call(f32[8,128]{1,0:T(8,128)} %get-tuple-element.220.refs_0_, bf16[768,768]{1,0:T(8,128)(2,1)} %get-tuple-element.221.refs_1_, bf16[256,768]{1,0:T(8,128)(2,1)} %get-tuple-element.222.refs_2_, ...), custom_call_target="tpu_custom_call" | custom-call | flops 15000000512 | bytes 96000000 | tf_op jit(solution)/shard_map/turn/pallas_call | solution.py:171
  57.1 2.1 collective-permute-done.2.refs_2_
  59.3 7.4 %dense_start.2 = (f32[8,128]{1,0:T(8,128)}, f32[256,768]{1,0:T(8,128)}, bf16[256,768]{1,0:T(8,128)(2,1)}, bf16[256,1536]{1,0:T(8,128)(2,1)}, f32[256,1536]{1,0:T(8,128)}, /*index=5*/f32[256,768]{1,0:T(8,128)S(1)}) custom-call(f32[8,128]{1,0:T(8,128)} %get-tuple-element.226.refs_0_, f32[256,768]{1,0:T(8,128)S(1)} %get-tuple-element.227.refs_1_, ...), custom_call_target="tpu_custom_call" | custom-call | flops 35999997952 | bytes 230400000 | tf_op jit(solution)/shard_map/dense_start/pallas_call | solution.py:171
  66.7 2.1 collective-permute-start.4
  68.8 3.1 %collective-permute-done.3.refs_2_ = f32[192,768]{1,0:T(8,128)S(1)} collective-permute-done((f32[192,768]{1,0:T(8,128)S(1)}, f32[192,768]{1,0:T(8,128)S(1)}, u32[]{:S(2)}, u32[]{:S(2)}) %collective-permute-start.3) | collective-permute-done | bytes 589856 | tf_op jit(solution)/shard_map/ppermute | solution.py:847
  71.9 6.6 %dense_start.3 = (f32[8,128]{1,0:T(8,128)}, f32[192,768]{1,0:T(8,128)}, bf16[192,768]{1,0:T(8,128)(2,1)}, bf16[192,1536]{1,0:T(8,128)(2,1)}, f32[192,1536]{1,0:T(8,128)}, /*index=5*/f32[192,768]{1,0:T(8,128)S(1)}) custom-call(f32[8,128]{1,0:T(8,128)} %get-tuple-element.229.refs_0_, f32[192,768]{1,0:T(8,128)S(1)} %get-tuple-element.230.refs_1_, ...), custom_call_target="tpu_custom_call" | custom-call | flops 35999997952 | bytes 230400000 | tf_op jit(solution)/shard_map/dense_start/pallas_call | solution.py:171
  78.5 2.1 collective-permute-start.5
  80.7 4.3 %turn.3 = (f32[8,128]{1,0:T(8,128)}, bf16[768,256]{1,0:T(8,128)(2,1)}, bf16[768,192]{1,0:T(8,128)(2,1)}) custom-call(f32[8,128]{1,0:T(8,128)} %get-tuple-element.232.refs_0_, bf16[768,768]{1,0:T(8,128)(2,1)} %get-tuple-element.221.refs_1_, bf16[768,768]{1,0:T(8,128)(2,1)} %get-tuple-element.233.refs_2_, bf16[256,768]{1,0:T(8,128)(2,1)} %get-tuple-element.234.refs_3_, ...), custom_call_target="tpu_custom_call" | custom-call | flops 15000000512 | bytes 96000000 | tf_op jit(solution)/shard_map/turn/pallas_call | solution.py:171
  85.0 3.8 %collective-permute-done.4.refs_2_ = f32[256,768]{1,0:T(8,128)S(1)} collective-permute-done((f32[256,768]{1,0:T(8,128)S(1)}, f32[256,768]{1,0:T(8,128)S(1)}, u32[]{:S(2)}, u32[]{:S(2)}) %collective-permute-start.4) | collective-permute-done | bytes 786464 | tf_op jit(solution)/shard_map/ppermute | solution.py:847
  88.8 7.3 %dense_back.2 = (f32[8,128]{1,0:T(8,128)}, bf16[256,768]{1,0:T(8,128)(2,1)}, f32[256,768]{1,0:T(8,128)}, bf16[256,768]{1,0:T(8,128)(2,1)}, bf16[256,1536]{1,0:T(...) custom-call(f32[8,128]{1,0:T(8,128)} %get-tuple-element.236.refs_0_, ...), custom_call_target="tpu_custom_call" | custom-call | flops 35999997952 | bytes 230400000 | tf_op jit(solution)/shard_map/dense_back/pallas_call | solution.py:171
  96.1 2.1 collective-permute-start.6
  98.2 3.2 %collective-permute-done.5.refs_2_ = f32[192,768]{1,0:T(8,128)S(1)} collective-permute-done((f32[192,768]{1,0:T(8,128)S(1)}, f32[192,768]{1,0:T(8,128)S(1)}, u32[]{:S(2)}, u32[]{:S(2)}) %collective-permute-start.5) | collective-permute-done | bytes 589856 | tf_op jit(solution)/shard_map/ppermute | solution.py:847
  101.4 7.7 %dense_back.3 = (f32[8,128]{1,0:T(8,128)}, bf16[192,768]{1,0:T(8,128)(2,1)}, f32[192,768]{1,0:T(8,128)}, bf16[192,768]{1,0:T(8,128)(2,1)}, bf16[192,1536]{1,0:T(...) custom-call(f32[8,128]{1,0:T(8,128)} %get-tuple-element.240.refs_0_, ...), custom_call_target="tpu_custom_call" | custom-call | flops 35999997952 | bytes 230400000 | tf_op jit(solution)/shard_map/dense_back/pallas_call | solution.py:171
  110.4 5.1 %dense_sent.1 = (f32[8,128]{1,0:T(8,128)}, f32[384,3072]{1,0:T(8,128)S(1)}, bf16[768,256]{1,0:T(8,128)(2,1)}, bf16[768,192]{1,0:T(8,128)(2,1)}) custom-call(f32[8,128]{1,0:T(8,128)} %get-tuple-element.244.refs_0_, bf16[768,768]{1,0:T(8,128)(2,1)} %get-tuple-element.221.refs_1_, bf16[768,768]{1,0:T(8,128)(2,1)} %get-tuple-element.233.refs_2_, ...), custom_call_target="tpu_custom_call" | custom-call | flops 89999998976 | bytes 576000000 | tf_op jit(solution)/shard_map/dense_sent/pallas_call | solution.py:171
  115.6 2.1 collective-permute-start.8
  118.7 4.7 %collective-permute-done.7.refs_1_ = f32[384,3072]{1,0:T(8,128)S(1)} collective-permute-done((f32[384,3072]{1,0:T(8,128)S(1)}, f32[384,3072]{1,0:T(8,128)S(1)}, u32[]{:S(2)}, u32[]{:S(2)}) %collective-permute-start.7) | collective-permute-done | bytes 4718624 | tf_op jit(solution)/shard_map/ppermute | solution.py:851
  123.5 4.2 %dense_kept.1 = (f32[8,128]{1,0:T(8,128)}, f32[192,1536]{1,0:T(8,128)}, f32[192,1536]{1,0:T(8,128)S(1)}, f32[192,1536]{1,0:T(8,128)}, f32[192,1536]{1,0:T(8,128)S(1)}) custom-call(f32[8,128]{1,0:T(8,128)} %pause.2.refs_0_, f32[384,3072]{1,0:T(8,128)S(1)} %collective-permute-done.7.refs_1_, bf16[768,256]{1,0:T(8,128)(2,1)} %get-tuple-element.256.refs_2_, ...), custom_call_target="tpu_custom_call" | custom-call | flops 89999998976 | bytes 576000000 | tf_op jit(solution)/shard_map/dense_kept/pallas_call | solution.py:171
  127.7 2.1 collective-permute-start.10
  129.8 1.6 collective-permute-start.11
  132.2 22.6 %cross_back.1 = (f32[8,128]{1,0:T(8,128)}, f32[256,768]{1,0:T(8,128)}, bf16[256,768]{1,0:T(8,128)(2,1)}, f32[192,768]{1,0:T(8,128)}, bf16[192,768]{1,0:T(8,128)(...) custom-call(f32[8,128]{1,0:T(8,128)} %get-tuple-element.258.refs_0_,, ...), custom_call_target="tpu_custom_call" | custom-call | flops 299999985664 | bytes 1920000000 | tf_op jit(solution)/shard_map/cross_back/pallas_call | solution.py:171
  154.8 2.0 collective-permute-start.12
  156.9 1.0 collective-permute-done.11.refs_5_
  157.8 2.9 %steps.2 = (f32[8,128]{1,0:T(8,128)}, f32[96,1536]{1,0:T(8,128)}, f32[96,1536]{1,0:T(8,128)S(1)}, f32[96,1536]{1,0:T(8,128)}, f32[96,1536]{1,0:T(8,128)S(1)}) custom-call(f32[8,128]{1,0:T(8,128)} %get-tuple-element.269.refs_0_, f32[384,384]{1,0:T(8,128)} %collective-permute-done.9.refs_1_.refs_5_, f32[192,1536]{1,0:T(8,128)S(1)} %get-tuple-element.271.refs_2_, ...), custom_call_target="tpu_custom_call" | custom-call | flops 15000000512 | bytes 96000000 | tf_op jit(solution)/shard_map/steps/pallas_call | solution.py:171
  160.8 5.8 %cross_sent.1 = (f32[8,128]{1,0:T(8,128)}, f32[384,1536]{1,0:T(8,128)S(1)}, bf16[768,256]{1,0:T(8,128)(2,1)}, bf16[768,192]{1,0:T(8,128)(2,1)}) custom-call(f32[8,128]{1,0:T(8,128)} %get-tuple-element.275.refs_0_, bf16[768,768]{1,0:T(8,128)(2,1)} %get-tuple-element.221.refs_1_, bf16[256,768]{1,0:T(8,128)(2,1)} %get-tuple-element.276.refs_2_, ...), custom_call_target="tpu_custom_call" | custom-call | flops 89999998976 | bytes 576000000 | tf_op jit(solution)/shard_map/cross_sent/pallas_call | solution.py:171
  166.6 1.6 collective-permute-start.15
  168.2 1.6 collective-permute-start.16
  169.7 3.5 %collective-permute-done.12.refs_1_.refs_3_ = f32[448,384]{1,0:T(8,128)S(1)} collective-permute-done((f32[448,384]{1,0:T(8,128)S(1)}, f32[448,384]{1,0:T(8,128)S(1)}, u32[]{:S(2)}, u32[]{:S(2)}) %collective-permute-start.12) | collective-permute-done | bytes 688160 | tf_op jit(solution)/shard_map/ppermute | solution.py:847
  173.3 3.0 %collective-permute-start.17 = (f32[96,1536]{1,0:T(8,128)}, f32[96,1536]{1,0:T(8,128)}, u32[]{:S(2)}, u32[]{:S(2)}) collective-permute-start(f32[96,1536]{1,0:T(8,128)} %get-tuple-element.306), channel_id=1, source_target_pairs={{0,16},{2,18},{4,20},{6,22},{8,24},{10,26},{12,28},{14,30},{16,0},... | collective-permute-start | bytes 1769480 | tf_op jit(solution)/shard_map/ppermute | solution.py:851
  176.3 5.6 %cross_kept.1 = (f32[8,128]{1,0:T(8,128)}, f32[192,1536]{1,0:T(8,128)}, f32[192,1536]{1,0:T(8,128)S(1)}) custom-call(f32[8,128]{1,0:T(8,128)} %pause.3.refs_0_, f32[384,1536]{1,0:T(8,128)S(1)} %collective-permute-done.13.refs_1_, bf16[768,256]{1,0:T(8,128)(2,1)} %get-tuple-element.290.refs_2_, bf16[768,192]{1,0:T(8,128)(2,1)} %get-tuple-element.291.refs_3_, ...), custom_call_target="tpu_custom_call" | custom-call | flops 74999996416 | bytes 480000000 | tf_op jit(solution)/shard_map/cross_kept/pallas_call | solution.py:171
  181.9 1.6 collective-permute-start.18
  183.5 1.5 collective-permute-start.19
  185.0 14.5 %self_back.1 = (f32[8,128]{1,0:T(8,128)}, f32[256,768]{1,0:T(8,128)}, bf16[256,768]{1,0:T(8,128)(2,1)}, f32[192,768]{1,0:T(8,128)}, bf16[192,768]{1,0:T(8,128)(2...) custom-call(f32[8,128]{1,0:T(8,128)} %get-tuple-element.292.refs_0_,, ...), custom_call_target="tpu_custom_call" | custom-call | flops 179999997952 | bytes 1152000000 | tf_op jit(solution)/shard_map/self_back/pallas_call | solution.py:171
  200.7 2.1 steps.3
  204.2 4.7 %self_sent.1 = (f32[8,128]{1,0:T(8,128)}, f32[384,1536]{1,0:T(8,128)S(1)}, bf16[768,256]{1,0:T(8,128)(2,1)}, bf16[768,192]{1,0:T(8,128)(2,1)}) custom-call(f32[8,128]{1,0:T(8,128)} %get-tuple-element.307.refs_0_, bf16[768,768]{1,0:T(8,128)(2,1)} %get-tuple-element.221.refs_1_, bf16[256,768]{1,0:T(8,128)(2,1)} %get-tuple-element.308.refs_2_, ...), custom_call_target="tpu_custom_call" | custom-call | flops 74999996416 | bytes 480000000 | tf_op jit(solution)/shard_map/self_sent/pallas_call | solution.py:171
  209.0 1.7 collective-permute-done.19.refs_3_
  211.3 2.3 cross0_step.2
  213.6 4.5 %collective-permute-done.20.refs_5_ = f32[256,768]{1,0:T(8,128)S(1)} collective-permute-done((f32[256,768]{1,0:T(8,128)S(1)}, f32[256,768]{1,0:T(8,128)S(1)}, u32[]{:S(2)}, u32[]{:S(2)}) %collective-permute-start.20) | collective-permute-done | bytes 786464 | tf_op jit(solution)/shard_map/ppermute | solution.py:847
  218.3 3.0 %tokens_end.2 = (f32[8,128]{1,0:T(8,128)}, f32[256,768]{1,0:T(8,128)}, f32[8,768]{1,0:T(8,128)}) custom-call(f32[8,128]{1,0:T(8,128)} %get-tuple-element.321.refs_0_, bf16[448,768]{1,0:T(8,128)(2,1)} %bitcast.32, f32[4,768]{1,0:T(4,128)} %refs_2_.5, f32[256,768]{1,0:T(8,128)} %get-tuple-element.322.refs_3_, f32[256,768]{1,0:T(8,128)S(1)} %get-tuple-element.323.refs_4_, ...), custom_call_target="tpu_custom_call" | custom-call | flops 74999996416 | bytes 480000000 | tf_op jit(solution)/shard_map/tokens_end/pallas_call | solution.py:171
  221.4 1.9 ends.1
  223.3 3.2 %self_kept.1 = (f32[8,128]{1,0:T(8,128)}, f32[192,768]{1,0:T(8,128)S(1)}, f32[192,768]{1,0:T(8,128)S(1)}, f32[192,768]{1,0:T(8,128)S(1)}, f32[192,768]{1,0:T(8,128)S(1)}) custom-call(f32[8,128]{1,0:T(8,128)} %get-tuple-element.329.refs_0_, f32[384,1536]{1,0:T(8,128)S(1)} %collective-permute-done.23.refs_1_, bf16[768,256]{1,0:T(8,128)(2,1)} %get-tuple-element.331.refs_2_, ...), custom_call_target="tpu_custom_call" | custom-call | flops 60000002048 | bytes 384000000 | tf_op jit(solution)/shard_map/self_kept/pallas_call | solution.py:171
  227.0 1.0 collective-permute-done.24.refs_5_
  228.0 5.0 %tokens_end.3 = (f32[8,128]{1,0:T(8,128)}, f32[448,768]{1,0:T(8,128)}, f32[15,768]{1,0:T(8,128)S(1)}, bf16[448,768]{1,0:T(8,128)(2,1)}) custom-call(f32[8,128]{1,0:T(8,128)} %get-tuple-element.333.refs_0_, bf16[448,768]{1,0:T(8,128)(2,1)} %bitcast.33, f32[4,768]{1,0:T(4,128)} %refs_2_.5, f32[192,768]{1,0:T(8,128)} %get-tuple-element.334.refs_3_, ...), custom_call_target="tpu_custom_call" | custom-call | flops 74999996416 | bytes 480000000 | tf_op jit(solution)/shard_map/tokens_end/pallas_call | solution.py:171
  233.0 1.7 collective-permute-start.27
  235.9 1.1 cross0_step.3
  237.1 2.6 collective-permute-start.30
  239.7 1.8 collective-permute-done.26.refs_2_
  241.9 1.0 collective-permute-start.32
  242.9 5.1 %collective-permute-done.28.refs_1_.refs_7_ = f32[376,384]{1,0:T(8,128)S(1)} collective-permute-done((f32[376,384]{1,0:T(8,128)S(1)}, f32[376,384]{1,0:T(8,128)S(1)}, u32[]{:S(2)}, u32[]{:S(2)}) %collective-permute-start.28) | collective-permute-done | bytes 577568 | tf_op jit(solution)/shard_map/ppermute | solution.py:847
  248.0 3.9 %collective-permute-done.29.refs_3_ = f32[192,768]{1,0:T(8,128)S(1)} collective-permute-done((f32[192,768]{1,0:T(8,128)S(1)}, f32[192,768]{1,0:T(8,128)S(1)}, u32[]{:S(2)}, u32[]{:S(2)}) %collective-permute-start.29) | collective-permute-done | bytes 589856 | tf_op jit(solution)/shard_map/ppermute | solution.py:851
  254.2 1.4 collective-permute-done.31.refs_2_
  255.8 5.1 %collective-permute-done.33.refs_2_ = f32[96,768]{1,0:T(8,128)S(1)} collective-permute-done((f32[96,768]{1,0:T(8,128)S(1)}, f32[96,768]{1,0:T(8,128)S(1)}, u32[]{:S(2)}, u32[]{:S(2)}) %collective-permute-start.33) | collective-permute-done | bytes 294944 | tf_op jit(solution)/shard_map/ppermute | solution.py:851
  262.7 2.9 %collective-permute-done.35.refs_8_ = f32[376,384]{1,0:T(8,128)S(1)} collective-permute-done((f32[376,384]{1,0:T(8,128)S(1)}, f32[376,384]{1,0:T(8,128)S(1)}, u32[]{:S(2)}, u32[]{:S(2)}) %collective-permute-start.35) | collective-permute-done | bytes 577568 | tf_op jit(solution)/shard_map/ppermute | solution.py:847
  266.5 5.6 %frames_kept.1 = (f32[8,128]{1,0:T(8,128)}, f32[1500,1,384]{2,1,0:T(1,128)}) custom-call(f32[8,128]{1,0:T(8,128)} %get-tuple-element.375.refs_0_, s32[1]{0:T(128)} %bitcast.5.refs_19_.refs_1_, bf16[1536,384]{1,0:T(8,128)(2,1)} %get-tuple-element.285.refs_11_.refs_2_, bf16[1536,384]{1,0:T(8,128)(2,1)} %get-tuple-element.286.refs_13_.refs_3_, ...), custom_call_target="tpu_custom_call" | custom-call | flops 89999998976 | bytes 576000000 | tf_op jit(solution)/shard_map/frames_kept/pallas_call | solution.py:171
  (96 shorter events, 19.2 us)
Async XLA Ops:
  8.4 21.4 %collective-permute-start = (f32[256,768]{1,0:T(8,128)S(1)}, f32[256,768]{1,0:T(8,128)S(1)}, u32[]{:S(2)}, u32[]{:S(2)}) collective-permute-start(f32[256,768]{1,0:T(8,128)S(1)} %get-tuple-element.215.refs_1_), channel_id=1, source_target_pairs={{0,1},{1,0},{2,3},{3,2},{4,5},{5,4},{6,7},{7,6},{8,9},{9,8},{10,11... | collective-permute-start | bytes 2359304 | tf_op jit(solution)/shard_map/ppermute | solution.py:847
  11.4 4.3 %copy-start.8 = (bf16[768,2,384]{2,1,0:T(2,128)(2,1)S(1)}, bf16[768,2,384]{2,1,0:T(2,128)(2,1)}, u32[]{:S(2)}) copy-start(bf16[768,2,384]{2,1,0:T(2,128)(2,1)} %param.25) | copy-start | bytes 3538948
  15.6 26.8 %collective-permute-start.1 = (f32[192,768]{1,0:T(8,128)S(1)}, f32[192,768]{1,0:T(8,128)S(1)}, u32[]{:S(2)}, u32[]{:S(2)}) collective-permute-start(f32[192,768]{1,0:T(8,128)S(1)} %get-tuple-element.219.refs_1_), channel_id=1, source_target_pairs={{0,1},{1,0},{2,3},{3,2},{4,5},{5,4},{6,7},{7,6},{8,9},{9,8},{10,11... | collective-permute-start | bytes 1769480 | tf_op jit(solution)/shard_map/ppermute | solution.py:847
  17.8 9.0 %copy-start.10 = (f32[1536]{0:T(1024)S(1)}, f32[1536]{0:T(1024)}, u32[]{:S(2)}) copy-start(f32[1536]{0:T(1024)} %param.29) | copy-start | bytes 18436
  17.8 9.6 %copy-start.9 = (bf16[768,384]{1,0:T(8,128)(2,1)S(1)}, bf16[768,384]{1,0:T(8,128)(2,1)}, u32[]{:S(2)}) copy-start(bf16[768,384]{1,0:T(8,128)(2,1)} %refs_4_.16) | copy-start | bytes 1769476
  37.4 21.9 %collective-permute-start.2 = (f32[256,768]{1,0:T(8,128)S(1)}, f32[256,768]{1,0:T(8,128)S(1)}, u32[]{:S(2)}, u32[]{:S(2)}) collective-permute-start(f32[256,768]{1,0:T(8,128)S(1)} %get-tuple-element.227.refs_1_), channel_id=1, source_target_pairs={{0,1},{1,0},{2,3},{3,2},{4,5},{5,4},{6,7},{7,6},{8,9},{9,8},{10,11... | collective-permute-start | bytes 2359304 | tf_op jit(solution)/shard_map/ppermute | solution.py:847
  49.3 22.6 %collective-permute-start.3 = (f32[192,768]{1,0:T(8,128)S(1)}, f32[192,768]{1,0:T(8,128)S(1)}, u32[]{:S(2)}, u32[]{:S(2)}) collective-permute-start(f32[192,768]{1,0:T(8,128)S(1)} %get-tuple-element.230.refs_1_), channel_id=1, source_target_pairs={{0,1},{1,0},{2,3},{3,2},{4,5},{5,4},{6,7},{7,6},{8,9},{9,8},{10,11... | collective-permute-start | bytes 1769480 | tf_op jit(solution)/shard_map/ppermute | solution.py:847
  66.7 22.1 %collective-permute-start.4 = (f32[256,768]{1,0:T(8,128)S(1)}, f32[256,768]{1,0:T(8,128)S(1)}, u32[]{:S(2)}, u32[]{:S(2)}) collective-permute-start(f32[256,768]{1,0:T(8,128)S(1)} %get-tuple-element.237.refs_1_), channel_id=1, source_target_pairs={{0,1},{1,0},{2,3},{3,2},{4,5},{5,4},{6,7},{7,6},{8,9},{9,8},{10,11... | collective-permute-start | bytes 2359304 | tf_op jit(solution)/shard_map/ppermute | solution.py:847
  78.5 22.9 %collective-permute-start.5 = (f32[192,768]{1,0:T(8,128)S(1)}, f32[192,768]{1,0:T(8,128)S(1)}, u32[]{:S(2)}, u32[]{:S(2)}) collective-permute-start(f32[192,768]{1,0:T(8,128)S(1)} %get-tuple-element.241.refs_1_), channel_id=1, source_target_pairs={{0,1},{1,0},{2,3},{3,2},{4,5},{5,4},{6,7},{7,6},{8,9},{9,8},{10,11... | collective-permute-start | bytes 1769480 | tf_op jit(solution)/shard_map/ppermute | solution.py:847
  96.0 13.1 %copy-start = (f32[256,768]{1,0:T(8,128)}, f32[256,768]{1,0:T(8,128)S(1)}, u32[]{:S(2)}) copy-start(f32[256,768]{1,0:T(8,128)S(1)} %get-tuple-element.254.refs_1_) | copy-start | bytes 2359300
  96.0 13.1 %copy-start.2 = (f32[8,1536]{1,0:T(8,128)}, f32[8,1536]{1,0:T(8,128)S(1)}, u32[]{:S(2)}) copy-start(f32[8,1536]{1,0:T(8,128)S(1)} %get-tuple-element.343.refs_12_) | copy-start | bytes 147460
  96.0 13.1 %copy-start.4 = (f32[8,768]{1,0:T(8,128)}, f32[8,768]{1,0:T(8,128)S(1)}, u32[]{:S(2)}) copy-start(f32[8,768]{1,0:T(8,128)S(1)} %get-tuple-element.341.refs_10_) | copy-start | bytes 73732
  96.1 21.7 %collective-permute-start.6 = (f32[256,768]{1,0:T(8,128)S(1)}, f32[256,768]{1,0:T(8,128)S(1)}, u32[]{:S(2)}, u32[]{:S(2)}) collective-permute-start(f32[256,768]{1,0:T(8,128)S(1)} %get-tuple-element.254.refs_1_), channel_id=1, source_target_pairs={{0,1},{1,0},{2,3},{3,2},{4,5},{5,4},{6,7},{7,6},{8,9},{9,8},{10,11... | collective-permute-start | bytes 2359304 | tf_op jit(solution)/shard_map/ppermute | solution.py:847
  109.1 0.6 copy-start.3
  109.8 0.6 copy-start.5
  115.5 8.0 %collective-permute-start.7 = (f32[384,3072]{1,0:T(8,128)S(1)}, f32[384,3072]{1,0:T(8,128)S(1)}, u32[]{:S(2)}, u32[]{:S(2)}) collective-permute-start(f32[384,3072]{1,0:T(8,128)S(1)} %get-tuple-element.255), channel_id=1, source_target_pairs={{0,2},{2,0},{4,6},{6,4},{8,10},{10,8},{12,14},{14,12},{16,18},{18,... | collective-permute-start | bytes 14155784 | tf_op jit(solution)/shard_map/ppermute | solution.py:851
  115.6 16.6 %collective-permute-start.8 = (f32[192,768]{1,0:T(8,128)}, f32[192,768]{1,0:T(8,128)}, u32[]{:S(2)}, u32[]{:S(2)}) collective-permute-start(f32[192,768]{1,0:T(8,128)} %get-tuple-element.264.refs_8_), channel_id=1, source_target_pairs={{0,1},{1,0},{2,3},{3,2},{4,5},{5,4},{6,7},{7,6},{8,9},{9,8},{10,11... | collective-permute-start | bytes 1769480 | tf_op jit(solution)/shard_map/ppermute | solution.py:847
  117.7 39.2 %collective-permute-start.9 = (f32[384,384]{1,0:T(8,128)}, f32[384,384]{1,0:T(8,128)}, u32[]{:S(2)}, u32[]{:S(2)}) collective-permute-start(f32[384,384]{1,0:T(8,128)} %dynamic-slice_convert_fusion), channel_id=1, source_target_pairs={{0,1},{1,0},{2,3},{3,2},{4,5},{5,4},{6,7},{7,6},{8,9},{9,8},{10,11... | collective-permute-start | bytes 1769480 | tf_op jit(solution)/shard_map/ppermute | solution.py:847
  117.8 0.9 copy-start.11
  127.7 29.2 %collective-permute-start.10 = (f32[192,1536]{1,0:T(8,128)}, f32[192,1536]{1,0:T(8,128)}, u32[]{:S(2)}, u32[]{:S(2)}) collective-permute-start(f32[192,1536]{1,0:T(8,128)} %get-tuple-element.272), channel_id=1, source_target_pairs={{0,4},{2,6},{4,0},{6,2},{8,12},{10,14},{12,8},{14,10},{16,20},{18,... | collective-permute-start | bytes 3538952 | tf_op jit(solution)/shard_map/ppermute | solution.py:851
  129.8 28.0 %collective-permute-start.11 = (f32[192,1536]{1,0:T(8,128)}, f32[192,1536]{1,0:T(8,128)}, u32[]{:S(2)}, u32[]{:S(2)}) collective-permute-start(f32[192,1536]{1,0:T(8,128)} %get-tuple-element.274), channel_id=1, source_target_pairs={{0,8},{2,10},{4,12},{6,14},{8,0},{10,2},{12,4},{14,6},{16,24},{18,... | collective-permute-start | bytes 3538952 | tf_op jit(solution)/shard_map/ppermute | solution.py:851
  154.8 5.9 %copy-start.1 = (f32[448,384]{1,0:T(8,128)}, f32[448,384]{1,0:T(8,128)S(1)}, u32[]{:S(2)}) copy-start(f32[448,384]{1,0:T(8,128)S(1)} %get-tuple-element.288.refs_2_) | copy-start | bytes 2064388
  154.8 5.9 %copy-start.6 = (f32[8,768]{1,0:T(8,128)}, f32[8,768]{1,0:T(8,128)S(1)}, u32[]{:S(2)}) copy-start(f32[8,768]{1,0:T(8,128)S(1)} %get-tuple-element.340.refs_9_) | copy-start | bytes 73732
  154.8 18.4 %collective-permute-start.12 = (f32[448,384]{1,0:T(8,128)S(1)}, f32[448,384]{1,0:T(8,128)S(1)}, u32[]{:S(2)}, u32[]{:S(2)}) collective-permute-start(f32[448,384]{1,0:T(8,128)S(1)} %get-tuple-element.288.refs_2_), channel_id=1, source_target_pairs={{0,1},{1,0},{2,3},{3,2},{4,5},{5,4},{6,7},{7,6},{8,9},{9,8},{10,11... | collective-permute-start | bytes 2064392 | tf_op jit(solution)/shard_map/ppermute | solution.py:847
  156.8 26.6 %collective-permute-start.14 = (f32[384,384]{1,0:T(8,128)}, f32[384,384]{1,0:T(8,128)}, u32[]{:S(2)}, u32[]{:S(2)}) collective-permute-start(f32[384,384]{1,0:T(8,128)} %collective-permute-done.9.refs_1_.refs_5_), channel_id=1, source_target_pairs={{0,2},{2,0},{4,6},{6,4},{8,10},{10,8},{12,14},{14,12},{16,18},{18,... | collective-permute-start | bytes 1769480 | tf_op jit(solution)/shard_map/ppermute | solution.py:851
  166.5 9.8 %collective-permute-start.13 = (f32[384,1536]{1,0:T(8,128)S(1)}, f32[384,1536]{1,0:T(8,128)S(1)}, u32[]{:S(2)}, u32[]{:S(2)}) collective-permute-start(f32[384,1536]{1,0:T(8,128)S(1)} %get-tuple-element.289), channel_id=1, source_target_pairs={{0,2},{2,0},{4,6},{6,4},{8,10},{10,8},{12,14},{14,12},{16,18},{18,... | collective-permute-start | bytes 7077896 | tf_op jit(solution)/shard_map/ppermute | solution.py:851
  166.6 33.6 %collective-permute-start.15 = (f32[376,384]{1,0:T(8,128)}, f32[376,384]{1,0:T(8,128)}, u32[]{:S(2)}, u32[]{:S(2)}) collective-permute-start(f32[376,384]{1,0:T(8,128)} %get-tuple-element.302), channel_id=1, source_target_pairs={{0,1},{1,0},{2,3},{3,2},{4,5},{5,4},{6,7},{7,6},{8,9},{9,8},{10,11... | collective-permute-start | bytes 1732616 | tf_op jit(solution)/shard_map/ppermute | solution.py:847
  168.2 32.6 %collective-permute-start.16 = (f32[96,1536]{1,0:T(8,128)}, f32[96,1536]{1,0:T(8,128)}, u32[]{:S(2)}, u32[]{:S(2)}) collective-permute-start(f32[96,1536]{1,0:T(8,128)} %get-tuple-element.304), channel_id=1, source_target_pairs={{0,8},{2,10},{4,12},{6,14},{8,0},{10,2},{12,4},{14,6},{16,24},{18,... | collective-permute-start | bytes 1769480 | tf_op jit(solution)/shard_map/ppermute | solution.py:851
  173.3 3.0 %copy-start.12 = (f32[448,384]{1,0:T(8,128)}, f32[448,384]{1,0:T(8,128)S(1)}, u32[]{:S(2)}) copy-start(f32[448,384]{1,0:T(8,128)S(1)} %collective-permute-done.12.refs_1_.refs_3_) | copy-start | bytes 2064388
  173.3 27.5 %collective-permute-start.17 = (f32[96,1536]{1,0:T(8,128)}, f32[96,1536]{1,0:T(8,128)}, u32[]{:S(2)}, u32[]{:S(2)}) collective-permute-start(f32[96,1536]{1,0:T(8,128)} %get-tuple-element.306), channel_id=1, source_target_pairs={{0,16},{2,18},{4,20},{6,22},{8,24},{10,26},{12,28},{14,30},{16,0},... | collective-permute-start | bytes 1769480 | tf_op jit(solution)/shard_map/ppermute | solution.py:851
  181.9 27.0 %collective-permute-start.18 = (f32[376,384]{1,0:T(8,128)}, f32[376,384]{1,0:T(8,128)}, u32[]{:S(2)}, u32[]{:S(2)}) collective-permute-start(f32[376,384]{1,0:T(8,128)} %get-tuple-element.318), channel_id=1, source_target_pairs={{0,1},{1,0},{2,3},{3,2},{4,5},{5,4},{6,7},{7,6},{8,9},{9,8},{10,11... | collective-permute-start | bytes 1732616 | tf_op jit(solution)/shard_map/ppermute | solution.py:847
  183.5 27.3 %collective-permute-start.19 = (f32[192,1536]{1,0:T(8,128)}, f32[192,1536]{1,0:T(8,128)}, u32[]{:S(2)}, u32[]{:S(2)}) collective-permute-start(f32[192,1536]{1,0:T(8,128)} %get-tuple-element.320), channel_id=1, source_target_pairs={{0,4},{2,6},{4,0},{6,2},{8,12},{10,14},{12,8},{14,10},{16,20},{18,... | collective-permute-start | bytes 3538952 | tf_op jit(solution)/shard_map/ppermute | solution.py:851
  199.6 0.6 copy-start.7
  200.2 17.9 %collective-permute-start.20 = (f32[256,768]{1,0:T(8,128)S(1)}, f32[256,768]{1,0:T(8,128)S(1)}, u32[]{:S(2)}, u32[]{:S(2)}) collective-permute-start(f32[256,768]{1,0:T(8,128)S(1)} %get-tuple-element.323.refs_4_), channel_id=1, source_target_pairs={{0,1},{1,0},{2,3},{3,2},{4,5},{5,4},{6,7},{7,6},{8,9},{9,8},{10,11... | collective-permute-start | bytes 2359304 | tf_op jit(solution)/shard_map/ppermute | solution.py:847
  202.8 18.5 %collective-permute-start.21 = (f32[48,1536]{1,0:T(8,128)}, f32[48,1536]{1,0:T(8,128)}, u32[]{:S(2)}, u32[]{:S(2)}) collective-permute-start(f32[48,1536]{1,0:T(8,128)} %get-tuple-element.326), channel_id=1, source_target_pairs={{0,16},{2,18},{4,20},{6,22},{8,24},{10,26},{12,28},{14,30},{16,0},... | collective-permute-start | bytes 884744 | tf_op jit(solution)/shard_map/ppermute | solution.py:851
  203.7 17.6 %collective-permute-start.22 = (f32[48,1536]{1,0:T(8,128)}, f32[48,1536]{1,0:T(8,128)}, u32[]{:S(2)}, u32[]{:S(2)}) collective-permute-start(f32[48,1536]{1,0:T(8,128)} %get-tuple-element.328), channel_id=1, source_target_pairs={{0,4},{2,6},{4,0},{6,2},{8,12},{10,14},{12,8},{14,10},{16,20},{18,... | collective-permute-start | bytes 884744 | tf_op jit(solution)/shard_map/ppermute | solution.py:851
  208.9 14.3 %collective-permute-start.23 = (f32[384,1536]{1,0:T(8,128)S(1)}, f32[384,1536]{1,0:T(8,128)S(1)}, u32[]{:S(2)}, u32[]{:S(2)}) collective-permute-start(f32[384,1536]{1,0:T(8,128)S(1)} %get-tuple-element.330), channel_id=1, source_target_pairs={{0,2},{2,0},{4,6},{6,4},{8,10},{10,8},{12,14},{14,12},{16,18},{18,... | collective-permute-start | bytes 7077896 | tf_op jit(solution)/shard_map/ppermute | solution.py:851
  210.8 17.2 %collective-permute-start.24 = (f32[192,768]{1,0:T(8,128)}, f32[192,768]{1,0:T(8,128)}, u32[]{:S(2)}, u32[]{:S(2)}) collective-permute-start(f32[192,768]{1,0:T(8,128)} %get-tuple-element.336.refs_4_), channel_id=1, source_target_pairs={{0,1},{1,0},{2,3},{3,2},{4,5},{5,4},{6,7},{7,6},{8,9},{9,8},{10,11... | collective-permute-start | bytes 1769480 | tf_op jit(solution)/shard_map/ppermute | solution.py:847
  218.1 17.8 %collective-permute-start.25 = (f32[96,1536]{1,0:T(8,128)}, f32[96,1536]{1,0:T(8,128)}, u32[]{:S(2)}, u32[]{:S(2)}) collective-permute-start(f32[96,1536]{1,0:T(8,128)} %get-tuple-element.351), channel_id=1, source_target_pairs={{0,8},{2,10},{4,12},{6,14},{8,0},{10,2},{12,4},{14,6},{16,24},{18,... | collective-permute-start | bytes 1769480 | tf_op jit(solution)/shard_map/ppermute | solution.py:851
  226.5 15.1 %collective-permute-start.26 = (f32[192,768]{1,0:T(8,128)S(1)}, f32[192,768]{1,0:T(8,128)S(1)}, u32[]{:S(2)}, u32[]{:S(2)}) collective-permute-start(f32[192,768]{1,0:T(8,128)S(1)} %get-tuple-element.354), channel_id=1, source_target_pairs={{0,4},{2,6},{4,0},{6,2},{8,12},{10,14},{12,8},{14,10},{16,20},{18,... | collective-permute-start | bytes 1769480 | tf_op jit(solution)/shard_map/ppermute | solution.py:851
  228.0 6.7 %copy-start.14 = (f32[376,384]{1,0:T(8,128)S(1)}, f32[376,384]{1,0:T(8,128)}, u32[]{:S(2)}) copy-start(f32[376,384]{1,0:T(8,128)} %get-tuple-element.359) | copy-start | bytes 1732612
  233.0 8.9 %collective-permute-start.27 = (f32[15,768]{1,0:T(8,128)S(1)}, f32[15,768]{1,0:T(8,128)S(1)}, u32[]{:S(2)}, u32[]{:S(2)}) collective-permute-start(f32[15,768]{1,0:T(8,128)S(1)} %get-tuple-element.356.refs_1_), channel_id=1, source_target_pairs={{0,8},{2,10},{4,12},{6,14},{8,0},{10,2},{12,4},{14,6},{16,24},{18,... | collective-permute-start | bytes 138248 | tf_op jit(solution)/shard_map/ppermute | solution.py:851
  234.7 13.3 %collective-permute-start.28 = (f32[376,384]{1,0:T(8,128)S(1)}, f32[376,384]{1,0:T(8,128)S(1)}, u32[]{:S(2)}, u32[]{:S(2)}) collective-permute-start(f32[376,384]{1,0:T(8,128)S(1)} %copy-done.14), channel_id=1, source_target_pairs={{0,1},{1,0},{2,3},{3,2},{4,5},{5,4},{6,7},{7,6},{8,9},{9,8},{10,11... | collective-permute-start | bytes 1732616 | tf_op jit(solution)/shard_map/ppermute | solution.py:847
  235.2 16.7 %collective-permute-start.29 = (f32[192,768]{1,0:T(8,128)S(1)}, f32[192,768]{1,0:T(8,128)S(1)}, u32[]{:S(2)}, u32[]{:S(2)}) collective-permute-start(f32[192,768]{1,0:T(8,128)S(1)} %get-tuple-element.361), channel_id=1, source_target_pairs={{0,4},{2,6},{4,0},{6,2},{8,12},{10,14},{12,8},{14,10},{16,20},{18,... | collective-permute-start | bytes 1769480 | tf_op jit(solution)/shard_map/ppermute | solution.py:851
  237.1 16.4 %collective-permute-start.30 = (f32[48,1536]{1,0:T(8,128)S(1)}, f32[48,1536]{1,0:T(8,128)S(1)}, u32[]{:S(2)}, u32[]{:S(2)}) collective-permute-start(f32[48,1536]{1,0:T(8,128)S(1)} %get-tuple-element.364), channel_id=1, source_target_pairs={{0,16},{2,18},{4,20},{6,22},{8,24},{10,26},{12,28},{14,30},{16,0},... | collective-permute-start | bytes 884744 | tf_op jit(solution)/shard_map/ppermute | solution.py:851
  241.6 14.0 %collective-permute-start.31 = (f32[96,768]{1,0:T(8,128)S(1)}, f32[96,768]{1,0:T(8,128)S(1)}, u32[]{:S(2)}, u32[]{:S(2)}) collective-permute-start(f32[96,768]{1,0:T(8,128)S(1)} %get-tuple-element.367), channel_id=1, source_target_pairs={{0,8},{2,10},{4,12},{6,14},{8,0},{10,2},{12,4},{14,6},{16,24},{18,... | collective-permute-start | bytes 884744 | tf_op jit(solution)/shard_map/ppermute | solution.py:851
  241.9 13.7 %collective-permute-start.32 = (f32[15,768]{1,0:T(8,128)S(1)}, f32[15,768]{1,0:T(8,128)S(1)}, u32[]{:S(2)}, u32[]{:S(2)}) collective-permute-start(f32[15,768]{1,0:T(8,128)S(1)} %get-tuple-element.369.refs_1_), channel_id=1, source_target_pairs={{0,16},{2,18},{4,20},{6,22},{8,24},{10,26},{12,28},{14,30},{16,0},... | collective-permute-start | bytes 138248 | tf_op jit(solution)/shard_map/ppermute | solution.py:851
  248.0 3.9 %copy-start.15 = (f32[376,384]{1,0:T(8,128)}, f32[376,384]{1,0:T(8,128)S(1)}, u32[]{:S(2)}) copy-start(f32[376,384]{1,0:T(8,128)S(1)} %collective-permute-done.28.refs_1_.refs_7_) | copy-start | bytes 1732612
  251.9 1.1 copy-start.13
  251.9 9.0 %collective-permute-start.33 = (f32[96,768]{1,0:T(8,128)S(1)}, f32[96,768]{1,0:T(8,128)S(1)}, u32[]{:S(2)}, u32[]{:S(2)}) collective-permute-start(f32[96,768]{1,0:T(8,128)S(1)} %get-tuple-element.372), channel_id=1, source_target_pairs={{0,8},{2,10},{4,12},{6,14},{8,0},{10,2},{12,4},{14,6},{16,24},{18,... | collective-permute-start | bytes 884744 | tf_op jit(solution)/shard_map/ppermute | solution.py:851
  252.9 12.8 %collective-permute-start.35 = (f32[376,384]{1,0:T(8,128)S(1)}, f32[376,384]{1,0:T(8,128)S(1)}, u32[]{:S(2)}, u32[]{:S(2)}) collective-permute-start(f32[376,384]{1,0:T(8,128)S(1)} %copy-done.13), channel_id=1, source_target_pairs={{0,1},{1,0},{2,3},{3,2},{4,5},{5,4},{6,7},{7,6},{8,9},{9,8},{10,11... | collective-permute-start | bytes 1732616 | tf_op jit(solution)/shard_map/ppermute | solution.py:847
  255.7 6.1 %collective-permute-start.34 = (f32[15,768]{1,0:T(8,128)S(1)}, f32[15,768]{1,0:T(8,128)S(1)}, u32[]{:S(2)}, u32[]{:S(2)}) collective-permute-start(f32[15,768]{1,0:T(8,128)S(1)} %get-tuple-element.374.refs_1_), channel_id=1, source_target_pairs={{0,2},{2,0},{4,6},{6,4},{8,10},{10,8},{12,14},{14,12},{16,18},{18,... | collective-permute-start | bytes 138248 | tf_op jit(solution)/shard_map/ppermute | solution.py:851
  255.8 16.4 %collective-permute-start.36 = (f32[48,768]{1,0:T(8,128)S(1)}, f32[48,768]{1,0:T(8,128)S(1)}, u32[]{:S(2)}, u32[]{:S(2)}) collective-permute-start(f32[48,768]{1,0:T(8,128)S(1)} %get-tuple-element.381), channel_id=1, source_target_pairs={{0,16},{2,18},{4,20},{6,22},{8,24},{10,26},{12,28},{14,30},{16,0},... | collective-permute-start | bytes 442376 | tf_op jit(solution)/shard_map/ppermute | solution.py:851
  261.0 11.8 %collective-permute-start.37 = (f32[48,768]{1,0:T(8,128)S(1)}, f32[48,768]{1,0:T(8,128)S(1)}, u32[]{:S(2)}, u32[]{:S(2)}) collective-permute-start(f32[48,768]{1,0:T(8,128)S(1)} %get-tuple-element.385), channel_id=1, source_target_pairs={{0,16},{2,18},{4,20},{6,22},{8,24},{10,26},{12,28},{14,30},{16,0},... | collective-permute-start | bytes 442376 | tf_op jit(solution)/shard_map/ppermute | solution.py:851
  261.8 11.1 %collective-permute-start.38 = (f32[15,768]{1,0:T(8,128)S(1)}, f32[15,768]{1,0:T(8,128)S(1)}, u32[]{:S(2)}, u32[]{:S(2)}) collective-permute-start(f32[15,768]{1,0:T(8,128)S(1)} %get-tuple-element.389.refs_1_), channel_id=1, source_target_pairs={{0,4},{2,6},{4,0},{6,2},{8,12},{10,14},{12,8},{14,10},{16,20},{18,... | collective-permute-start | bytes 138248 | tf_op jit(solution)/shard_map/ppermute | solution.py:851
  265.7 0.8 copy-start.16
